TPU v7x, 32 devices: a whole 2x2x4 slice. The times are simulated.
32 devices in a mesh: alpha: 4 (over z), beta: 8 (over y, x, core).
Axes of the slice: x: 2, y: 2, z: 4, core: 2. Of those that a mesh axis runs over, the one named last changes fastest.
Arguments:
- ci_vectors: float32 [4, 128, 1024], P(None, 'alpha', 'beta'), may hold values from -2 to 2
- alpha_source: int32 [128, 256], P('alpha'), may hold values from 0 to 127, as said below
- alpha_sign: int32 [128, 256], P('alpha'), may hold values from -1 to 1, as said below
- beta_source: int32 [1024, 256], P('beta'), may hold values from 0 to 1023, as said below
- beta_sign: int32 [1024, 256], P('beta'), may hold values from -1 to 1, as said below
Outputs:
- one_body: float32 [4, 1024], replicated
- two_body: float32 [1024, 1024], P(('alpha', 'beta'))
Inputs may be any that keep to these rules, and one draw needn't show every extreme that they name: `alpha_source`: the source of a diagonal pair p p is the string itself. `beta_source`: the source of a diagonal pair p p is the string itself. `alpha_sign`: each string has 8 occupied orbitals; the sign is nonzero exactly where p is occupied and q equals p or is empty, 72 pairs a string, and is +1 on diagonal pairs. `beta_sign`: each string has 8 occupied orbitals; the sign is nonzero exactly where p is occupied and q equals p or is empty, 72 pairs a string, and is +1 on diagonal pairs.
All inputs are finite; a program needn't handle non-finite values.
Results may differ from a plain program's by a relative error of at most 0.0003.
Values sent between devices are 32-bit elements; how exact they have to be, the bound alone decides.
No kernel may reach another device: no remote copies, remote signals or barrier semaphores. Data moves between devices by JAX's collectives and lax.ppermute only.
A program may use at most 128 MiB of HBM per device.

v0:
```python
import functools

import jax
import jax.numpy as jnp
import numpy as np
from jax import lax
from jax.experimental import pallas as pl
from jax.experimental.pallas import tpu as pltpu
from jax.sharding import PartitionSpec as P

F32 = jnp.float32
BF16 = jnp.bfloat16
LANES = 128


def pair_lanes(norb):
    forward, backward = [], []
    for p in range(norb):
        for q in range(p + 1, norb):
            forward.append(p * norb + q)
            backward.append(q * norb + p)
    for p in range(norb // 2):
        forward.append(p * (norb + 1))
        backward.append((p + norb // 2) * (norb + 1))
    return np.array(forward, np.int32), np.array(backward, np.int32)


def pick_lanes(left, right, lane):
    low = jnp.broadcast_to(lane & (LANES - 1), left.shape)
    from_left = jnp.take_along_axis(left, low, axis=1)
    from_right = jnp.take_along_axis(right, low, axis=1)
    return jnp.where(lane < LANES, from_left, from_right)


def split_two(value):
    high = value.astype(BF16)
    return high, (value - high.astype(F32)).astype(BF16)


def main_kernel(
    rows_each,
    orders,
    columns,
    place_ref,
    lane_ref,
    alpha_ref,
    beta_ref,
    flat_ref,
    asrc_ref,
    asgn_ref,
    bsrc_ref,
    bsgn_ref,
    *refs,
):
    streams = len(columns)
    send_refs = refs[:streams]
    keep_refs = refs[streams : 2 * streams]
    one_ref = refs[2 * streams]
    (
        table_ref,
        turned_ref,
        aidx_ref,
        asf_ref,
        asb_ref,
        bidx_ref,
        bsf_ref,
        bsb_ref,
        right_ref,
        low_ref,
        left_ref,
        state_ref,
        perm_ref,
    ) = refs[2 * streams + 1 :]
    states, alpha_count, beta_rows = alpha_ref.shape
    alpha_rows = beta_ref.shape[1]
    beta_count = beta_ref.shape[2]
    both = states * alpha_rows
    pairs = 2 * LANES
    my_alpha = place_ref[0]
    my_beta = place_ref[1]
    forward = lane_ref[0:1, 0:LANES]
    backward = lane_ref[0:1, LANES:pairs]

    def tables(src_ref, sgn_ref, idx_ref, sf_ref, sb_ref, count):
        for r in range(0, count, 8):
            rows = slice(r, r + 8)
            s0, s1 = sgn_ref[rows, 0:LANES], sgn_ref[rows, LANES:pairs]
            i0, i1 = src_ref[rows, 0:LANES], src_ref[rows, LANES:pairs]
            sf = pick_lanes(s0, s1, forward)
            sb = pick_lanes(s0, s1, backward)
            idx_ref[rows, :] = jnp.where(
                sf != 0, pick_lanes(i0, i1, forward), pick_lanes(i0, i1, backward)
            )
            sf_ref[rows, :] = sf.astype(F32)
            sb_ref[rows, :] = sb.astype(F32)

    tables(asrc_ref, asgn_ref, aidx_ref, asf_ref, asb_ref, alpha_rows)
    tables(bsrc_ref, bsgn_ref, bidx_ref, bsf_ref, bsb_ref, beta_rows)

    whole = beta_ref[...].reshape(both, beta_count)
    high, mid = split_two(whole)
    table_ref[0:both, :] = high
    table_ref[both : 2 * both, :] = mid
    for j in range(states):
        turned_ref[j] = alpha_ref[j].T

    flat = flat_ref[...]
    flat_high = flat.astype(BF16).astype(F32)
    flat_mid = flat - flat_high
    pad = jnp.zeros((16 - 2 * states, flat.shape[1]), F32)
    state_ref[...] = jnp.concatenate([flat_high, flat_mid, pad], axis=0).astype(BF16)

    natural = lane_ref[0:1, :]
    row = lax.broadcasted_iota(jnp.int32, (pairs, pairs), 0)
    shift = rows_each.bit_length() - 1
    wanted = (((row >> shift) ^ my_beta) << shift) | (row & (rows_each - 1))
    perm_ref[...] = jnp.where(natural == wanted, 1.0, 0.0).astype(BF16)

    chunk = min(1024, beta_count)
    chunks = beta_count // chunk
    step = 4

    def one_hot_dot(idx0, idx1, first):
        where = lax.broadcasted_iota(jnp.int32, (chunk, LANES), 0) + first
        picks = jnp.concatenate(
            [
                jnp.where(where == idx0, 1.0, 0.0).astype(BF16),
                jnp.where(where == idx1, 1.0, 0.0).astype(BF16),
            ],
            axis=1,
        )
        if chunks == 1:
            part = table_ref[...]
        else:
            part = table_ref[:, pl.ds(pl.multiple_of(first, chunk), chunk)]
        return jnp.dot(part, picks, preferred_element_type=F32)

    def build(block, carry):
        for u in range(step // 2):
            b0 = block * step + 2 * u
            idx0 = bidx_ref[pl.ds(b0, 1), :]
            idx1 = bidx_ref[pl.ds(b0 + 1, 1), :]
            if chunks == 1:
                got = one_hot_dot(idx0, idx1, 0)
            else:
                got = lax.fori_loop(
                    0,
                    chunks,
                    lambda c, acc: acc + one_hot_dot(idx0, idx1, c * chunk),
                    jnp.zeros((2 * both, 2 * LANES), F32),
                )
            picked = got[0:both] + got[both : 2 * both]
            for v in range(2):
                b = b0 + v
                sf = bsf_ref[pl.ds(b, 1), :]
                sb = bsb_ref[pl.ds(b, 1), :]
                first = pl.multiple_of(b * alpha_rows, alpha_rows)
                for j in range(states):
                    source = jnp.broadcast_to(turned_ref[j, pl.ds(b, 1), :], (8, LANES))
                    from_alpha = jnp.concatenate(
                        [
                            jnp.take_along_axis(source, aidx_ref[r : r + 8, :], axis=1)
                            for r in range(0, alpha_rows, 8)
                        ],
                        axis=0,
                    )
                    from_beta = picked[
                        j * alpha_rows : (j + 1) * alpha_rows, v * LANES : (v + 1) * LANES
                    ]
                    for half, asg, bsg in ((0, asf_ref, sf), (1, asb_ref, sb)):
                        value = asg[...] * from_alpha + bsg * from_beta
                        top, rest = split_two(value)
                        col = j * pairs + half * LANES
                        right_ref[pl.ds(first, alpha_rows), col : col + LANES] = top
                        low_ref[pl.ds(first, alpha_rows), col : col + LANES] = rest
        return carry

    lax.fori_loop(0, beta_rows // step, build, 0)

    depth = alpha_rows * beta_rows
    piece = 512

    def turn(k, carry):
        first = pl.multiple_of(k * piece, piece)
        for ja in range(states):
            col = pl.multiple_of((my_alpha ^ ja) * pairs, pairs)
            value = lax.dot_general(
                perm_ref[...],
                right_ref[pl.ds(first, piece), pl.ds(col, pairs)],
                (((1,), (1,)), ((), ())),
                preferred_element_type=F32,
            )
            left_ref[ja * pairs : (ja + 1) * pairs, pl.ds(first, piece)] = value.astype(BF16)
        return carry

    lax.fori_loop(0, depth // piece, turn, 0)

    beta_bits = (pairs // rows_each).bit_length() - 1
    for ja in range(states):
        value = jnp.dot(
            left_ref[ja * pairs : (ja + 1) * pairs, :],
            right_ref[...],
            preferred_element_type=F32,
        )
        for jb in range(1 << beta_bits):
            rows = value[jb * rows_each : (jb + 1) * rows_each]
            first_col = 0
            for s in range(streams):
                place = 0
                for kind, bit in orders[s]:
                    source = jb if kind == "beta" else ja
                    place = 2 * place + ((source >> bit) & 1)
                target = send_refs[s] if jb & 1 else keep_refs[s]
                target[place * rows_each : (place + 1) * rows_each, :] = rows[
                    :, first_col : first_col + columns[s]
                ]
                first_col += columns[s]

    one = jnp.dot(state_ref[...], right_ref[...], preferred_element_type=F32)
    one_low = jnp.dot(state_ref[...], low_ref[...], preferred_element_type=F32)
    total = one + one_low
    one_ref[...] = total[0:states] + total[states : 2 * states]


def last_kernel(columns, lane_ref, one_a_ref, one_b_ref, *refs):
    streams = len(columns)
    kept, got = refs[:streams], refs[streams : 2 * streams]
    one_ref, two_ref = refs[2 * streams :]
    pairs = 2 * LANES
    back0, back1 = lane_ref[0:1, 0:LANES], lane_ref[0:1, LANES:pairs]
    value = jnp.concatenate([kept[s][...] + got[s][...] for s in range(streams)], axis=1)

    def place(whole, out_ref):
        rows, total = whole.shape
        for col in range(0, total, pairs):
            for r in range(0, rows, 8):
                n = min(8, rows - r)
                left = whole[r : r + n, col : col + LANES]
                right = whole[r : r + n, col + LANES : col + pairs]
                out_ref[r : r + n, col : col + LANES] = pick_lanes(left, right, back0)
                out_ref[r : r + n, col + LANES : col + pairs] = pick_lanes(left, right, back1)

    def full(whole):
        rows = whole.shape[0]
        if rows % 8 == 0:
            return whole
        return jnp.concatenate([whole] * (8 // rows), axis=0)

    place_rows(place, full, value, two_ref)
    place_rows(place, full, one_a_ref[...] + one_b_ref[...], one_ref)


def place_rows(place, full, whole, out_ref):
    rows = whole.shape[0]
    if rows % 8 == 0:
        place(whole, out_ref)
        return

    class Cut:
        def __setitem__(self, where, value):
            out_ref[0:rows, where[1]] = value[0:rows]

    place(full(whole), Cut())


def swap(value, kind, bit, size):
    return lax.ppermute(value, kind, [(i, i ^ (1 << bit)) for i in range(size)])


def shards(sizes, ci_vectors, alpha_source, alpha_sign, beta_source, beta_sign):
    states, alpha_rows, beta_rows = ci_vectors.shape
    pairs = alpha_source.shape[1]
    total = states * pairs
    norb = int(round(pairs ** 0.5))
    forward, backward = pair_lanes(norb)
    lane = np.concatenate([forward, backward]).reshape(1, pairs)
    inverse = np.argsort(lane[0]).astype(np.int32).reshape(1, pairs)
    rows_each = total // (sizes["alpha"] * sizes["beta"])
    alpha_bits = sizes["alpha"].bit_length() - 1
    beta_bits = sizes["beta"].bit_length() - 1

    alpha_whole = lax.all_gather(ci_vectors, "alpha", axis=1, tiled=True)
    beta_whole = lax.all_gather(ci_vectors, "beta", axis=2, tiled=True)
    flat = jnp.transpose(ci_vectors, (0, 2, 1)).reshape(states, alpha_rows * beta_rows)
    place = jnp.stack([lax.axis_index("alpha"), lax.axis_index("beta")]).astype(jnp.int32)

    in_beta = [("beta", i) for i in range(1, beta_bits)]
    in_alpha = [("alpha", i) for i in range(alpha_bits)]
    orders = [
        in_beta + in_alpha,
        in_beta[1:] + in_alpha + in_beta[:1],
        in_alpha + in_beta,
    ]
    columns = [384, 384, 256]
    streams = len(orders)
    half = total // 2
    beta_count = beta_whole.shape[2]
    depth = alpha_rows * beta_rows
    vmem = pl.BlockSpec(memory_space=pltpu.VMEM)
    results = pl.pallas_call(
        functools.partial(main_kernel, rows_each, orders, columns),
        out_shape=[jax.ShapeDtypeStruct((half, c), F32) for c in columns] * 2
        + [jax.ShapeDtypeStruct((states, total), F32)],
        in_specs=[pl.BlockSpec(memory_space=pltpu.SMEM)] + [vmem] * 8,
        out_specs=[vmem] * (2 * streams + 1),
        scratch_shapes=[
            pltpu.VMEM((2 * states * alpha_rows, beta_count), BF16),
            pltpu.VMEM((states, beta_rows, alpha_whole.shape[1]), F32),
            pltpu.VMEM((alpha_rows, LANES), jnp.int32),
            pltpu.VMEM((alpha_rows, LANES), F32),
            pltpu.VMEM((alpha_rows, LANES), F32),
            pltpu.VMEM((beta_rows, LANES), jnp.int32),
            pltpu.VMEM((beta_rows, LANES), F32),
            pltpu.VMEM((beta_rows, LANES), F32),
            pltpu.VMEM((depth, total), BF16),
            pltpu.VMEM((depth, total), BF16),
            pltpu.VMEM((total, depth), BF16),
            pltpu.VMEM((16, depth), BF16),
            pltpu.VMEM((pairs, pairs), BF16),
        ],
        compiler_params=pltpu.CompilerParams(vmem_limit_bytes=58 << 20),
        name="excite",
    )(
        place,
        jnp.asarray(lane),
        alpha_whole,
        beta_whole,
        flat,
        alpha_source,
        alpha_sign,
        beta_source,
        beta_sign,
    )
    send, keep, one = list(results[:streams]), list(results[streams:-1]), results[-1]
    got = [swap(send[s], "beta", 0, sizes["beta"]) for s in range(streams)]
    one = one + swap(one, "beta", 0, sizes["beta"])
    steps = len(orders[0])
    for t in range(steps):
        for s in range(streams):
            kind, bit = orders[s][t]
            n = keep[s].shape[0] // 2
            out = keep[s][n:] + got[s][n:]
            mine = keep[s][:n] + got[s][:n]
            got[s] = swap(out, kind, bit, sizes[kind])
            keep[s] = mine
        kind, bit = orders[0][t]
        if t < steps - 1:
            one = one + swap(one, kind, bit, sizes[kind])
        else:
            other = swap(one, kind, bit, sizes[kind])
    one_body, two_body = pl.pallas_call(
        functools.partial(last_kernel, columns),
        out_shape=[
            jax.ShapeDtypeStruct((states, total), F32),
            jax.ShapeDtypeStruct((rows_each, total), F32),
        ],
        in_specs=[vmem] * (3 + 2 * streams),
        out_specs=[vmem] * 2,
        name="finish",
    )(jnp.asarray(inverse), one, other, *keep, *got)
    return (one_body, two_body)


def solution(mesh):
    return jax.shard_map(
        functools.partial(shards, dict(mesh.shape)),
        mesh=mesh,
        in_specs=(
            P(None, "alpha", "beta"),
            P("alpha", None),
            P("alpha", None),
            P("beta", None),
            P("beta", None),
        ),
        out_specs=(P(), P(("alpha", "beta"), None)),
        check_vma=False,
    )
```

profile of v0, /device:TPU:0, one launch (start us, length us, event | category | flops | bytes accessed | tf_op | source)
XLA Modules:
  0.0 117.6 jit_solution(8212038206980035687)
XLA Ops:
  0.6 0.0 copy-start.2
  0.6 17.6 %all_gather.6.alpha_ref = f32[4,128,128]{2,1,0:T(8,128)} all-gather(f32[4,32,128]{2,1,0:T(8,128)} %param.7), channel_id=1, replica_groups=mesh['alpha'=4,'beta'=8] {'alpha'}, dimensions={1}, use_global_device_ids=true | all-gather | bytes 327680 | tf_op jit(solution)/shard_map/all_gather | solution.py:282
  18.3 0.0 copy-done.2
  18.3 12.0 %all_gather.7.beta_ref = f32[4,32,1024]{2,1,0:T(8,128)} all-gather(f32[4,32,128]{2,1,0:T(8,128)S(1)} %copy-done.2), channel_id=1, replica_groups=mesh['alpha'=4,'beta'=8] {'beta'}, dimensions={2}, use_global_device_ids=true | all-gather | bytes 589824 | tf_op jit(solution)/shard_map/all_gather | solution.py:283
  30.2 0.1 copy.10
  30.4 0.8 reshape.7.flat_ref
  31.2 0.7 pad_add_fusion.place_ref
  31.8 35.1 %excite.1 = (f32[512,384]{1,0:T(8,128)}, f32[512,384]{1,0:T(8,128)}, f32[512,256]{1,0:T(8,128)}, f32[512,384]{1,0:T(8,128)}, f32[512,384]{1,0:T(8,128)}, /*index=5*/f32[512,256]{1,0:T(8,128)}, f32[4,1024]{1,0:T(4,128)}) custom-call(s32[2]{0:T(128)} %pad_add_fusion.place_ref, s32[1,256]{1,0:T(1,128)} %constant.12.clone.lane_ref, ...), custom_call_target="tpu_custom_call" | custom-call | tf_op jit(solution)/shard_map/excite/pallas_call | solution.py:300
  67.0 0.3 collective-permute-start.13
  67.3 0.2 collective-permute-start.5
  67.5 0.3 collective-permute-start.9
  67.8 1.3 %collective-permute-done.13 = f32[512,256]{1,0:T(8,128)S(1)} collective-permute-done((f32[512,256]{1,0:T(8,128)}, f32[512,256]{1,0:T(8,128)S(1)}, u32[]{:S(2)}, u32[]{:S(2)}) %collective-permute-start.13) | collective-permute-done | bytes 524320 | tf_op jit(solution)/shard_map/ppermute | solution.py:267
  69.1 1.1 slice_add_fusion.5
  70.2 0.0 copy-start.1
  70.2 0.6 collective-permute-start.14
  70.8 0.0 copy-done.7
  70.8 0.1 collective-permute-start
  70.8 1.1 collective-permute-done
  72.0 1.4 %collective-permute-start.1 = (f32[4,1024]{1,0:T(4,128)S(1)}, f32[4,1024]{1,0:T(4,128)S(1)}, u32[]{:S(2)}, u32[]{:S(2)}) collective-permute-start(f32[4,1024]{1,0:T(4,128)S(1)} %add.84), channel_id=1, source_target_pairs={{0,2},{1,3},{2,0},{3,1},{4,6},{5,7},{6,4},{7,5},{8,10},{9,11},{10,... | collective-permute-start | bytes 49160 | tf_op jit(solution)/shard_map/ppermute | solution.py:267
  73.4 2.3 %collective-permute-done.1 = f32[4,1024]{1,0:T(4,128)S(1)} collective-permute-done((f32[4,1024]{1,0:T(4,128)S(1)}, f32[4,1024]{1,0:T(4,128)S(1)}, u32[]{:S(2)}, u32[]{:S(2)}) %collective-permute-start.1) | collective-permute-done | bytes 16416 | tf_op jit(solution)/shard_map/ppermute | solution.py:267
  75.7 1.4 %collective-permute-start.2 = (f32[4,1024]{1,0:T(4,128)S(1)}, f32[4,1024]{1,0:T(4,128)S(1)}, u32[]{:S(2)}, u32[]{:S(2)}) collective-permute-start(f32[4,1024]{1,0:T(4,128)S(1)} %add.85), channel_id=1, source_target_pairs={{0,4},{1,5},{2,6},{3,7},{4,0},{5,1},{6,2},{7,3},{8,12},{9,13},{10,... | collective-permute-start | bytes 49160 | tf_op jit(solution)/shard_map/ppermute | solution.py:267
  77.1 2.3 %collective-permute-done.2 = f32[4,1024]{1,0:T(4,128)S(1)} collective-permute-done((f32[4,1024]{1,0:T(4,128)S(1)}, f32[4,1024]{1,0:T(4,128)S(1)}, u32[]{:S(2)}, u32[]{:S(2)}) %collective-permute-start.2) | collective-permute-done | bytes 16416 | tf_op jit(solution)/shard_map/ppermute | solution.py:267
  79.5 1.5 %collective-permute-start.3 = (f32[4,1024]{1,0:T(4,128)S(1)}, f32[4,1024]{1,0:T(4,128)S(1)}, u32[]{:S(2)}, u32[]{:S(2)}) collective-permute-start(f32[4,1024]{1,0:T(4,128)S(1)} %add.86), channel_id=1, source_target_pairs={{0,8},{8,0},{16,24},{24,16},{1,9},{9,1},{17,25},{25,17},{2,10},{10... | collective-permute-start | bytes 49160 | tf_op jit(solution)/shard_map/ppermute | solution.py:267
  81.0 0.0 collective-permute-done.14
  81.0 1.1 collective-permute-start.15
  82.1 0.0 collective-permute-done.5
  82.1 0.0 copy-done.1
  82.1 0.1 slice_add_fusion.3
  82.2 1.5 %collective-permute-start.6 = (f32[256,384]{1,0:T(8,128)S(1)}, f32[256,384]{1,0:T(8,128)S(1)}, u32[]{:S(2)}, u32[]{:S(2)}) collective-permute-start(f32[256,384]{1,0:T(8,128)S(1)} %get-tuple-element.19), channel_id=1, source_target_pairs={{0,2},{1,3},{2,0},{3,1},{4,6},{5,7},{6,4},{7,5},{8,10},{9,11},{10,... | collective-permute-start | bytes 1179656 | tf_op jit(solution)/shard_map/ppermute | solution.py:267
  83.7 0.0 collective-permute-done.9
  83.7 0.0 copy-done
  83.7 0.1 slice_add_fusion.1
  83.8 1.0 collective-permute-start.10
  84.8 3.5 %collective-permute-done.15 = f32[128,256]{1,0:T(8,128)S(1)} collective-permute-done((f32[128,256]{1,0:T(8,128)S(1)}, f32[128,256]{1,0:T(8,128)S(1)}, u32[]{:S(2)}, u32[]{:S(2)}) %collective-permute-start.15) | collective-permute-done | bytes 131104 | tf_op jit(solution)/shard_map/ppermute | solution.py:267
  88.3 1.5 %collective-permute-start.16 = (f32[64,256]{1,0:T(8,128)S(1)}, f32[64,256]{1,0:T(8,128)S(1)}, u32[]{:S(2)}, u32[]{:S(2)}) collective-permute-start(f32[64,256]{1,0:T(8,128)S(1)} %get-tuple-element.33), channel_id=1, source_target_pairs={{0,2},{1,3},{2,0},{3,1},{4,6},{5,7},{6,4},{7,5},{8,10},{9,11},{10,... | collective-permute-start | bytes 196616 | tf_op jit(solution)/shard_map/ppermute | solution.py:267
  89.8 2.3 %collective-permute-done.6 = f32[256,384]{1,0:T(8,128)S(1)} collective-permute-done((f32[256,384]{1,0:T(8,128)S(1)}, f32[256,384]{1,0:T(8,128)S(1)}, u32[]{:S(2)}, u32[]{:S(2)}) %collective-permute-start.6) | collective-permute-done | bytes 393248 | tf_op jit(solution)/shard_map/ppermute | solution.py:267
  92.1 1.5 %collective-permute-start.7 = (f32[128,384]{1,0:T(8,128)S(1)}, f32[128,384]{1,0:T(8,128)S(1)}, u32[]{:S(2)}, u32[]{:S(2)}) collective-permute-start(f32[128,384]{1,0:T(8,128)S(1)} %get-tuple-element.25), channel_id=1, source_target_pairs={{0,4},{1,5},{2,6},{3,7},{4,0},{5,1},{6,2},{7,3},{8,12},{9,13},{10,... | collective-permute-start | bytes 589832 | tf_op jit(solution)/shard_map/ppermute | solution.py:267
  93.6 0.4 collective-permute-done.10
  94.1 2.0 %collective-permute-start.11 = (f32[128,384]{1,0:T(8,128)S(1)}, f32[128,384]{1,0:T(8,128)S(1)}, u32[]{:S(2)}, u32[]{:S(2)}) collective-permute-start(f32[128,384]{1,0:T(8,128)S(1)} %get-tuple-element.23), channel_id=1, source_target_pairs={{0,8},{8,0},{16,24},{24,16},{1,9},{9,1},{17,25},{25,17},{2,10},{10... | collective-permute-start | bytes 589832 | tf_op jit(solution)/shard_map/ppermute | solution.py:267
  96.1 1.8 %collective-permute-done.7 = f32[128,384]{1,0:T(8,128)S(1)} collective-permute-done((f32[128,384]{1,0:T(8,128)S(1)}, f32[128,384]{1,0:T(8,128)S(1)}, u32[]{:S(2)}, u32[]{:S(2)}) %collective-permute-start.7) | collective-permute-done | bytes 196640 | tf_op jit(solution)/shard_map/ppermute | solution.py:267
  97.9 1.6 %collective-permute-start.8 = (f32[64,384]{1,0:T(8,128)S(1)}, f32[64,384]{1,0:T(8,128)S(1)}, u32[]{:S(2)}, u32[]{:S(2)}) collective-permute-start(f32[64,384]{1,0:T(8,128)S(1)} %get-tuple-element.31), channel_id=1, source_target_pairs={{0,8},{8,0},{16,24},{24,16},{1,9},{9,1},{17,25},{25,17},{2,10},{10... | collective-permute-start | bytes 294920 | tf_op jit(solution)/shard_map/ppermute | solution.py:267
  99.5 2.0 %collective-permute-done.11 = f32[128,384]{1,0:T(8,128)S(1)} collective-permute-done((f32[128,384]{1,0:T(8,128)S(1)}, f32[128,384]{1,0:T(8,128)S(1)}, u32[]{:S(2)}, u32[]{:S(2)}) %collective-permute-start.11) | collective-permute-done | bytes 196640 | tf_op jit(solution)/shard_map/ppermute | solution.py:267
  101.5 1.8 %collective-permute-start.12 = (f32[64,384]{1,0:T(8,128)S(1)}, f32[64,384]{1,0:T(8,128)S(1)}, u32[]{:S(2)}, u32[]{:S(2)}) collective-permute-start(f32[64,384]{1,0:T(8,128)S(1)} %get-tuple-element.29), channel_id=1, source_target_pairs={{0,16},{8,24},{16,0},{24,8},{1,17},{9,25},{17,1},{25,9},{2,18},{10... | collective-permute-start | bytes 294920 | tf_op jit(solution)/shard_map/ppermute | solution.py:267
  103.3 0.0 collective-permute-done.8
  103.3 0.6 slice_add_fusion.19
  103.9 1.2 %collective-permute-start.17 = (f32[32,384]{1,0:T(8,128)S(1)}, f32[32,384]{1,0:T(8,128)S(1)}, u32[]{:S(2)}, u32[]{:S(2)}) collective-permute-start(f32[32,384]{1,0:T(8,128)S(1)} %get-tuple-element.36), channel_id=1, source_target_pairs={{0,16},{8,24},{16,0},{24,8},{1,17},{9,25},{17,1},{25,9},{2,18},{10... | collective-permute-start | bytes 147464 | tf_op jit(solution)/shard_map/ppermute | solution.py:267
  105.1 2.0 %collective-permute-done.12 = f32[64,384]{1,0:T(8,128)S(1)} collective-permute-done((f32[64,384]{1,0:T(8,128)S(1)}, f32[64,384]{1,0:T(8,128)S(1)}, u32[]{:S(2)}, u32[]{:S(2)}) %collective-permute-start.12) | collective-permute-done | bytes 98336 | tf_op jit(solution)/shard_map/ppermute | solution.py:267
  107.1 0.6 slice_add_fusion.18
  107.7 1.3 %collective-permute-start.18 = (f32[32,384]{1,0:T(8,128)S(1)}, f32[32,384]{1,0:T(8,128)S(1)}, u32[]{:S(2)}, u32[]{:S(2)}) collective-permute-start(f32[32,384]{1,0:T(8,128)S(1)} %get-tuple-element.34), channel_id=1, source_target_pairs={{0,2},{1,3},{2,0},{3,1},{4,6},{5,7},{6,4},{7,5},{8,10},{9,11},{10,... | collective-permute-start | bytes 147464 | tf_op jit(solution)/shard_map/ppermute | solution.py:267
  109.0 0.0 collective-permute-done.16
  109.0 0.6 slice_add_fusion.22
  109.6 0.8 collective-permute-start.19
  110.4 0.0 collective-permute-done.3
  110.4 1.9 %collective-permute-start.4 = (f32[4,1024]{1,0:T(4,128)S(1)}, f32[4,1024]{1,0:T(4,128)S(1)}, u32[]{:S(2)}, u32[]{:S(2)}) collective-permute-start(f32[4,1024]{1,0:T(4,128)S(1)} %add.87.one_a_ref), channel_id=1, source_target_pairs={{0,16},{8,24},{16,0},{24,8},{1,17},{9,25},{17,1},{25,9},{2,18},{10... | collective-permute-start | bytes 49160 | tf_op jit(solution)/shard_map/ppermute | solution.py:267
  112.3 2.8 %collective-permute-done.4.one_b_ref = f32[4,1024]{1,0:T(4,128)S(1)} collective-permute-done((f32[4,1024]{1,0:T(4,128)S(1)}, f32[4,1024]{1,0:T(4,128)S(1)}, u32[]{:S(2)}, u32[]{:S(2)}) %collective-permute-start.4) | collective-permute-done | bytes 16416 | tf_op jit(solution)/shard_map/ppermute | solution.py:267
  115.1 0.0 collective-permute-done.19.refs_5_
  115.1 0.0 collective-permute-done.17.refs_3_
  115.1 0.0 copy-start.4
  115.1 0.0 collective-permute-done.18.refs_4_
  115.1 0.5 copy-done.8
  115.7 0.0 copy-done.6
  115.7 0.0 copy-done.4
  115.7 0.0 copy-done.5
  115.7 1.8 %finish.1 = (f32[4,1024]{1,0:T(4,128)}, f32[32,1024]{1,0:T(8,128)}) custom-call(s32[1,256]{1,0:T(1,128)} %constant.13.clone.lane_ref, f32[4,1024]{1,0:T(4,128)} %copy-done.3, f32[4,1024]{1,0:T(4,128)} %copy-done.8, f32[32,384]{1,0:T(8,128)} %get-tuple-element.37.refs_0_, f32[32,384]{1,0:T(8,128)} %get-tuple-element.35.refs_1_, ...), custom_call_target="tpu_custom_call" | custom-call | tf_op jit(solution)/shard_map/finish/pallas_call | solution.py:351
  (17 shorter events, 0.2 us)
Async XLA Ops:
  0.6 17.6 %copy-start.2 = (f32[4,32,128]{2,1,0:T(8,128)S(1)}, f32[4,32,128]{2,1,0:T(8,128)}, u32[]{:S(2)}) copy-start(f32[4,32,128]{2,1,0:T(8,128)} %param.7) | copy-start | bytes 196612
  67.0 2.1 %collective-permute-start.13 = (f32[512,256]{1,0:T(8,128)}, f32[512,256]{1,0:T(8,128)S(1)}, u32[]{:S(2)}, u32[]{:S(2)}) collective-permute-start(f32[512,256]{1,0:T(8,128)} %get-tuple-element.15), channel_id=1, source_target_pairs={{0,1},{1,0},{2,3},{3,2},{4,5},{5,4},{6,7},{7,6},{8,9},{9,8},{10,11... | collective-permute-start | bytes 1572872 | tf_op jit(solution)/shard_map/ppermute | solution.py:267
  67.3 14.8 %collective-permute-start.5 = (f32[512,384]{1,0:T(8,128)}, f32[512,384]{1,0:T(8,128)S(1)}, u32[]{:S(2)}, u32[]{:S(2)}) collective-permute-start(f32[512,384]{1,0:T(8,128)} %get-tuple-element.11), channel_id=1, source_target_pairs={{0,1},{1,0},{2,3},{3,2},{4,5},{5,4},{6,7},{7,6},{8,9},{9,8},{10,11... | collective-permute-start | bytes 2359304 | tf_op jit(solution)/shard_map/ppermute | solution.py:267
  67.5 16.2 %collective-permute-start.9 = (f32[512,384]{1,0:T(8,128)}, f32[512,384]{1,0:T(8,128)S(1)}, u32[]{:S(2)}, u32[]{:S(2)}) collective-permute-start(f32[512,384]{1,0:T(8,128)} %get-tuple-element.13), channel_id=1, source_target_pairs={{0,1},{1,0},{2,3},{3,2},{4,5},{5,4},{6,7},{7,6},{8,9},{9,8},{10,11... | collective-permute-start | bytes 2359304 | tf_op jit(solution)/shard_map/ppermute | solution.py:267
  69.1 1.7 %copy-start.7 = (f32[4,1024]{1,0:T(4,128)S(1)}, f32[4,1024]{1,0:T(4,128)}, u32[]{:S(2)}) copy-start(f32[4,1024]{1,0:T(4,128)} %get-tuple-element.9) | copy-start | bytes 49156
  70.2 11.9 %copy-start.1 = (f32[512,384]{1,0:T(8,128)S(1)}, f32[512,384]{1,0:T(8,128)}, u32[]{:S(2)}) copy-start(f32[512,384]{1,0:T(8,128)} %get-tuple-element.10) | copy-start | bytes 2359300
  70.2 10.8 %collective-permute-start.14 = (f32[256,256]{1,0:T(8,128)S(1)}, f32[256,256]{1,0:T(8,128)S(1)}, u32[]{:S(2)}, u32[]{:S(2)}) collective-permute-start(f32[256,256]{1,0:T(8,128)S(1)} %get-tuple-element.21), channel_id=1, source_target_pairs={{0,8},{8,0},{16,24},{24,16},{1,9},{9,1},{17,25},{25,17},{2,10},{10... | collective-permute-start | bytes 786440 | tf_op jit(solution)/shard_map/ppermute | solution.py:267
  70.8 1.2 %collective-permute-start = (f32[4,1024]{1,0:T(4,128)S(1)}, f32[4,1024]{1,0:T(4,128)S(1)}, u32[]{:S(2)}, u32[]{:S(2)}) collective-permute-start(f32[4,1024]{1,0:T(4,128)S(1)} %copy-done.7), channel_id=1, source_target_pairs={{0,1},{1,0},{2,3},{3,2},{4,5},{5,4},{6,7},{7,6},{8,9},{9,8},{10,11... | collective-permute-start | bytes 49160 | tf_op jit(solution)/shard_map/ppermute | solution.py:267
  72.0 3.7 %collective-permute-start.1 = (f32[4,1024]{1,0:T(4,128)S(1)}, f32[4,1024]{1,0:T(4,128)S(1)}, u32[]{:S(2)}, u32[]{:S(2)}) collective-permute-start(f32[4,1024]{1,0:T(4,128)S(1)} %add.84), channel_id=1, source_target_pairs={{0,2},{1,3},{2,0},{3,1},{4,6},{5,7},{6,4},{7,5},{8,10},{9,11},{10,... | collective-permute-start | bytes 49160 | tf_op jit(solution)/shard_map/ppermute | solution.py:267
  75.7 3.7 %collective-permute-start.2 = (f32[4,1024]{1,0:T(4,128)S(1)}, f32[4,1024]{1,0:T(4,128)S(1)}, u32[]{:S(2)}, u32[]{:S(2)}) collective-permute-start(f32[4,1024]{1,0:T(4,128)S(1)} %add.85), channel_id=1, source_target_pairs={{0,4},{1,5},{2,6},{3,7},{4,0},{5,1},{6,2},{7,3},{8,12},{9,13},{10,... | collective-permute-start | bytes 49160 | tf_op jit(solution)/shard_map/ppermute | solution.py:267
  79.5 30.9 %collective-permute-start.3 = (f32[4,1024]{1,0:T(4,128)S(1)}, f32[4,1024]{1,0:T(4,128)S(1)}, u32[]{:S(2)}, u32[]{:S(2)}) collective-permute-start(f32[4,1024]{1,0:T(4,128)S(1)} %add.86), channel_id=1, source_target_pairs={{0,8},{8,0},{16,24},{24,16},{1,9},{9,1},{17,25},{25,17},{2,10},{10... | collective-permute-start | bytes 49160 | tf_op jit(solution)/shard_map/ppermute | solution.py:267
  81.0 7.3 %collective-permute-start.15 = (f32[128,256]{1,0:T(8,128)S(1)}, f32[128,256]{1,0:T(8,128)S(1)}, u32[]{:S(2)}, u32[]{:S(2)}) collective-permute-start(f32[128,256]{1,0:T(8,128)S(1)} %get-tuple-element.27), channel_id=1, source_target_pairs={{0,16},{8,24},{16,0},{24,8},{1,17},{9,25},{17,1},{25,9},{2,18},{10... | collective-permute-start | bytes 393224 | tf_op jit(solution)/shard_map/ppermute | solution.py:267
  82.1 1.6 %copy-start = (f32[512,384]{1,0:T(8,128)S(1)}, f32[512,384]{1,0:T(8,128)}, u32[]{:S(2)}) copy-start(f32[512,384]{1,0:T(8,128)} %get-tuple-element.12) | copy-start | bytes 2359300
  82.2 9.9 %collective-permute-start.6 = (f32[256,384]{1,0:T(8,128)S(1)}, f32[256,384]{1,0:T(8,128)S(1)}, u32[]{:S(2)}, u32[]{:S(2)}) collective-permute-start(f32[256,384]{1,0:T(8,128)S(1)} %get-tuple-element.19), channel_id=1, source_target_pairs={{0,2},{1,3},{2,0},{3,1},{4,6},{5,7},{6,4},{7,5},{8,10},{9,11},{10,... | collective-permute-start | bytes 1179656 | tf_op jit(solution)/shard_map/ppermute | solution.py:267
  83.8 10.3 %collective-permute-start.10 = (f32[256,384]{1,0:T(8,128)S(1)}, f32[256,384]{1,0:T(8,128)S(1)}, u32[]{:S(2)}, u32[]{:S(2)}) collective-permute-start(f32[256,384]{1,0:T(8,128)S(1)} %get-tuple-element.17), channel_id=1, source_target_pairs={{0,4},{1,5},{2,6},{3,7},{4,0},{5,1},{6,2},{7,3},{8,12},{9,13},{10,... | collective-permute-start | bytes 1179656 | tf_op jit(solution)/shard_map/ppermute | solution.py:267
  88.3 20.6 %collective-permute-start.16 = (f32[64,256]{1,0:T(8,128)S(1)}, f32[64,256]{1,0:T(8,128)S(1)}, u32[]{:S(2)}, u32[]{:S(2)}) collective-permute-start(f32[64,256]{1,0:T(8,128)S(1)} %get-tuple-element.33), channel_id=1, source_target_pairs={{0,2},{1,3},{2,0},{3,1},{4,6},{5,7},{6,4},{7,5},{8,10},{9,11},{10,... | collective-permute-start | bytes 196616 | tf_op jit(solution)/shard_map/ppermute | solution.py:267
  92.1 5.7 %collective-permute-start.7 = (f32[128,384]{1,0:T(8,128)S(1)}, f32[128,384]{1,0:T(8,128)S(1)}, u32[]{:S(2)}, u32[]{:S(2)}) collective-permute-start(f32[128,384]{1,0:T(8,128)S(1)} %get-tuple-element.25), channel_id=1, source_target_pairs={{0,4},{1,5},{2,6},{3,7},{4,0},{5,1},{6,2},{7,3},{8,12},{9,13},{10,... | collective-permute-start | bytes 589832 | tf_op jit(solution)/shard_map/ppermute | solution.py:267
  94.1 7.4 %collective-permute-start.11 = (f32[128,384]{1,0:T(8,128)S(1)}, f32[128,384]{1,0:T(8,128)S(1)}, u32[]{:S(2)}, u32[]{:S(2)}) collective-permute-start(f32[128,384]{1,0:T(8,128)S(1)} %get-tuple-element.23), channel_id=1, source_target_pairs={{0,8},{8,0},{16,24},{24,16},{1,9},{9,1},{17,25},{25,17},{2,10},{10... | collective-permute-start | bytes 589832 | tf_op jit(solution)/shard_map/ppermute | solution.py:267
  97.9 5.4 %collective-permute-start.8 = (f32[64,384]{1,0:T(8,128)S(1)}, f32[64,384]{1,0:T(8,128)S(1)}, u32[]{:S(2)}, u32[]{:S(2)}) collective-permute-start(f32[64,384]{1,0:T(8,128)S(1)} %get-tuple-element.31), channel_id=1, source_target_pairs={{0,8},{8,0},{16,24},{24,16},{1,9},{9,1},{17,25},{25,17},{2,10},{10... | collective-permute-start | bytes 294920 | tf_op jit(solution)/shard_map/ppermute | solution.py:267
  101.5 5.6 %collective-permute-start.12 = (f32[64,384]{1,0:T(8,128)S(1)}, f32[64,384]{1,0:T(8,128)S(1)}, u32[]{:S(2)}, u32[]{:S(2)}) collective-permute-start(f32[64,384]{1,0:T(8,128)S(1)} %get-tuple-element.29), channel_id=1, source_target_pairs={{0,16},{8,24},{16,0},{24,8},{1,17},{9,25},{17,1},{25,9},{2,18},{10... | collective-permute-start | bytes 294920 | tf_op jit(solution)/shard_map/ppermute | solution.py:267
  103.9 11.2 %collective-permute-start.17 = (f32[32,384]{1,0:T(8,128)S(1)}, f32[32,384]{1,0:T(8,128)S(1)}, u32[]{:S(2)}, u32[]{:S(2)}) collective-permute-start(f32[32,384]{1,0:T(8,128)S(1)} %get-tuple-element.36), channel_id=1, source_target_pairs={{0,16},{8,24},{16,0},{24,8},{1,17},{9,25},{17,1},{25,9},{2,18},{10... | collective-permute-start | bytes 147464 | tf_op jit(solution)/shard_map/ppermute | solution.py:267
  107.7 7.4 %collective-permute-start.18 = (f32[32,384]{1,0:T(8,128)S(1)}, f32[32,384]{1,0:T(8,128)S(1)}, u32[]{:S(2)}, u32[]{:S(2)}) collective-permute-start(f32[32,384]{1,0:T(8,128)S(1)} %get-tuple-element.34), channel_id=1, source_target_pairs={{0,2},{1,3},{2,0},{3,1},{4,6},{5,7},{6,4},{7,5},{8,10},{9,11},{10,... | collective-permute-start | bytes 147464 | tf_op jit(solution)/shard_map/ppermute | solution.py:267
  109.6 5.5 %collective-permute-start.19 = (f32[32,256]{1,0:T(8,128)S(1)}, f32[32,256]{1,0:T(8,128)S(1)}, u32[]{:S(2)}, u32[]{:S(2)}) collective-permute-start(f32[32,256]{1,0:T(8,128)S(1)} %get-tuple-element.38), channel_id=1, source_target_pairs={{0,4},{1,5},{2,6},{3,7},{4,0},{5,1},{6,2},{7,3},{8,12},{9,13},{10,... | collective-permute-start | bytes 98312 | tf_op jit(solution)/shard_map/ppermute | solution.py:267
  110.4 4.8 %copy-start.3 = (f32[4,1024]{1,0:T(4,128)}, f32[4,1024]{1,0:T(4,128)S(1)}, u32[]{:S(2)}) copy-start(f32[4,1024]{1,0:T(4,128)S(1)} %add.87.one_a_ref) | copy-start | bytes 49156
  110.4 4.7 %collective-permute-start.4 = (f32[4,1024]{1,0:T(4,128)S(1)}, f32[4,1024]{1,0:T(4,128)S(1)}, u32[]{:S(2)}, u32[]{:S(2)}) collective-permute-start(f32[4,1024]{1,0:T(4,128)S(1)} %add.87.one_a_ref), channel_id=1, source_target_pairs={{0,16},{8,24},{16,0},{24,8},{1,17},{9,25},{17,1},{25,9},{2,18},{10... | collective-permute-start | bytes 49160 | tf_op jit(solution)/shard_map/ppermute | solution.py:267
  115.1 0.6 copy-start.8
  115.1 0.6 copy-start.6
  115.1 0.6 copy-start.4
  115.1 0.6 copy-start.5
where the time goes:
time: 118 us
  Pallas kernels  36.9 us (31%)
  blocking collectives  29.6 us (25%)
  starting transfers between devices  22.9 us (19%)
  waiting for transfers between devices  21.8 us (18%)
  other arithmetic  4 us (3%)
  local copies, waits for them, and re-layouts  1.54 us (1%)
    pallas_call x1, Pallas kernels, shards(): pl.pallas_call(functools.partial(main_kernel, rows_each, orders, columns)...  35.1 us
    ppermute x20, starting transfers between devices, swap(): return lax.ppermute(value, kind, [(i, i ^ 1 << bit) for i in range(size)])  22.9 us
    ppermute x20, waiting for transfers between devices, swap(): return lax.ppermute(value, kind, [(i, i ^ 1 << bit) for i in range(size)])  21.8 us
    all_gather x1, blocking collectives, shards(): alpha_whole = lax.all_gather(ci_vectors, 'alpha', axis=1, tiled=True)  17.6 us
    all_gather x1, blocking collectives, shards(): beta_whole = lax.all_gather(ci_vectors, 'beta', axis=2, tiled=True)  12 us
  transfers between devices with their start and end apart: 20, of which 11 were waited for; matrix products, arithmetic and copies ran while one was open for 3% of the time, Pallas kernels for 0%

commit v1 on v0

--- a/solution.py
+++ b/solution.py
@@ -11,6 +11,7 @@
 F32 = jnp.float32
 BF16 = jnp.bfloat16
 LANES = 128
+ONE_ROWS = 16
 
 
 def pair_lanes(norb):
@@ -41,10 +42,9 @@
     rows_each,
     orders,
     columns,
+    parts,
     place_ref,
     lane_ref,
-    alpha_ref,
-    beta_ref,
     flat_ref,
     asrc_ref,
     asgn_ref,
@@ -52,10 +52,13 @@
     bsgn_ref,
     *refs,
 ):
+    alpha_parts, beta_parts = parts
+    alpha_refs = refs[:alpha_parts]
+    beta_refs = (refs[0],) + refs[alpha_parts : alpha_parts + beta_parts - 1]
+    refs = refs[alpha_parts + beta_parts - 1 :]
     streams = len(columns)
     send_refs = refs[:streams]
     keep_refs = refs[streams : 2 * streams]
-    one_ref = refs[2 * streams]
     (
         table_ref,
         turned_ref,
@@ -70,10 +73,9 @@
         left_ref,
         state_ref,
         perm_ref,
-    ) = refs[2 * streams + 1 :]
-    states, alpha_count, beta_rows = alpha_ref.shape
-    alpha_rows = beta_ref.shape[1]
-    beta_count = beta_ref.shape[2]
+    ) = refs[2 * streams :]
+    states, alpha_rows, beta_rows = alpha_refs[0].shape
+    beta_count = beta_parts * beta_rows
     both = states * alpha_rows
     pairs = 2 * LANES
     my_alpha = place_ref[0]
@@ -81,28 +83,30 @@
     forward = lane_ref[0:1, 0:LANES]
     backward = lane_ref[0:1, LANES:pairs]
 
-    def tables(src_ref, sgn_ref, idx_ref, sf_ref, sb_ref, count):
+    def tables(src_ref, sgn_ref, idx_ref, sf_ref, sb_ref, count, flip):
         for r in range(0, count, 8):
             rows = slice(r, r + 8)
             s0, s1 = sgn_ref[rows, 0:LANES], sgn_ref[rows, LANES:pairs]
             i0, i1 = src_ref[rows, 0:LANES], src_ref[rows, LANES:pairs]
             sf = pick_lanes(s0, s1, forward)
             sb = pick_lanes(s0, s1, backward)
-            idx_ref[rows, :] = jnp.where(
+            source = jnp.where(
                 sf != 0, pick_lanes(i0, i1, forward), pick_lanes(i0, i1, backward)
             )
+            idx_ref[rows, :] = source ^ flip
             sf_ref[rows, :] = sf.astype(F32)
             sb_ref[rows, :] = sb.astype(F32)
 
-    tables(asrc_ref, asgn_ref, aidx_ref, asf_ref, asb_ref, alpha_rows)
-    tables(bsrc_ref, bsgn_ref, bidx_ref, bsf_ref, bsb_ref, beta_rows)
-
-    whole = beta_ref[...].reshape(both, beta_count)
-    high, mid = split_two(whole)
-    table_ref[0:both, :] = high
-    table_ref[both : 2 * both, :] = mid
+    tables(asrc_ref, asgn_ref, aidx_ref, asf_ref, asb_ref, alpha_rows, my_alpha * alpha_rows)
+    tables(bsrc_ref, bsgn_ref, bidx_ref, bsf_ref, bsb_ref, beta_rows, my_beta * beta_rows)
+
+    for k in range(beta_parts):
+        high, mid = split_two(beta_refs[k][...].reshape(both, beta_rows))
+        table_ref[0:both, k * beta_rows : (k + 1) * beta_rows] = high
+        table_ref[both : 2 * both, k * beta_rows : (k + 1) * beta_rows] = mid
     for j in range(states):
-        turned_ref[j] = alpha_ref[j].T
+        rows = jnp.concatenate([alpha_refs[k][j] for k in range(alpha_parts)], axis=0)
+        turned_ref[j] = rows.T
 
     flat = flat_ref[...]
     flat_high = flat.astype(BF16).astype(F32)
@@ -118,7 +122,7 @@
 
     chunk = min(1024, beta_count)
     chunks = beta_count // chunk
-    step = 4
+    step = 16
 
     def one_hot_dot(idx0, idx1, first):
         where = lax.broadcasted_iota(jnp.int32, (chunk, LANES), 0) + first
@@ -211,7 +215,8 @@
                     source = jb if kind == "beta" else ja
                     place = 2 * place + ((source >> bit) & 1)
                 target = send_refs[s] if jb & 1 else keep_refs[s]
-                target[place * rows_each : (place + 1) * rows_each, :] = rows[
+                first_row = place * rows_each + (ONE_ROWS if s == streams - 1 else 0)
+                target[first_row : first_row + rows_each, :] = rows[
                     :, first_col : first_col + columns[s]
                 ]
                 first_col += columns[s]
@@ -219,52 +224,48 @@
     one = jnp.dot(state_ref[...], right_ref[...], preferred_element_type=F32)
     one_low = jnp.dot(state_ref[...], low_ref[...], preferred_element_type=F32)
     total = one + one_low
-    one_ref[...] = total[0:states] + total[states : 2 * states]
-
-
-def last_kernel(columns, lane_ref, one_a_ref, one_b_ref, *refs):
-    streams = len(columns)
-    kept, got = refs[:streams], refs[streams : 2 * streams]
-    one_ref, two_ref = refs[2 * streams :]
+    one = total[0:states] + total[states : 2 * states]
+    one_rows = jnp.concatenate(
+        [one[:, j * pairs : (j + 1) * pairs] for j in range(states)], axis=0
+    )
+    send_refs[-1][0:ONE_ROWS, :] = one_rows
+    keep_refs[-1][0:ONE_ROWS, :] = one_rows
+
+
+def last_kernel(groups, lane_ref, *refs):
+    count = len(groups)
+    kept, got = refs[:count], refs[count : 2 * count]
+    one_ref, two_ref = refs[2 * count :]
     pairs = 2 * LANES
     back0, back1 = lane_ref[0:1, 0:LANES], lane_ref[0:1, LANES:pairs]
-    value = jnp.concatenate([kept[s][...] + got[s][...] for s in range(streams)], axis=1)
-
-    def place(whole, out_ref):
+    sums = [kept[s][...] + got[s][...] for s in range(count)]
+    one_rows = sums[-1][0:ONE_ROWS]
+    states = ONE_ROWS // one_ref.shape[0]
+    sums[-1] = sums[-1][ONE_ROWS:]
+    value = jnp.concatenate(sums, axis=1)
+
+    def place(whole, out_ref, first_col):
         rows, total = whole.shape
         for col in range(0, total, pairs):
             for r in range(0, rows, 8):
                 n = min(8, rows - r)
                 left = whole[r : r + n, col : col + LANES]
                 right = whole[r : r + n, col + LANES : col + pairs]
-                out_ref[r : r + n, col : col + LANES] = pick_lanes(left, right, back0)
-                out_ref[r : r + n, col + LANES : col + pairs] = pick_lanes(left, right, back1)
-
-    def full(whole):
-        rows = whole.shape[0]
-        if rows % 8 == 0:
-            return whole
-        return jnp.concatenate([whole] * (8 // rows), axis=0)
-
-    place_rows(place, full, value, two_ref)
-    place_rows(place, full, one_a_ref[...] + one_b_ref[...], one_ref)
-
-
-def place_rows(place, full, whole, out_ref):
-    rows = whole.shape[0]
-    if rows % 8 == 0:
-        place(whole, out_ref)
-        return
-
-    class Cut:
-        def __setitem__(self, where, value):
-            out_ref[0:rows, where[1]] = value[0:rows]
-
-    place(full(whole), Cut())
-
-
-def swap(value, kind, bit, size):
-    return lax.ppermute(value, kind, [(i, i ^ (1 << bit)) for i in range(size)])
+                if n < 8:
+                    left = jnp.concatenate([left] * (8 // n), axis=0)
+                    right = jnp.concatenate([right] * (8 // n), axis=0)
+                to = first_col + col
+                out_ref[r : r + n, to : to + LANES] = pick_lanes(left, right, back0)[0:n]
+                out_ref[r : r + n, to + LANES : to + pairs] = pick_lanes(left, right, back1)[0:n]
+
+    place(value, two_ref, 0)
+    rows = one_ref.shape[0]
+    for j in range(states):
+        place(one_rows[j * rows : (j + 1) * rows], one_ref, j * pairs)
+
+
+def swap(value, kind, flip, sizes):
+    return lax.ppermute(value, kind, [(i, i ^ flip) for i in range(sizes[kind])])
 
 
 def shards(sizes, ci_vectors, alpha_source, alpha_sign, beta_source, beta_sign):
@@ -279,8 +280,15 @@
     alpha_bits = sizes["alpha"].bit_length() - 1
     beta_bits = sizes["beta"].bit_length() - 1
 
-    alpha_whole = lax.all_gather(ci_vectors, "alpha", axis=1, tiled=True)
-    beta_whole = lax.all_gather(ci_vectors, "beta", axis=2, tiled=True)
+    beta_parts = [ci_vectors] + [None] * (sizes["beta"] - 1)
+    alpha_parts = [ci_vectors] + [None] * (sizes["alpha"] - 1)
+    beta_parts[1] = swap(ci_vectors, "beta", 1, sizes)
+    for j in range(2, sizes["beta"], 2):
+        beta_parts[j] = swap(ci_vectors, "beta", j, sizes)
+    for j in range(1, sizes["alpha"]):
+        alpha_parts[j] = swap(ci_vectors, "alpha", j, sizes)
+    for j in range(2, sizes["beta"], 2):
+        beta_parts[j + 1] = swap(beta_parts[j], "beta", 1, sizes)
     flat = jnp.transpose(ci_vectors, (0, 2, 1)).reshape(states, alpha_rows * beta_rows)
     place = jnp.stack([lax.axis_index("alpha"), lax.axis_index("beta")]).astype(jnp.int32)
 
@@ -288,24 +296,30 @@
     in_alpha = [("alpha", i) for i in range(alpha_bits)]
     orders = [
         in_beta + in_alpha,
-        in_beta[1:] + in_alpha + in_beta[:1],
+        in_beta[::-1] + in_alpha,
         in_alpha + in_beta,
     ]
     columns = [384, 384, 256]
     streams = len(orders)
+    extra = [0, 0, ONE_ROWS]
     half = total // 2
-    beta_count = beta_whole.shape[2]
+    beta_count = sizes["beta"] * beta_rows
     depth = alpha_rows * beta_rows
     vmem = pl.BlockSpec(memory_space=pltpu.VMEM)
     results = pl.pallas_call(
-        functools.partial(main_kernel, rows_each, orders, columns),
-        out_shape=[jax.ShapeDtypeStruct((half, c), F32) for c in columns] * 2
-        + [jax.ShapeDtypeStruct((states, total), F32)],
-        in_specs=[pl.BlockSpec(memory_space=pltpu.SMEM)] + [vmem] * 8,
-        out_specs=[vmem] * (2 * streams + 1),
+        functools.partial(
+            main_kernel, rows_each, orders, columns, (sizes["alpha"], sizes["beta"])
+        ),
+        out_shape=[
+            jax.ShapeDtypeStruct((half + extra[s], columns[s]), F32) for s in range(streams)
+        ]
+        * 2,
+        in_specs=[pl.BlockSpec(memory_space=pltpu.SMEM)]
+        + [vmem] * (5 + sizes["alpha"] + sizes["beta"]),
+        out_specs=[vmem] * (2 * streams),
         scratch_shapes=[
             pltpu.VMEM((2 * states * alpha_rows, beta_count), BF16),
-            pltpu.VMEM((states, beta_rows, alpha_whole.shape[1]), F32),
+            pltpu.VMEM((states, beta_rows, sizes["alpha"] * alpha_rows), F32),
             pltpu.VMEM((alpha_rows, LANES), jnp.int32),
             pltpu.VMEM((alpha_rows, LANES), F32),
             pltpu.VMEM((alpha_rows, LANES), F32),
@@ -323,41 +337,44 @@
     )(
         place,
         jnp.asarray(lane),
-        alpha_whole,
-        beta_whole,
         flat,
         alpha_source,
         alpha_sign,
         beta_source,
         beta_sign,
+        *alpha_parts,
+        *beta_parts[1:],
     )
-    send, keep, one = list(results[:streams]), list(results[streams:-1]), results[-1]
-    got = [swap(send[s], "beta", 0, sizes["beta"]) for s in range(streams)]
-    one = one + swap(one, "beta", 0, sizes["beta"])
-    steps = len(orders[0])
-    for t in range(steps):
-        for s in range(streams):
+    send, keep = list(results[:streams]), list(results[streams:])
+    got = [swap(send[s], "beta", 1, sizes) for s in range(streams)]
+    for t in range(len(orders[0])):
+        if t:
+            keep, got = lax.optimization_barrier((keep, got))
+        if len(keep) == 3 and orders[0][t:] == orders[1][t:]:
+            keep = [jnp.concatenate(keep[:2], axis=1), keep[2]]
+            got = [jnp.concatenate(got[:2], axis=1), got[2]]
+            orders = orders[1:]
+            extra = extra[1:]
+        out = [None] * len(keep)
+        for s in range(len(keep)):
+            n = (keep[s].shape[0] - extra[s]) // 2 + extra[s]
+            out[s] = keep[s][n:] + got[s][n:]
+            if extra[s]:
+                out[s] = jnp.concatenate([keep[s][: extra[s]] + got[s][: extra[s]], out[s]], axis=0)
+            keep[s] = keep[s][:n] + got[s][:n]
+        for s in range(len(keep)):
             kind, bit = orders[s][t]
-            n = keep[s].shape[0] // 2
-            out = keep[s][n:] + got[s][n:]
-            mine = keep[s][:n] + got[s][:n]
-            got[s] = swap(out, kind, bit, sizes[kind])
-            keep[s] = mine
-        kind, bit = orders[0][t]
-        if t < steps - 1:
-            one = one + swap(one, kind, bit, sizes[kind])
-        else:
-            other = swap(one, kind, bit, sizes[kind])
+            got[s] = swap(out[s], kind, 1 << bit, sizes)
     one_body, two_body = pl.pallas_call(
-        functools.partial(last_kernel, columns),
+        functools.partial(last_kernel, [k.shape[1] for k in keep]),
         out_shape=[
             jax.ShapeDtypeStruct((states, total), F32),
             jax.ShapeDtypeStruct((rows_each, total), F32),
         ],
-        in_specs=[vmem] * (3 + 2 * streams),
+        in_specs=[vmem] * (1 + 2 * len(keep)),
         out_specs=[vmem] * 2,
         name="finish",
-    )(jnp.asarray(inverse), one, other, *keep, *got)
+    )(jnp.asarray(inverse), *keep, *got)
     return (one_body, two_body)
 
 

time: 118 us -> 95.5 us (0.81)
  blocking collectives: 29.6 us -> 0 us
  waiting for transfers between devices: 21.8 us -> 30.7 us
  Pallas kernels: 36.9 us -> 34.4 us
  local copies, waits for them, and re-layouts: 1.54 us -> 3.79 us
  starting transfers between devices: 22.9 us -> 21.2 us
    all_gather x2 -> x0, blocking collectives: 29.6 us -> none  [the longest x1 17.6 us: shards(): alpha_whole = lax.all_gather(ci_vectors, 'alpha', axis=1, tiled=True)]
    ppermute x20 -> x23, waiting for transfers between devices: 21.8 us -> 30.7 us  [swap(): lax.ppermute(value, kind, [(i, i ^ flip) for i in range(sizes[kind])])]
    pallas_call x2, Pallas kernels: 36.9 us -> 34.4 us  [the longest x1 32.6 us: shards(): pl.pallas_call(functools.partial(main_kernel, rows_each, orders, columns,...]
    ppermute x20 -> x23, starting transfers between devices: 22.9 us -> 21.2 us  [swap(): lax.ppermute(value, kind, [(i, i ^ flip) for i in range(sizes[kind])])]
    unnamed x18 -> x34, local copies, waits for them, and re-layouts: 0.63 us -> 1.98 us
    add x16 -> x18, other arithmetic: 3.34 us -> 3.42 us  [the longest x10 1.97 us: shards(): out[s] = keep[s][n:] + got[s][n:]]
  transfers between devices with their start and end apart: 20 -> 23, of which waited for: 11 -> 12; matrix products, arithmetic and copies ran while one was open for 3% -> 6% of each run, Pallas kernels for 0% -> 0%
where the time goes in v1:
time: 95.5 us; the launch traced here: 95.1 us
  Pallas kernels  34.4 us (36%)
  waiting for transfers between devices  30.7 us (32%)
  starting transfers between devices  21.2 us (22%)
  other arithmetic  4.04 us (4%)
  local copies, waits for them, and re-layouts  3.79 us (4%)
    pallas_call x1, Pallas kernels, shards(): pl.pallas_call(functools.partial(main_kernel, rows_each, orders, columns,...  32.6 us
    ppermute x23, waiting for transfers between devices, swap(): lax.ppermute(value, kind, [(i, i ^ flip) for i in range(sizes[kind])])  30.7 us
    ppermute x23, starting transfers between devices, swap(): lax.ppermute(value, kind, [(i, i ^ flip) for i in range(sizes[kind])])  21.2 us
    unnamed x34, local copies, waits for them, and re-layouts  1.98 us
    add x10, other arithmetic, shards(): out[s] = keep[s][n:] + got[s][n:]  1.97 us
  transfers between devices with their start and end apart: 23, of which 12 were waited for; matrix products, arithmetic and copies ran while one was open for 6% of the time, Pallas kernels for 0%

profile of v1, /device:TPU:0, one launch (start us, length us, event | category | flops | bytes accessed | tf_op | source)
XLA Modules:
  0.0 95.1 jit_solution(3558868936933859440)
XLA Ops:
  0.6 3.0 %collective-permute-start.6 = (f32[4,32,128]{2,1,0:T(8,128)}, f32[4,32,128]{2,1,0:T(8,128)S(1)}, u32[]{:S(2)}, u32[]{:S(2)}) collective-permute-start(f32[4,32,128]{2,1,0:T(8,128)} %refs_0_.1), channel_id=1, source_target_pairs={{0,4},{1,5},{2,6},{3,7},{4,0},{5,1},{6,2},{7,3},{8,12},{9,13},{10,... | collective-permute-start | bytes 196616 | tf_op jit(solution)/shard_map/ppermute | solution.py:268
  3.7 1.5 %collective-permute-start.4 = (f32[4,32,128]{2,1,0:T(8,128)}, f32[4,32,128]{2,1,0:T(8,128)S(1)}, u32[]{:S(2)}, u32[]{:S(2)}) collective-permute-start(f32[4,32,128]{2,1,0:T(8,128)} %refs_0_.1), channel_id=1, source_target_pairs={{0,2},{1,3},{2,0},{3,1},{4,6},{5,7},{6,4},{7,5},{8,10},{9,11},{10,... | collective-permute-start | bytes 196616 | tf_op jit(solution)/shard_map/ppermute | solution.py:268
  5.2 0.0 collective-permute-start.3
  5.2 3.6 %collective-permute-start.2 = (f32[4,32,128]{2,1,0:T(8,128)}, f32[4,32,128]{2,1,0:T(8,128)S(1)}, u32[]{:S(2)}, u32[]{:S(2)}) collective-permute-start(f32[4,32,128]{2,1,0:T(8,128)} %refs_0_.1), channel_id=1, source_target_pairs={{0,24},{8,16},{16,8},{24,0},{1,25},{9,17},{17,9},{25,1},{2,26},{10... | collective-permute-start | bytes 196616 | tf_op jit(solution)/shard_map/ppermute | solution.py:268
  8.8 0.5 collective-permute-start.8
  9.2 1.0 %copy.10 = f32[4,128,32]{2,1,0:T(8,128)S(1)} copy(f32[4,128,32]{1,2,0:T(8,128)} %bitcast.3) | data formatting | bytes 131072 | tf_op jit(solution)/shard_map/transpose | solution.py:292
  10.2 0.0 copy-start.3
  10.3 0.8 reshape.7.flat_ref
  11.0 0.0 collective-permute-done.6.refs_7_
  11.0 0.0 copy-done.3
  11.1 0.0 collective-permute-start.1
  11.1 0.0 collective-permute-done.4.refs_5_
  11.1 0.5 collective-permute-start
  11.7 0.0 collective-permute-done.3.refs_4_
  11.7 0.0 collective-permute-start.7
  11.7 0.1 collective-permute-done.2.refs_3_
  11.8 0.4 collective-permute-start.5
  12.2 1.9 %collective-permute-done.8.refs_9_ = f32[4,32,128]{2,1,0:T(8,128)S(1)} collective-permute-done((f32[4,32,128]{2,1,0:T(8,128)}, f32[4,32,128]{2,1,0:T(8,128)S(1)}, u32[]{:S(2)}, u32[]{:S(2)}) %collective-permute-start.8) | collective-permute-done | bytes 65568 | tf_op jit(solution)/shard_map/ppermute | solution.py:268
  14.1 0.0 collective-permute-start.9
  14.1 0.6 pad_add_fusion.place_ref
  14.7 2.0 %collective-permute-done.1.refs_2_ = f32[4,32,128]{2,1,0:T(8,128)S(1)} collective-permute-done((f32[4,32,128]{2,1,0:T(8,128)S(1)}, f32[4,32,128]{2,1,0:T(8,128)S(1)}, u32[]{:S(2)}, u32[]{:S(2)}) %collective-permute-start.1) | collective-permute-done | bytes 65568 | tf_op jit(solution)/shard_map/ppermute | solution.py:268
  16.8 0.0 collective-permute-done.refs_1_
  16.8 0.0 collective-permute-done.7.refs_8_
  16.8 0.0 collective-permute-done.5.refs_6_
  16.8 0.0 collective-permute-done.9.refs_10_
  16.9 0.5 copy-done.10
  17.4 0.0 copy-done.11
  17.4 0.0 copy-done.12
  17.4 0.0 copy-done.13
  17.5 0.6 copy-done.14
  18.1 32.6 %excite.1 = (f32[512,384]{1,0:T(8,128)}, f32[512,384]{1,0:T(8,128)}, f32[528,256]{1,0:T(8,128)}, f32[512,384]{1,0:T(8,128)}, f32[512,384]{1,0:T(8,128)}, /*index=5*/f32[528,256]{1,0:T(8,128)}) custom-call(s32[2]{0:T(128)} %pad_add_fusion.place_ref, s32[1,256]{1,0:T(1,128)} %constant.12.clone.lane_ref, f32[4,4096]{1,0:T(4,128)} %reshape.7.flat_ref, ...), custom_call_target="tpu_custom_call" | custom-call | tf_op jit(solution)/shard_map/excite/pallas_call | solution.py:309
  50.7 0.1 collective-permute-start.12
  50.8 0.5 collective-permute-start.10
  51.3 0.1 collective-permute-start.11
  51.4 1.6 %collective-permute-done.12 = f32[528,256]{1,0:T(8,128)S(1)} collective-permute-done((f32[528,256]{1,0:T(8,128)}, f32[528,256]{1,0:T(8,128)S(1)}, u32[]{:S(2)}, u32[]{:S(2)}) %collective-permute-start.12) | collective-permute-done | bytes 540704 | tf_op jit(solution)/shard_map/ppermute | solution.py:268
  52.9 0.7 slice_add_fusion.20
  53.6 1.0 %slice_add_fusion.5 = f32[256,256]{1,0:T(8,128)S(1)} fusion(f32[528,256]{1,0:T(8,128)S(1)} %collective-permute-done.12, f32[528,256]{1,0:T(8,128)} %get-tuple-element.28), kind=kLoop, calls=%fused_computation.6 | loop fusion | flops 65536 | bytes 786432 | tf_op jit(solution)/shard_map/add | solution.py:361
  54.7 0.1 slice_add_fusion.1
  54.7 1.6 %collective-permute-start.13 = (f32[256,384]{1,0:T(8,128)S(1)}, f32[256,384]{1,0:T(8,128)S(1)}, u32[]{:S(2)}, u32[]{:S(2)}) collective-permute-start(f32[256,384]{1,0:T(8,128)S(1)} %get-tuple-element.48), channel_id=1, source_target_pairs={{0,2},{1,3},{2,0},{3,1},{4,6},{5,7},{6,4},{7,5},{8,10},{9,11},{10,... | collective-permute-start | bytes 1179656 | tf_op jit(solution)/shard_map/ppermute | solution.py:268
  56.3 0.1 slice_add_fusion
  56.4 1.6 %collective-permute-start.14 = (f32[256,384]{1,0:T(8,128)S(1)}, f32[256,384]{1,0:T(8,128)S(1)}, u32[]{:S(2)}, u32[]{:S(2)}) collective-permute-start(f32[256,384]{1,0:T(8,128)S(1)} %get-tuple-element.46), channel_id=1, source_target_pairs={{0,4},{1,5},{2,6},{3,7},{4,0},{5,1},{6,2},{7,3},{8,12},{9,13},{10,... | collective-permute-start | bytes 1179656 | tf_op jit(solution)/shard_map/ppermute | solution.py:268
  58.0 0.1 collective-permute-start.15
  58.1 8.1 %collective-permute-done.15 = f32[272,256]{1,0:T(8,128)S(1)} collective-permute-done((f32[272,256]{1,0:T(8,128)S(1)}, f32[272,256]{1,0:T(8,128)S(1)}, u32[]{:S(2)}, u32[]{:S(2)}) %collective-permute-start.15) | collective-permute-done | bytes 278560 | tf_op jit(solution)/shard_map/ppermute | solution.py:268
  66.2 0.0 collective-permute-done.13
  66.2 1.1 %collective-permute-done.14 = f32[256,384]{1,0:T(8,128)S(1)} collective-permute-done((f32[256,384]{1,0:T(8,128)S(1)}, f32[256,384]{1,0:T(8,128)S(1)}, u32[]{:S(2)}, u32[]{:S(2)}) %collective-permute-start.14) | collective-permute-done | bytes 393248 | tf_op jit(solution)/shard_map/ppermute | solution.py:268
  67.4 1.6 %collective-permute-start.18 = (f32[144,256]{1,0:T(8,128)S(1)}, f32[144,256]{1,0:T(8,128)S(1)}, u32[]{:S(2)}, u32[]{:S(2)}) collective-permute-start(f32[144,256]{1,0:T(8,128)S(1)} %pad_maximum_fusion.1), channel_id=1, source_target_pairs={{0,16},{8,24},{16,0},{24,8},{1,17},{9,25},{17,1},{25,9},{2,18},{10... | collective-permute-start | bytes 442376 | tf_op jit(solution)/shard_map/ppermute | solution.py:268
  69.0 1.6 %collective-permute-start.16 = (f32[128,384]{1,0:T(8,128)S(1)}, f32[128,384]{1,0:T(8,128)S(1)}, u32[]{:S(2)}, u32[]{:S(2)}) collective-permute-start(f32[128,384]{1,0:T(8,128)S(1)} %get-tuple-element.54), channel_id=1, source_target_pairs={{0,4},{1,5},{2,6},{3,7},{4,0},{5,1},{6,2},{7,3},{8,12},{9,13},{10,... | collective-permute-start | bytes 589832 | tf_op jit(solution)/shard_map/ppermute | solution.py:268
  70.6 0.1 slice_add_fusion.8
  70.7 1.3 %collective-permute-start.17 = (f32[128,384]{1,0:T(8,128)S(1)}, f32[128,384]{1,0:T(8,128)S(1)}, u32[]{:S(2)}, u32[]{:S(2)}) collective-permute-start(f32[128,384]{1,0:T(8,128)S(1)} %get-tuple-element.52), channel_id=1, source_target_pairs={{0,2},{1,3},{2,0},{3,1},{4,6},{5,7},{6,4},{7,5},{8,10},{9,11},{10,... | collective-permute-start | bytes 589832 | tf_op jit(solution)/shard_map/ppermute | solution.py:268
  72.0 3.7 %collective-permute-done.18 = f32[144,256]{1,0:T(8,128)S(1)} collective-permute-done((f32[144,256]{1,0:T(8,128)S(1)}, f32[144,256]{1,0:T(8,128)S(1)}, u32[]{:S(2)}, u32[]{:S(2)}) %collective-permute-start.18) | collective-permute-done | bytes 147488 | tf_op jit(solution)/shard_map/ppermute | solution.py:268
  75.6 0.0 collective-permute-done.16
  75.6 0.7 collective-permute-done.17
  76.4 1.3 %collective-permute-start.20 = (f32[80,256]{1,0:T(8,128)S(1)}, f32[80,256]{1,0:T(8,128)S(1)}, u32[]{:S(2)}, u32[]{:S(2)}) collective-permute-start(f32[80,256]{1,0:T(8,128)S(1)} %pad_maximum_fusion.2), channel_id=1, source_target_pairs={{0,2},{1,3},{2,0},{3,1},{4,6},{5,7},{6,4},{7,5},{8,10},{9,11},{10,... | collective-permute-start | bytes 245768 | tf_op jit(solution)/shard_map/ppermute | solution.py:268
  77.9 0.5 collective-permute-start.19
  78.3 2.6 %collective-permute-done.20 = f32[80,256]{1,0:T(8,128)S(1)} collective-permute-done((f32[80,256]{1,0:T(8,128)S(1)}, f32[80,256]{1,0:T(8,128)S(1)}, u32[]{:S(2)}, u32[]{:S(2)}) %collective-permute-start.20) | collective-permute-done | bytes 81952 | tf_op jit(solution)/shard_map/ppermute | solution.py:268
  80.9 3.1 %collective-permute-done.19 = f32[64,768]{1,0:T(8,128)S(1)} collective-permute-done((f32[64,768]{1,0:T(8,128)S(1)}, f32[64,768]{1,0:T(8,128)S(1)}, u32[]{:S(2)}, u32[]{:S(2)}) %collective-permute-start.19) | collective-permute-done | bytes 196640 | tf_op jit(solution)/shard_map/ppermute | solution.py:268
  84.1 1.6 %collective-permute-start.22 = (f32[48,256]{1,0:T(8,128)S(1)}, f32[48,256]{1,0:T(8,128)S(1)}, u32[]{:S(2)}, u32[]{:S(2)}) collective-permute-start(f32[48,256]{1,0:T(8,128)S(1)} %pad_maximum_fusion.3), channel_id=1, source_target_pairs={{0,4},{1,5},{2,6},{3,7},{4,0},{5,1},{6,2},{7,3},{8,12},{9,13},{10,... | collective-permute-start | bytes 147464 | tf_op jit(solution)/shard_map/ppermute | solution.py:268
  85.7 0.7 slice_add_fusion.14
  86.3 0.0 collective-permute-start.21
  86.3 0.6 slice_add_fusion.18.refs_1_
  87.0 1.3 %collective-permute-done.22.refs_3_ = f32[48,256]{1,0:T(8,128)S(1)} collective-permute-done((f32[48,256]{1,0:T(8,128)S(1)}, f32[48,256]{1,0:T(8,128)S(1)}, u32[]{:S(2)}, u32[]{:S(2)}) %collective-permute-start.22) | collective-permute-done | bytes 49184 | tf_op jit(solution)/shard_map/ppermute | solution.py:268
  88.2 4.4 %collective-permute-done.21.refs_2_ = f32[32,768]{1,0:T(8,128)S(1)} collective-permute-done((f32[32,768]{1,0:T(8,128)S(1)}, f32[32,768]{1,0:T(8,128)S(1)}, u32[]{:S(2)}, u32[]{:S(2)}) %collective-permute-start.21) | collective-permute-done | bytes 98336 | tf_op jit(solution)/shard_map/ppermute | solution.py:268
  92.6 0.6 copy-done.4
  93.3 1.8 %finish.1 = (f32[4,1024]{1,0:T(4,128)}, f32[32,1024]{1,0:T(8,128)}) custom-call(s32[1,256]{1,0:T(1,128)} %constant.13.clone.lane_ref, f32[32,768]{1,0:T(8,128)} %get-tuple-element.57.refs_0_, f32[48,256]{1,0:T(8,128)} %slice_add_fusion.18.refs_1_, f32[32,768]{1,0:T(8,128)} %copy-done.4, f32[48,256]{1,0:T(8,128)} %copy-done.15), custom_call_target="tpu_custom_call" | custom-call | tf_op jit(solution)/shard_map/finish/pallas_call | solution.py:368
  (44 shorter events, 0.4 us)
Async XLA Ops:
  0.6 10.4 %collective-permute-start.6 = (f32[4,32,128]{2,1,0:T(8,128)}, f32[4,32,128]{2,1,0:T(8,128)S(1)}, u32[]{:S(2)}, u32[]{:S(2)}) collective-permute-start(f32[4,32,128]{2,1,0:T(8,128)} %refs_0_.1), channel_id=1, source_target_pairs={{0,4},{1,5},{2,6},{3,7},{4,0},{5,1},{6,2},{7,3},{8,12},{9,13},{10,... | collective-permute-start | bytes 196616 | tf_op jit(solution)/shard_map/ppermute | solution.py:268
  3.7 7.5 %collective-permute-start.4 = (f32[4,32,128]{2,1,0:T(8,128)}, f32[4,32,128]{2,1,0:T(8,128)S(1)}, u32[]{:S(2)}, u32[]{:S(2)}) collective-permute-start(f32[4,32,128]{2,1,0:T(8,128)} %refs_0_.1), channel_id=1, source_target_pairs={{0,2},{1,3},{2,0},{3,1},{4,6},{5,7},{6,4},{7,5},{8,10},{9,11},{10,... | collective-permute-start | bytes 196616 | tf_op jit(solution)/shard_map/ppermute | solution.py:268
  5.2 6.5 %collective-permute-start.3 = (f32[4,32,128]{2,1,0:T(8,128)}, f32[4,32,128]{2,1,0:T(8,128)S(1)}, u32[]{:S(2)}, u32[]{:S(2)}) collective-permute-start(f32[4,32,128]{2,1,0:T(8,128)} %refs_0_.1), channel_id=1, source_target_pairs={{0,1},{1,0},{2,3},{3,2},{4,5},{5,4},{6,7},{7,6},{8,9},{9,8},{10,11... | collective-permute-start | bytes 196616 | tf_op jit(solution)/shard_map/ppermute | solution.py:268
  5.2 6.7 %collective-permute-start.2 = (f32[4,32,128]{2,1,0:T(8,128)}, f32[4,32,128]{2,1,0:T(8,128)S(1)}, u32[]{:S(2)}, u32[]{:S(2)}) collective-permute-start(f32[4,32,128]{2,1,0:T(8,128)} %refs_0_.1), channel_id=1, source_target_pairs={{0,24},{8,16},{16,8},{24,0},{1,25},{9,17},{17,9},{25,1},{2,26},{10... | collective-permute-start | bytes 196616 | tf_op jit(solution)/shard_map/ppermute | solution.py:268
  8.8 5.4 %collective-permute-start.8 = (f32[4,32,128]{2,1,0:T(8,128)}, f32[4,32,128]{2,1,0:T(8,128)S(1)}, u32[]{:S(2)}, u32[]{:S(2)}) collective-permute-start(f32[4,32,128]{2,1,0:T(8,128)} %refs_0_.1), channel_id=1, source_target_pairs={{0,6},{1,7},{2,4},{3,5},{4,2},{5,3},{6,0},{7,1},{8,14},{9,15},{10,... | collective-permute-start | bytes 196616 | tf_op jit(solution)/shard_map/ppermute | solution.py:268
  10.2 0.8 copy-start.3
  11.1 5.7 %copy-start.5 = (f32[4,32,128]{2,1,0:T(8,128)}, f32[4,32,128]{2,1,0:T(8,128)S(1)}, u32[]{:S(2)}) copy-start(f32[4,32,128]{2,1,0:T(8,128)S(1)} %collective-permute-done.6.refs_7_) | copy-start | bytes 196612
  11.1 5.7 %collective-permute-start.1 = (f32[4,32,128]{2,1,0:T(8,128)S(1)}, f32[4,32,128]{2,1,0:T(8,128)S(1)}, u32[]{:S(2)}, u32[]{:S(2)}) collective-permute-start(f32[4,32,128]{2,1,0:T(8,128)S(1)} %copy-done.3), channel_id=1, source_target_pairs={{0,16},{8,24},{16,0},{24,8},{1,17},{9,25},{17,1},{25,9},{2,18},{10... | collective-permute-start | bytes 196616 | tf_op jit(solution)/shard_map/ppermute | solution.py:268
  11.1 5.7 %copy-start.6 = (f32[4,32,128]{2,1,0:T(8,128)}, f32[4,32,128]{2,1,0:T(8,128)S(1)}, u32[]{:S(2)}) copy-start(f32[4,32,128]{2,1,0:T(8,128)S(1)} %collective-permute-done.4.refs_5_) | copy-start | bytes 196612
  11.1 5.6 %collective-permute-start = (f32[4,32,128]{2,1,0:T(8,128)S(1)}, f32[4,32,128]{2,1,0:T(8,128)S(1)}, u32[]{:S(2)}, u32[]{:S(2)}) collective-permute-start(f32[4,32,128]{2,1,0:T(8,128)S(1)} %copy-done.3), channel_id=1, source_target_pairs={{0,8},{8,0},{16,24},{24,16},{1,9},{9,1},{17,25},{25,17},{2,10},{10... | collective-permute-start | bytes 196616 | tf_op jit(solution)/shard_map/ppermute | solution.py:268
  11.7 5.2 %copy-start.7 = (f32[4,32,128]{2,1,0:T(8,128)}, f32[4,32,128]{2,1,0:T(8,128)S(1)}, u32[]{:S(2)}) copy-start(f32[4,32,128]{2,1,0:T(8,128)S(1)} %collective-permute-done.3.refs_4_) | copy-start | bytes 196612
  11.7 5.1 %collective-permute-start.7 = (f32[4,32,128]{2,1,0:T(8,128)S(1)}, f32[4,32,128]{2,1,0:T(8,128)S(1)}, u32[]{:S(2)}, u32[]{:S(2)}) collective-permute-start(f32[4,32,128]{2,1,0:T(8,128)S(1)} %collective-permute-done.6.refs_7_), channel_id=1, source_target_pairs={{0,1},{1,0},{2,3},{3,2},{4,5},{5,4},{6,7},{7,6},{8,9},{9,8},{10,11... | collective-permute-start | bytes 196616 | tf_op jit(solution)/shard_map/ppermute | solution.py:268
  11.8 5.0 %copy-start.8 = (f32[4,32,128]{2,1,0:T(8,128)}, f32[4,32,128]{2,1,0:T(8,128)S(1)}, u32[]{:S(2)}) copy-start(f32[4,32,128]{2,1,0:T(8,128)S(1)} %collective-permute-done.2.refs_3_) | copy-start | bytes 196612
  11.8 5.0 %collective-permute-start.5 = (f32[4,32,128]{2,1,0:T(8,128)S(1)}, f32[4,32,128]{2,1,0:T(8,128)S(1)}, u32[]{:S(2)}, u32[]{:S(2)}) collective-permute-start(f32[4,32,128]{2,1,0:T(8,128)S(1)} %collective-permute-done.4.refs_5_), channel_id=1, source_target_pairs={{0,1},{1,0},{2,3},{3,2},{4,5},{5,4},{6,7},{7,6},{8,9},{9,8},{10,11... | collective-permute-start | bytes 196616 | tf_op jit(solution)/shard_map/ppermute | solution.py:268
  14.1 2.7 %copy-start.9 = (f32[4,32,128]{2,1,0:T(8,128)}, f32[4,32,128]{2,1,0:T(8,128)S(1)}, u32[]{:S(2)}) copy-start(f32[4,32,128]{2,1,0:T(8,128)S(1)} %collective-permute-done.8.refs_9_) | copy-start | bytes 196612
  14.1 2.7 %collective-permute-start.9 = (f32[4,32,128]{2,1,0:T(8,128)S(1)}, f32[4,32,128]{2,1,0:T(8,128)S(1)}, u32[]{:S(2)}, u32[]{:S(2)}) collective-permute-start(f32[4,32,128]{2,1,0:T(8,128)S(1)} %collective-permute-done.8.refs_9_), channel_id=1, source_target_pairs={{0,1},{1,0},{2,3},{3,2},{4,5},{5,4},{6,7},{7,6},{8,9},{9,8},{10,11... | collective-permute-start | bytes 196616 | tf_op jit(solution)/shard_map/ppermute | solution.py:268
  16.8 0.6 copy-start.10
  16.8 0.7 copy-start.11
  16.8 0.7 copy-start.12
  16.8 0.7 copy-start.13
  17.5 0.6 copy-start.14
  50.7 3.9 %copy-start.1 = (f32[512,384]{1,0:T(8,128)S(1)}, f32[512,384]{1,0:T(8,128)}, u32[]{:S(2)}) copy-start(f32[512,384]{1,0:T(8,128)} %get-tuple-element.24) | copy-start | bytes 2359300
  50.7 2.2 %collective-permute-start.12 = (f32[528,256]{1,0:T(8,128)}, f32[528,256]{1,0:T(8,128)S(1)}, u32[]{:S(2)}, u32[]{:S(2)}) collective-permute-start(f32[528,256]{1,0:T(8,128)} %get-tuple-element.29), channel_id=1, source_target_pairs={{0,1},{1,0},{2,3},{3,2},{4,5},{5,4},{6,7},{7,6},{8,9},{9,8},{10,11... | collective-permute-start | bytes 1622024 | tf_op jit(solution)/shard_map/ppermute | solution.py:268
  50.8 3.8 %collective-permute-start.10 = (f32[512,384]{1,0:T(8,128)}, f32[512,384]{1,0:T(8,128)S(1)}, u32[]{:S(2)}, u32[]{:S(2)}) collective-permute-start(f32[512,384]{1,0:T(8,128)} %get-tuple-element.25), channel_id=1, source_target_pairs={{0,1},{1,0},{2,3},{3,2},{4,5},{5,4},{6,7},{7,6},{8,9},{9,8},{10,11... | collective-permute-start | bytes 2359304 | tf_op jit(solution)/shard_map/ppermute | solution.py:268
  51.3 5.0 %collective-permute-start.11 = (f32[512,384]{1,0:T(8,128)}, f32[512,384]{1,0:T(8,128)S(1)}, u32[]{:S(2)}, u32[]{:S(2)}) collective-permute-start(f32[512,384]{1,0:T(8,128)} %get-tuple-element.27), channel_id=1, source_target_pairs={{0,1},{1,0},{2,3},{3,2},{4,5},{5,4},{6,7},{7,6},{8,9},{9,8},{10,11... | collective-permute-start | bytes 2359304 | tf_op jit(solution)/shard_map/ppermute | solution.py:268
  54.6 1.7 %copy-start = (f32[512,384]{1,0:T(8,128)S(1)}, f32[512,384]{1,0:T(8,128)}, u32[]{:S(2)}) copy-start(f32[512,384]{1,0:T(8,128)} %get-tuple-element.26) | copy-start | bytes 2359300
  54.7 11.5 %collective-permute-start.13 = (f32[256,384]{1,0:T(8,128)S(1)}, f32[256,384]{1,0:T(8,128)S(1)}, u32[]{:S(2)}, u32[]{:S(2)}) collective-permute-start(f32[256,384]{1,0:T(8,128)S(1)} %get-tuple-element.48), channel_id=1, source_target_pairs={{0,2},{1,3},{2,0},{3,1},{4,6},{5,7},{6,4},{7,5},{8,10},{9,11},{10,... | collective-permute-start | bytes 1179656 | tf_op jit(solution)/shard_map/ppermute | solution.py:268
  56.4 1.7 %copy-start.2 = (f32[528,256]{1,0:T(8,128)S(1)}, f32[528,256]{1,0:T(8,128)}, u32[]{:S(2)}) copy-start(f32[528,256]{1,0:T(8,128)} %get-tuple-element.28) | copy-start | bytes 1622020
  56.4 10.9 %collective-permute-start.14 = (f32[256,384]{1,0:T(8,128)S(1)}, f32[256,384]{1,0:T(8,128)S(1)}, u32[]{:S(2)}, u32[]{:S(2)}) collective-permute-start(f32[256,384]{1,0:T(8,128)S(1)} %get-tuple-element.46), channel_id=1, source_target_pairs={{0,4},{1,5},{2,6},{3,7},{4,0},{5,1},{6,2},{7,3},{8,12},{9,13},{10,... | collective-permute-start | bytes 1179656 | tf_op jit(solution)/shard_map/ppermute | solution.py:268
  58.0 8.2 %collective-permute-start.15 = (f32[272,256]{1,0:T(8,128)S(1)}, f32[272,256]{1,0:T(8,128)S(1)}, u32[]{:S(2)}, u32[]{:S(2)}) collective-permute-start(f32[272,256]{1,0:T(8,128)S(1)} %pad_maximum_fusion), channel_id=1, source_target_pairs={{0,8},{8,0},{16,24},{24,16},{1,9},{9,1},{17,25},{25,17},{2,10},{10... | collective-permute-start | bytes 835592 | tf_op jit(solution)/shard_map/ppermute | solution.py:268
  67.4 8.2 %collective-permute-start.18 = (f32[144,256]{1,0:T(8,128)S(1)}, f32[144,256]{1,0:T(8,128)S(1)}, u32[]{:S(2)}, u32[]{:S(2)}) collective-permute-start(f32[144,256]{1,0:T(8,128)S(1)} %pad_maximum_fusion.1), channel_id=1, source_target_pairs={{0,16},{8,24},{16,0},{24,8},{1,17},{9,25},{17,1},{25,9},{2,18},{10... | collective-permute-start | bytes 442376 | tf_op jit(solution)/shard_map/ppermute | solution.py:268
  69.0 6.6 %collective-permute-start.16 = (f32[128,384]{1,0:T(8,128)S(1)}, f32[128,384]{1,0:T(8,128)S(1)}, u32[]{:S(2)}, u32[]{:S(2)}) collective-permute-start(f32[128,384]{1,0:T(8,128)S(1)} %get-tuple-element.54), channel_id=1, source_target_pairs={{0,4},{1,5},{2,6},{3,7},{4,0},{5,1},{6,2},{7,3},{8,12},{9,13},{10,... | collective-permute-start | bytes 589832 | tf_op jit(solution)/shard_map/ppermute | solution.py:268
  70.7 5.7 %collective-permute-start.17 = (f32[128,384]{1,0:T(8,128)S(1)}, f32[128,384]{1,0:T(8,128)S(1)}, u32[]{:S(2)}, u32[]{:S(2)}) collective-permute-start(f32[128,384]{1,0:T(8,128)S(1)} %get-tuple-element.52), channel_id=1, source_target_pairs={{0,2},{1,3},{2,0},{3,1},{4,6},{5,7},{6,4},{7,5},{8,10},{9,11},{10,... | collective-permute-start | bytes 589832 | tf_op jit(solution)/shard_map/ppermute | solution.py:268
  76.4 4.5 %collective-permute-start.20 = (f32[80,256]{1,0:T(8,128)S(1)}, f32[80,256]{1,0:T(8,128)S(1)}, u32[]{:S(2)}, u32[]{:S(2)}) collective-permute-start(f32[80,256]{1,0:T(8,128)S(1)} %pad_maximum_fusion.2), channel_id=1, source_target_pairs={{0,2},{1,3},{2,0},{3,1},{4,6},{5,7},{6,4},{7,5},{8,10},{9,11},{10,... | collective-permute-start | bytes 245768 | tf_op jit(solution)/shard_map/ppermute | solution.py:268
  77.9 6.2 %collective-permute-start.19 = (f32[64,768]{1,0:T(8,128)S(1)}, f32[64,768]{1,0:T(8,128)S(1)}, u32[]{:S(2)}, u32[]{:S(2)}) collective-permute-start(f32[64,768]{1,0:T(8,128)S(1)} %get-tuple-element.50), channel_id=1, source_target_pairs={{0,8},{8,0},{16,24},{24,16},{1,9},{9,1},{17,25},{25,17},{2,10},{10... | collective-permute-start | bytes 589832 | tf_op jit(solution)/shard_map/ppermute | solution.py:268
  84.1 4.2 %collective-permute-start.22 = (f32[48,256]{1,0:T(8,128)S(1)}, f32[48,256]{1,0:T(8,128)S(1)}, u32[]{:S(2)}, u32[]{:S(2)}) collective-permute-start(f32[48,256]{1,0:T(8,128)S(1)} %pad_maximum_fusion.3), channel_id=1, source_target_pairs={{0,4},{1,5},{2,6},{3,7},{4,0},{5,1},{6,2},{7,3},{8,12},{9,13},{10,... | collective-permute-start | bytes 147464 | tf_op jit(solution)/shard_map/ppermute | solution.py:268
  86.3 6.3 %collective-permute-start.21 = (f32[32,768]{1,0:T(8,128)S(1)}, f32[32,768]{1,0:T(8,128)S(1)}, u32[]{:S(2)}, u32[]{:S(2)}) collective-permute-start(f32[32,768]{1,0:T(8,128)S(1)} %get-tuple-element.56), channel_id=1, source_target_pairs={{0,16},{8,24},{16,0},{24,8},{1,17},{9,25},{17,1},{25,9},{2,18},{10... | collective-permute-start | bytes 294920 | tf_op jit(solution)/shard_map/ppermute | solution.py:268
  88.2 4.4 %copy-start.15 = (f32[48,256]{1,0:T(8,128)}, f32[48,256]{1,0:T(8,128)S(1)}, u32[]{:S(2)}) copy-start(f32[48,256]{1,0:T(8,128)S(1)} %collective-permute-done.22.refs_3_) | copy-start | bytes 147460
  92.6 0.6 copy-start.4

commit v2 on v1

--- a/solution.py
+++ b/solution.py
@@ -43,7 +43,6 @@
     orders,
     columns,
     parts,
-    place_ref,
     lane_ref,
     flat_ref,
     asrc_ref,
@@ -53,9 +52,14 @@
     *refs,
 ):
     alpha_parts, beta_parts = parts
-    alpha_refs = refs[:alpha_parts]
-    beta_refs = (refs[0],) + refs[alpha_parts : alpha_parts + beta_parts - 1]
-    refs = refs[alpha_parts + beta_parts - 1 :]
+    count = alpha_parts + beta_parts - 1
+    given, refs = refs[:count], refs[count:]
+    parts_ref, sems = refs[-2:]
+    copies = [
+        pltpu.make_async_copy(given[k], parts_ref.at[k], sems.at[k]) for k in range(count)
+    ]
+    for copy in copies:
+        copy.start()
     streams = len(columns)
     send_refs = refs[:streams]
     keep_refs = refs[streams : 2 * streams]
@@ -73,13 +77,13 @@
         left_ref,
         state_ref,
         perm_ref,
-    ) = refs[2 * streams :]
-    states, alpha_rows, beta_rows = alpha_refs[0].shape
+    ) = refs[2 * streams : -2]
+    states, alpha_rows, beta_rows = given[0].shape
     beta_count = beta_parts * beta_rows
     both = states * alpha_rows
     pairs = 2 * LANES
-    my_alpha = place_ref[0]
-    my_beta = place_ref[1]
+    my_alpha = lax.axis_index("alpha")
+    my_beta = lax.axis_index("beta")
     forward = lane_ref[0:1, 0:LANES]
     backward = lane_ref[0:1, LANES:pairs]
 
@@ -100,14 +104,6 @@
     tables(asrc_ref, asgn_ref, aidx_ref, asf_ref, asb_ref, alpha_rows, my_alpha * alpha_rows)
     tables(bsrc_ref, bsgn_ref, bidx_ref, bsf_ref, bsb_ref, beta_rows, my_beta * beta_rows)
 
-    for k in range(beta_parts):
-        high, mid = split_two(beta_refs[k][...].reshape(both, beta_rows))
-        table_ref[0:both, k * beta_rows : (k + 1) * beta_rows] = high
-        table_ref[both : 2 * both, k * beta_rows : (k + 1) * beta_rows] = mid
-    for j in range(states):
-        rows = jnp.concatenate([alpha_refs[k][j] for k in range(alpha_parts)], axis=0)
-        turned_ref[j] = rows.T
-
     flat = flat_ref[...]
     flat_high = flat.astype(BF16).astype(F32)
     flat_mid = flat - flat_high
@@ -119,6 +115,17 @@
     shift = rows_each.bit_length() - 1
     wanted = (((row >> shift) ^ my_beta) << shift) | (row & (rows_each - 1))
     perm_ref[...] = jnp.where(natural == wanted, 1.0, 0.0).astype(BF16)
+
+    for copy in copies:
+        copy.wait()
+    for k in range(beta_parts):
+        at = alpha_parts + k - 1 if k else 0
+        high, mid = split_two(parts_ref[at].reshape(both, beta_rows))
+        table_ref[0:both, k * beta_rows : (k + 1) * beta_rows] = high
+        table_ref[both : 2 * both, k * beta_rows : (k + 1) * beta_rows] = mid
+    for j in range(states):
+        rows = jnp.concatenate([parts_ref[k, j] for k in range(alpha_parts)], axis=0)
+        turned_ref[j] = rows.T
 
     chunk = min(1024, beta_count)
     chunks = beta_count // chunk
@@ -182,7 +189,7 @@
     lax.fori_loop(0, beta_rows // step, build, 0)
 
     depth = alpha_rows * beta_rows
-    piece = 512
+    piece = 1024
 
     def turn(k, carry):
         first = pl.multiple_of(k * piece, piece)
@@ -285,12 +292,14 @@
     beta_parts[1] = swap(ci_vectors, "beta", 1, sizes)
     for j in range(2, sizes["beta"], 2):
         beta_parts[j] = swap(ci_vectors, "beta", j, sizes)
-    for j in range(1, sizes["alpha"]):
+    for j in range(2, sizes["alpha"], 2):
         alpha_parts[j] = swap(ci_vectors, "alpha", j, sizes)
+    for j in range(0, sizes["alpha"], 2):
+        alpha_parts[j + 1] = swap(alpha_parts[j], "alpha", 1, sizes)
     for j in range(2, sizes["beta"], 2):
         beta_parts[j + 1] = swap(beta_parts[j], "beta", 1, sizes)
-    flat = jnp.transpose(ci_vectors, (0, 2, 1)).reshape(states, alpha_rows * beta_rows)
-    place = jnp.stack([lax.axis_index("alpha"), lax.axis_index("beta")]).astype(jnp.int32)
+    late, _ = lax.optimization_barrier((ci_vectors, (alpha_parts[2], beta_parts[-2])))
+    flat = jnp.transpose(late, (0, 2, 1)).reshape(states, alpha_rows * beta_rows)
 
     in_beta = [("beta", i) for i in range(1, beta_bits)]
     in_alpha = [("alpha", i) for i in range(alpha_bits)]
@@ -314,8 +323,8 @@
             jax.ShapeDtypeStruct((half + extra[s], columns[s]), F32) for s in range(streams)
         ]
         * 2,
-        in_specs=[pl.BlockSpec(memory_space=pltpu.SMEM)]
-        + [vmem] * (5 + sizes["alpha"] + sizes["beta"]),
+        in_specs=[vmem] * 6
+        + [pl.BlockSpec(memory_space=pltpu.HBM)] * (sizes["alpha"] + sizes["beta"] - 1),
         out_specs=[vmem] * (2 * streams),
         scratch_shapes=[
             pltpu.VMEM((2 * states * alpha_rows, beta_count), BF16),
@@ -331,11 +340,12 @@
             pltpu.VMEM((total, depth), BF16),
             pltpu.VMEM((16, depth), BF16),
             pltpu.VMEM((pairs, pairs), BF16),
+            pltpu.VMEM((sizes["alpha"] + sizes["beta"] - 1,) + ci_vectors.shape, F32),
+            pltpu.SemaphoreType.DMA((sizes["alpha"] + sizes["beta"] - 1,)),
         ],
         compiler_params=pltpu.CompilerParams(vmem_limit_bytes=58 << 20),
         name="excite",
     )(
-        place,
         jnp.asarray(lane),
         flat,
         alpha_source,
@@ -357,6 +367,10 @@
             extra = extra[1:]
         out = [None] * len(keep)
         for s in range(len(keep)):
+            if s:
+                out[s - 1], keep[s], got[s] = lax.optimization_barrier(
+                    (out[s - 1], keep[s], got[s])
+                )
             n = (keep[s].shape[0] - extra[s]) // 2 + extra[s]
             out[s] = keep[s][n:] + got[s][n:]
             if extra[s]:

time: 95.5 us -> 93.2 us (0.976)
  waiting for transfers between devices: 30.7 us -> 23.8 us
  starting transfers between devices: 21.2 us -> 26.5 us
  other arithmetic: 4.04 us -> 2.97 us
    ppermute x23, waiting for transfers between devices: 30.7 us -> 23.8 us  [swap(): lax.ppermute(value, kind, [(i, i ^ flip) for i in range(sizes[kind])])]
    ppermute x23, starting transfers between devices: 21.2 us -> 26.5 us  [swap(): lax.ppermute(value, kind, [(i, i ^ flip) for i in range(sizes[kind])])]
    unnamed x34 -> x30, local copies, waits for them, and re-layouts: 1.98 us -> 2.54 us
  transfers between devices with their start and end apart: 23 -> 23, of which waited for: 12 -> 12; matrix products, arithmetic and copies ran while one was open for 6% -> 4% of each run, Pallas kernels for 0% -> 0%
where the time goes in v2:
time: 93.2 us; the launch traced here: 92.8 us
  Pallas kernels  34.3 us (37%)
  starting transfers between devices  26.5 us (28%)
  waiting for transfers between devices  23.8 us (26%)
  local copies, waits for them, and re-layouts  4.35 us (5%)
  other arithmetic  2.97 us (3%)
    pallas_call x1, Pallas kernels, shards(): pl.pallas_call(functools.partial(main_kernel, rows_each, orders, columns,...  32.5 us
    ppermute x23, starting transfers between devices, swap(): lax.ppermute(value, kind, [(i, i ^ flip) for i in range(sizes[kind])])  26.5 us
    ppermute x23, waiting for transfers between devices, swap(): lax.ppermute(value, kind, [(i, i ^ flip) for i in range(sizes[kind])])  23.8 us
    unnamed x30, local copies, waits for them, and re-layouts  2.54 us
    add x10, other arithmetic, shards(): out[s] = keep[s][n:] + got[s][n:]  2.22 us
  transfers between devices with their start and end apart: 23, of which 12 were waited for; matrix products, arithmetic and copies ran while one was open for 4% of the time, Pallas kernels for 0%

profile of v2, /device:TPU:0, one launch (start us, length us, event | category | flops | bytes accessed | tf_op | source)
XLA Modules:
  0.0 92.8 jit_solution(3118020035484560570)
XLA Ops:
  0.6 3.0 %collective-permute-start.5 = (f32[4,32,128]{2,1,0:T(8,128)}, f32[4,32,128]{2,1,0:T(8,128)S(1)}, u32[]{:S(2)}, u32[]{:S(2)}) collective-permute-start(f32[4,32,128]{2,1,0:T(8,128)} %refs_0_.1), channel_id=1, source_target_pairs={{0,2},{1,3},{2,0},{3,1},{4,6},{5,7},{6,4},{7,5},{8,10},{9,11},{10,... | collective-permute-start | bytes 196616 | tf_op jit(solution)/shard_map/ppermute | solution.py:275
  3.6 0.0 collective-permute-start.4
  3.6 1.5 %collective-permute-start.1 = (f32[4,32,128]{2,1,0:T(8,128)}, f32[4,32,128]{2,1,0:T(8,128)S(1)}, u32[]{:S(2)}, u32[]{:S(2)}) collective-permute-start(f32[4,32,128]{2,1,0:T(8,128)} %refs_0_.1), channel_id=1, source_target_pairs={{0,6},{1,7},{2,4},{3,5},{4,2},{5,3},{6,0},{7,1},{8,14},{9,15},{10,... | collective-permute-start | bytes 196616 | tf_op jit(solution)/shard_map/ppermute | solution.py:275
  5.1 2.6 %collective-permute-start = (f32[4,32,128]{2,1,0:T(8,128)}, f32[4,32,128]{2,1,0:T(8,128)S(1)}, u32[]{:S(2)}, u32[]{:S(2)}) collective-permute-start(f32[4,32,128]{2,1,0:T(8,128)} %refs_0_.1), channel_id=1, source_target_pairs={{0,16},{8,24},{16,0},{24,8},{1,17},{9,25},{17,1},{25,9},{2,18},{10... | collective-permute-start | bytes 196616 | tf_op jit(solution)/shard_map/ppermute | solution.py:275
  7.7 0.5 collective-permute-start.7
  8.2 0.0 collective-permute-done.5.refs_5_
  8.2 1.6 %collective-permute-start.2 = (f32[4,32,128]{2,1,0:T(8,128)}, f32[4,32,128]{2,1,0:T(8,128)S(1)}, u32[]{:S(2)}, u32[]{:S(2)}) collective-permute-start(f32[4,32,128]{2,1,0:T(8,128)} %refs_0_.1), channel_id=1, source_target_pairs={{0,8},{8,0},{16,24},{24,16},{1,9},{9,1},{17,25},{25,17},{2,10},{10... | collective-permute-start | bytes 196616 | tf_op jit(solution)/shard_map/ppermute | solution.py:275
  9.8 0.0 collective-permute-done.4.refs_4_
  9.8 0.0 collective-permute-start.6
  9.8 0.0 collective-permute-done.1.refs_9_
  9.8 0.0 copy-start.5
  9.8 0.5 collective-permute-start.9
  10.3 1.3 %collective-permute-done.refs_2_ = f32[4,32,128]{2,1,0:T(8,128)S(1)} collective-permute-done((f32[4,32,128]{2,1,0:T(8,128)}, f32[4,32,128]{2,1,0:T(8,128)S(1)}, u32[]{:S(2)}, u32[]{:S(2)}) %collective-permute-start) | collective-permute-done | bytes 65568 | tf_op jit(solution)/shard_map/ppermute | solution.py:275
  11.6 1.1 %collective-permute-start.3 = (f32[4,32,128]{2,1,0:T(8,128)S(1)}, f32[4,32,128]{2,1,0:T(8,128)S(1)}, u32[]{:S(2)}, u32[]{:S(2)}) collective-permute-start(f32[4,32,128]{2,1,0:T(8,128)S(1)} %collective-permute-done.refs_2_), channel_id=1, source_target_pairs={{0,8},{8,0},{16,24},{24,16},{1,9},{9,1},{17,25},{25,17},{2,10},{10... | collective-permute-start | bytes 196616 | tf_op jit(solution)/shard_map/ppermute | solution.py:275
  12.7 0.0 collective-permute-done.7.refs_7_
  12.8 0.0 collective-permute-start.8
  12.8 1.0 %copy.10 = f32[4,128,32]{2,1,0:T(8,128)S(1)} copy(f32[4,128,32]{1,2,0:T(8,128)} %bitcast.1) | data formatting | bytes 131072 | tf_op jit(solution)/shard_map/transpose | solution.py:302
  13.8 0.8 reshape.7.flat_ref
  14.6 0.0 collective-permute-done.2.refs_1_
  14.6 0.0 collective-permute-done.6.refs_6_
  14.6 0.0 copy-start.9
  14.6 0.0 collective-permute-done.9.refs_10_
  14.6 1.3 %collective-permute-done.3.refs_3_ = f32[4,32,128]{2,1,0:T(8,128)S(1)} collective-permute-done((f32[4,32,128]{2,1,0:T(8,128)S(1)}, f32[4,32,128]{2,1,0:T(8,128)S(1)}, u32[]{:S(2)}, u32[]{:S(2)}) %collective-permute-start.3) | collective-permute-done | bytes 65568 | tf_op jit(solution)/shard_map/ppermute | solution.py:275
  15.9 0.0 collective-permute-done.8.refs_8_
  15.9 0.6 copy-done.11
  16.5 0.6 copy-done.12
  17.2 32.5 %excite.1 = (f32[512,384]{1,0:T(8,128)}, f32[512,384]{1,0:T(8,128)}, f32[528,256]{1,0:T(8,128)}, f32[512,384]{1,0:T(8,128)}, f32[512,384]{1,0:T(8,128)}, /*index=5*/f32[528,256]{1,0:T(8,128)}) custom-call(s32[1,256]{1,0:T(1,128)} %constant.4.clone.lane_ref, f32[4,4096]{1,0:T(4,128)} %reshape.7.flat_ref, s32[32,256]{1,0:T(8,128)} %asrc_ref.1, ...), custom_call_target="tpu_custom_call" | custom-call | tf_op jit(solution)/shard_map/excite/pallas_call | solution.py:318
  49.7 0.1 collective-permute-start.10
  49.8 0.5 collective-permute-start.11
  50.3 0.1 collective-permute-start.12
  50.3 1.9 %collective-permute-done.10 = f32[512,384]{1,0:T(8,128)S(1)} collective-permute-done((f32[512,384]{1,0:T(8,128)}, f32[512,384]{1,0:T(8,128)S(1)}, u32[]{:S(2)}, u32[]{:S(2)}) %collective-permute-start.10) | collective-permute-done | bytes 786464 | tf_op jit(solution)/shard_map/ppermute | solution.py:275
  52.2 1.3 %slice_add_fusion = (f32[256,384]{1,0:T(8,128)S(1)}, f32[256,384]{1,0:T(8,128)S(1)}) fusion(f32[512,384]{1,0:T(8,128)S(1)} %collective-permute-done.10, f32[512,384]{1,0:T(8,128)} %get-tuple-element.44), kind=kLoop, calls=%fused_computation | loop fusion | flops 196608 | bytes 2359296 | tf_op jit(solution)/shard_map/add | solution.py:375
  53.5 0.0 collective-permute-done.11
  53.5 0.1 copy-done
  53.6 0.1 slice_add_fusion.2
  53.7 0.4 collective-permute-done.12
  54.1 0.5 copy-done.1
  54.7 0.8 collective-permute-start.14
  55.5 1.6 %collective-permute-start.13 = (f32[256,384]{1,0:T(8,128)S(1)}, f32[256,384]{1,0:T(8,128)S(1)}, u32[]{:S(2)}, u32[]{:S(2)}) collective-permute-start(f32[256,384]{1,0:T(8,128)S(1)} %get-tuple-element.54), channel_id=1, source_target_pairs={{0,2},{1,3},{2,0},{3,1},{4,6},{5,7},{6,4},{7,5},{8,10},{9,11},{10,... | collective-permute-start | bytes 1179656 | tf_op jit(solution)/shard_map/ppermute | solution.py:275
  57.1 0.8 collective-permute-start.15
  57.9 7.4 %collective-permute-done.15 = f32[272,256]{1,0:T(8,128)S(1)} collective-permute-done((f32[272,256]{1,0:T(8,128)S(1)}, f32[272,256]{1,0:T(8,128)S(1)}, u32[]{:S(2)}, u32[]{:S(2)}) %collective-permute-start.15) | collective-permute-done | bytes 278560 | tf_op jit(solution)/shard_map/ppermute | solution.py:275
  65.3 0.6 collective-permute-done.14
  65.9 0.5 collective-permute-done.13
  66.4 0.1 slice_add_fusion.10
  66.4 0.1 slice_add_fusion.8
  66.5 2.2 %collective-permute-start.18 = (f32[144,256]{1,0:T(8,128)S(1)}, f32[144,256]{1,0:T(8,128)S(1)}, u32[]{:S(2)}, u32[]{:S(2)}) collective-permute-start(f32[144,256]{1,0:T(8,128)S(1)} %pad_maximum_fusion.1), channel_id=1, source_target_pairs={{0,16},{8,24},{16,0},{24,8},{1,17},{9,25},{17,1},{25,9},{2,18},{10... | collective-permute-start | bytes 442376 | tf_op jit(solution)/shard_map/ppermute | solution.py:275
  68.7 1.5 %collective-permute-start.17 = (f32[128,384]{1,0:T(8,128)S(1)}, f32[128,384]{1,0:T(8,128)S(1)}, u32[]{:S(2)}, u32[]{:S(2)}) collective-permute-start(f32[128,384]{1,0:T(8,128)S(1)} %get-tuple-element.67), channel_id=1, source_target_pairs={{0,2},{1,3},{2,0},{3,1},{4,6},{5,7},{6,4},{7,5},{8,10},{9,11},{10,... | collective-permute-start | bytes 589832 | tf_op jit(solution)/shard_map/ppermute | solution.py:275
  70.2 1.6 %collective-permute-start.16 = (f32[128,384]{1,0:T(8,128)S(1)}, f32[128,384]{1,0:T(8,128)S(1)}, u32[]{:S(2)}, u32[]{:S(2)}) collective-permute-start(f32[128,384]{1,0:T(8,128)S(1)} %get-tuple-element.66), channel_id=1, source_target_pairs={{0,4},{1,5},{2,6},{3,7},{4,0},{5,1},{6,2},{7,3},{8,12},{9,13},{10,... | collective-permute-start | bytes 589832 | tf_op jit(solution)/shard_map/ppermute | solution.py:275
  71.8 3.6 %collective-permute-done.18 = f32[144,256]{1,0:T(8,128)S(1)} collective-permute-done((f32[144,256]{1,0:T(8,128)S(1)}, f32[144,256]{1,0:T(8,128)S(1)}, u32[]{:S(2)}, u32[]{:S(2)}) %collective-permute-start.18) | collective-permute-done | bytes 147488 | tf_op jit(solution)/shard_map/ppermute | solution.py:275
  75.4 0.0 collective-permute-done.17
  75.4 0.4 collective-permute-done.16
  76.0 1.2 %collective-permute-start.20 = (f32[80,256]{1,0:T(8,128)S(1)}, f32[80,256]{1,0:T(8,128)S(1)}, u32[]{:S(2)}, u32[]{:S(2)}) collective-permute-start(f32[80,256]{1,0:T(8,128)S(1)} %pad_maximum_fusion.2), channel_id=1, source_target_pairs={{0,2},{1,3},{2,0},{3,1},{4,6},{5,7},{6,4},{7,5},{8,10},{9,11},{10,... | collective-permute-start | bytes 245768 | tf_op jit(solution)/shard_map/ppermute | solution.py:275
  77.2 1.4 %collective-permute-start.19 = (f32[64,768]{1,0:T(8,128)S(1)}, f32[64,768]{1,0:T(8,128)S(1)}, u32[]{:S(2)}, u32[]{:S(2)}) collective-permute-start(f32[64,768]{1,0:T(8,128)S(1)} %get-tuple-element.76), channel_id=1, source_target_pairs={{0,8},{8,0},{16,24},{24,16},{1,9},{9,1},{17,25},{25,17},{2,10},{10... | collective-permute-start | bytes 589832 | tf_op jit(solution)/shard_map/ppermute | solution.py:275
  78.6 1.9 %collective-permute-done.20 = f32[80,256]{1,0:T(8,128)S(1)} collective-permute-done((f32[80,256]{1,0:T(8,128)S(1)}, f32[80,256]{1,0:T(8,128)S(1)}, u32[]{:S(2)}, u32[]{:S(2)}) %collective-permute-start.20) | collective-permute-done | bytes 81952 | tf_op jit(solution)/shard_map/ppermute | solution.py:275
  80.5 2.4 %collective-permute-done.19 = f32[64,768]{1,0:T(8,128)S(1)} collective-permute-done((f32[64,768]{1,0:T(8,128)S(1)}, f32[64,768]{1,0:T(8,128)S(1)}, u32[]{:S(2)}, u32[]{:S(2)}) %collective-permute-start.19) | collective-permute-done | bytes 196640 | tf_op jit(solution)/shard_map/ppermute | solution.py:275
  82.9 0.6 slice_add_fusion.14
  83.6 1.3 %collective-permute-start.22 = (f32[48,256]{1,0:T(8,128)S(1)}, f32[48,256]{1,0:T(8,128)S(1)}, u32[]{:S(2)}, u32[]{:S(2)}) collective-permute-start(f32[48,256]{1,0:T(8,128)S(1)} %pad_maximum_fusion.3), channel_id=1, source_target_pairs={{0,4},{1,5},{2,6},{3,7},{4,0},{5,1},{6,2},{7,3},{8,12},{9,13},{10,... | collective-permute-start | bytes 147464 | tf_op jit(solution)/shard_map/ppermute | solution.py:275
  84.9 2.8 %collective-permute-start.21 = (f32[32,768]{1,0:T(8,128)S(1)}, f32[32,768]{1,0:T(8,128)S(1)}, u32[]{:S(2)}, u32[]{:S(2)}) collective-permute-start(f32[32,768]{1,0:T(8,128)S(1)} %get-tuple-element.83), channel_id=1, source_target_pairs={{0,16},{8,24},{16,0},{24,8},{1,17},{9,25},{17,1},{25,9},{2,18},{10... | collective-permute-start | bytes 294920 | tf_op jit(solution)/shard_map/ppermute | solution.py:275
  87.7 0.6 slice_add_fusion.18.refs_1_
  88.3 0.0 collective-permute-done.22.refs_3_
  88.3 2.1 %collective-permute-done.21.refs_2_ = f32[32,768]{1,0:T(8,128)S(1)} collective-permute-done((f32[32,768]{1,0:T(8,128)S(1)}, f32[32,768]{1,0:T(8,128)S(1)}, u32[]{:S(2)}, u32[]{:S(2)}) %collective-permute-start.21) | collective-permute-done | bytes 98336 | tf_op jit(solution)/shard_map/ppermute | solution.py:275
  90.4 0.0 copy-done.13
  90.4 0.6 copy-done.2
  91.0 1.8 %finish.1 = (f32[4,1024]{1,0:T(4,128)}, f32[32,1024]{1,0:T(8,128)}) custom-call(s32[1,256]{1,0:T(1,128)} %constant.5.clone.lane_ref, f32[32,768]{1,0:T(8,128)} %get-tuple-element.95.refs_0_, f32[48,256]{1,0:T(8,128)} %slice_add_fusion.18.refs_1_, f32[32,768]{1,0:T(8,128)} %copy-done.2, f32[48,256]{1,0:T(8,128)} %copy-done.13), custom_call_target="tpu_custom_call" | custom-call | tf_op jit(solution)/shard_map/finish/pallas_call | solution.py:382
  (39 shorter events, 0.3 us)
Async XLA Ops:
  0.6 7.6 %collective-permute-start.5 = (f32[4,32,128]{2,1,0:T(8,128)}, f32[4,32,128]{2,1,0:T(8,128)S(1)}, u32[]{:S(2)}, u32[]{:S(2)}) collective-permute-start(f32[4,32,128]{2,1,0:T(8,128)} %refs_0_.1), channel_id=1, source_target_pairs={{0,2},{1,3},{2,0},{3,1},{4,6},{5,7},{6,4},{7,5},{8,10},{9,11},{10,... | collective-permute-start | bytes 196616 | tf_op jit(solution)/shard_map/ppermute | solution.py:275
  3.6 6.2 %collective-permute-start.4 = (f32[4,32,128]{2,1,0:T(8,128)}, f32[4,32,128]{2,1,0:T(8,128)S(1)}, u32[]{:S(2)}, u32[]{:S(2)}) collective-permute-start(f32[4,32,128]{2,1,0:T(8,128)} %refs_0_.1), channel_id=1, source_target_pairs={{0,1},{1,0},{2,3},{3,2},{4,5},{5,4},{6,7},{7,6},{8,9},{9,8},{10,11... | collective-permute-start | bytes 196616 | tf_op jit(solution)/shard_map/ppermute | solution.py:275
  3.6 6.2 %collective-permute-start.1 = (f32[4,32,128]{2,1,0:T(8,128)}, f32[4,32,128]{2,1,0:T(8,128)S(1)}, u32[]{:S(2)}, u32[]{:S(2)}) collective-permute-start(f32[4,32,128]{2,1,0:T(8,128)} %refs_0_.1), channel_id=1, source_target_pairs={{0,6},{1,7},{2,4},{3,5},{4,2},{5,3},{6,0},{7,1},{8,14},{9,15},{10,... | collective-permute-start | bytes 196616 | tf_op jit(solution)/shard_map/ppermute | solution.py:275
  5.1 6.5 %collective-permute-start = (f32[4,32,128]{2,1,0:T(8,128)}, f32[4,32,128]{2,1,0:T(8,128)S(1)}, u32[]{:S(2)}, u32[]{:S(2)}) collective-permute-start(f32[4,32,128]{2,1,0:T(8,128)} %refs_0_.1), channel_id=1, source_target_pairs={{0,16},{8,24},{16,0},{24,8},{1,17},{9,25},{17,1},{25,9},{2,18},{10... | collective-permute-start | bytes 196616 | tf_op jit(solution)/shard_map/ppermute | solution.py:275
  7.7 5.0 %collective-permute-start.7 = (f32[4,32,128]{2,1,0:T(8,128)}, f32[4,32,128]{2,1,0:T(8,128)S(1)}, u32[]{:S(2)}, u32[]{:S(2)}) collective-permute-start(f32[4,32,128]{2,1,0:T(8,128)} %refs_0_.1), channel_id=1, source_target_pairs={{0,4},{1,5},{2,6},{3,7},{4,0},{5,1},{6,2},{7,3},{8,12},{9,13},{10,... | collective-permute-start | bytes 196616 | tf_op jit(solution)/shard_map/ppermute | solution.py:275
  8.2 5.5 %copy-start.3 = (f32[4,32,128]{2,1,0:T(8,128)}, f32[4,32,128]{2,1,0:T(8,128)S(1)}, u32[]{:S(2)}) copy-start(f32[4,32,128]{2,1,0:T(8,128)S(1)} %collective-permute-done.5.refs_5_) | copy-start | bytes 196612
  8.2 6.4 %collective-permute-start.2 = (f32[4,32,128]{2,1,0:T(8,128)}, f32[4,32,128]{2,1,0:T(8,128)S(1)}, u32[]{:S(2)}, u32[]{:S(2)}) collective-permute-start(f32[4,32,128]{2,1,0:T(8,128)} %refs_0_.1), channel_id=1, source_target_pairs={{0,8},{8,0},{16,24},{24,16},{1,9},{9,1},{17,25},{25,17},{2,10},{10... | collective-permute-start | bytes 196616 | tf_op jit(solution)/shard_map/ppermute | solution.py:275
  9.8 4.0 %copy-start.4 = (f32[4,32,128]{2,1,0:T(8,128)}, f32[4,32,128]{2,1,0:T(8,128)S(1)}, u32[]{:S(2)}) copy-start(f32[4,32,128]{2,1,0:T(8,128)S(1)} %collective-permute-done.4.refs_4_) | copy-start | bytes 196612
  9.8 4.8 %collective-permute-start.6 = (f32[4,32,128]{2,1,0:T(8,128)S(1)}, f32[4,32,128]{2,1,0:T(8,128)S(1)}, u32[]{:S(2)}, u32[]{:S(2)}) collective-permute-start(f32[4,32,128]{2,1,0:T(8,128)S(1)} %collective-permute-done.5.refs_5_), channel_id=1, source_target_pairs={{0,1},{1,0},{2,3},{3,2},{4,5},{5,4},{6,7},{7,6},{8,9},{9,8},{10,11... | collective-permute-start | bytes 196616 | tf_op jit(solution)/shard_map/ppermute | solution.py:275
  9.8 4.0 %copy-start.5 = (f32[4,32,128]{2,1,0:T(8,128)}, f32[4,32,128]{2,1,0:T(8,128)S(1)}, u32[]{:S(2)}) copy-start(f32[4,32,128]{2,1,0:T(8,128)S(1)} %collective-permute-done.1.refs_9_) | copy-start | bytes 196612
  9.8 4.8 %collective-permute-start.9 = (f32[4,32,128]{2,1,0:T(8,128)S(1)}, f32[4,32,128]{2,1,0:T(8,128)S(1)}, u32[]{:S(2)}, u32[]{:S(2)}) collective-permute-start(f32[4,32,128]{2,1,0:T(8,128)S(1)} %collective-permute-done.1.refs_9_), channel_id=1, source_target_pairs={{0,1},{1,0},{2,3},{3,2},{4,5},{5,4},{6,7},{7,6},{8,9},{9,8},{10,11... | collective-permute-start | bytes 196616 | tf_op jit(solution)/shard_map/ppermute | solution.py:275
  11.6 2.2 %copy-start.6 = (f32[4,32,128]{2,1,0:T(8,128)}, f32[4,32,128]{2,1,0:T(8,128)S(1)}, u32[]{:S(2)}) copy-start(f32[4,32,128]{2,1,0:T(8,128)S(1)} %collective-permute-done.refs_2_) | copy-start | bytes 196612
  11.6 4.3 %collective-permute-start.3 = (f32[4,32,128]{2,1,0:T(8,128)S(1)}, f32[4,32,128]{2,1,0:T(8,128)S(1)}, u32[]{:S(2)}, u32[]{:S(2)}) collective-permute-start(f32[4,32,128]{2,1,0:T(8,128)S(1)} %collective-permute-done.refs_2_), channel_id=1, source_target_pairs={{0,8},{8,0},{16,24},{24,16},{1,9},{9,1},{17,25},{25,17},{2,10},{10... | collective-permute-start | bytes 196616 | tf_op jit(solution)/shard_map/ppermute | solution.py:275
  12.7 1.1 %copy-start.7 = (f32[4,32,128]{2,1,0:T(8,128)}, f32[4,32,128]{2,1,0:T(8,128)S(1)}, u32[]{:S(2)}) copy-start(f32[4,32,128]{2,1,0:T(8,128)S(1)} %collective-permute-done.7.refs_7_) | copy-start | bytes 196612
  12.8 3.2 %collective-permute-start.8 = (f32[4,32,128]{2,1,0:T(8,128)S(1)}, f32[4,32,128]{2,1,0:T(8,128)S(1)}, u32[]{:S(2)}, u32[]{:S(2)}) collective-permute-start(f32[4,32,128]{2,1,0:T(8,128)S(1)} %collective-permute-done.7.refs_7_), channel_id=1, source_target_pairs={{0,1},{1,0},{2,3},{3,2},{4,5},{5,4},{6,7},{7,6},{8,9},{9,8},{10,11... | collective-permute-start | bytes 196616 | tf_op jit(solution)/shard_map/ppermute | solution.py:275
  14.6 1.3 %copy-start.8 = (f32[4,32,128]{2,1,0:T(8,128)}, f32[4,32,128]{2,1,0:T(8,128)S(1)}, u32[]{:S(2)}) copy-start(f32[4,32,128]{2,1,0:T(8,128)S(1)} %collective-permute-done.2.refs_1_) | copy-start | bytes 196612
  14.6 1.3 %copy-start.9 = (f32[4,32,128]{2,1,0:T(8,128)}, f32[4,32,128]{2,1,0:T(8,128)S(1)}, u32[]{:S(2)}) copy-start(f32[4,32,128]{2,1,0:T(8,128)S(1)} %collective-permute-done.6.refs_6_) | copy-start | bytes 196612
  14.6 1.3 %copy-start.10 = (f32[4,32,128]{2,1,0:T(8,128)}, f32[4,32,128]{2,1,0:T(8,128)S(1)}, u32[]{:S(2)}) copy-start(f32[4,32,128]{2,1,0:T(8,128)S(1)} %collective-permute-done.9.refs_10_) | copy-start | bytes 196612
  15.9 0.6 copy-start.11
  16.5 0.6 copy-start.12
  49.7 2.6 %collective-permute-start.10 = (f32[512,384]{1,0:T(8,128)}, f32[512,384]{1,0:T(8,128)S(1)}, u32[]{:S(2)}, u32[]{:S(2)}) collective-permute-start(f32[512,384]{1,0:T(8,128)} %get-tuple-element.45), channel_id=1, source_target_pairs={{0,1},{1,0},{2,3},{3,2},{4,5},{5,4},{6,7},{7,6},{8,9},{9,8},{10,11... | collective-permute-start | bytes 2359304 | tf_op jit(solution)/shard_map/ppermute | solution.py:275
  49.8 3.8 %collective-permute-start.11 = (f32[512,384]{1,0:T(8,128)}, f32[512,384]{1,0:T(8,128)S(1)}, u32[]{:S(2)}, u32[]{:S(2)}) collective-permute-start(f32[512,384]{1,0:T(8,128)} %get-tuple-element.47), channel_id=1, source_target_pairs={{0,1},{1,0},{2,3},{3,2},{4,5},{5,4},{6,7},{7,6},{8,9},{9,8},{10,11... | collective-permute-start | bytes 2359304 | tf_op jit(solution)/shard_map/ppermute | solution.py:275
  50.3 3.9 %collective-permute-start.12 = (f32[528,256]{1,0:T(8,128)}, f32[528,256]{1,0:T(8,128)S(1)}, u32[]{:S(2)}, u32[]{:S(2)}) collective-permute-start(f32[528,256]{1,0:T(8,128)} %get-tuple-element.51), channel_id=1, source_target_pairs={{0,1},{1,0},{2,3},{3,2},{4,5},{5,4},{6,7},{7,6},{8,9},{9,8},{10,11... | collective-permute-start | bytes 1622024 | tf_op jit(solution)/shard_map/ppermute | solution.py:275
  52.2 1.4 %copy-start = (f32[512,384]{1,0:T(8,128)S(1)}, f32[512,384]{1,0:T(8,128)}, u32[]{:S(2)}) copy-start(f32[512,384]{1,0:T(8,128)} %get-tuple-element.48) | copy-start | bytes 2359300
  53.6 1.0 %copy-start.1 = (f32[528,256]{1,0:T(8,128)S(1)}, f32[528,256]{1,0:T(8,128)}, u32[]{:S(2)}) copy-start(f32[528,256]{1,0:T(8,128)} %get-tuple-element.52) | copy-start | bytes 1622020
  54.7 11.2 %collective-permute-start.14 = (f32[256,384]{1,0:T(8,128)S(1)}, f32[256,384]{1,0:T(8,128)S(1)}, u32[]{:S(2)}, u32[]{:S(2)}) collective-permute-start(f32[256,384]{1,0:T(8,128)S(1)} %get-tuple-element.55), channel_id=1, source_target_pairs={{0,4},{1,5},{2,6},{3,7},{4,0},{5,1},{6,2},{7,3},{8,12},{9,13},{10,... | collective-permute-start | bytes 1179656 | tf_op jit(solution)/shard_map/ppermute | solution.py:275
  55.5 10.9 %collective-permute-start.13 = (f32[256,384]{1,0:T(8,128)S(1)}, f32[256,384]{1,0:T(8,128)S(1)}, u32[]{:S(2)}, u32[]{:S(2)}) collective-permute-start(f32[256,384]{1,0:T(8,128)S(1)} %get-tuple-element.54), channel_id=1, source_target_pairs={{0,2},{1,3},{2,0},{3,1},{4,6},{5,7},{6,4},{7,5},{8,10},{9,11},{10,... | collective-permute-start | bytes 1179656 | tf_op jit(solution)/shard_map/ppermute | solution.py:275
  57.1 8.2 %collective-permute-start.15 = (f32[272,256]{1,0:T(8,128)S(1)}, f32[272,256]{1,0:T(8,128)S(1)}, u32[]{:S(2)}, u32[]{:S(2)}) collective-permute-start(f32[272,256]{1,0:T(8,128)S(1)} %pad_maximum_fusion), channel_id=1, source_target_pairs={{0,8},{8,0},{16,24},{24,16},{1,9},{9,1},{17,25},{25,17},{2,10},{10... | collective-permute-start | bytes 835592 | tf_op jit(solution)/shard_map/ppermute | solution.py:275
  66.5 8.9 %collective-permute-start.18 = (f32[144,256]{1,0:T(8,128)S(1)}, f32[144,256]{1,0:T(8,128)S(1)}, u32[]{:S(2)}, u32[]{:S(2)}) collective-permute-start(f32[144,256]{1,0:T(8,128)S(1)} %pad_maximum_fusion.1), channel_id=1, source_target_pairs={{0,16},{8,24},{16,0},{24,8},{1,17},{9,25},{17,1},{25,9},{2,18},{10... | collective-permute-start | bytes 442376 | tf_op jit(solution)/shard_map/ppermute | solution.py:275
  68.7 6.7 %collective-permute-start.17 = (f32[128,384]{1,0:T(8,128)S(1)}, f32[128,384]{1,0:T(8,128)S(1)}, u32[]{:S(2)}, u32[]{:S(2)}) collective-permute-start(f32[128,384]{1,0:T(8,128)S(1)} %get-tuple-element.67), channel_id=1, source_target_pairs={{0,2},{1,3},{2,0},{3,1},{4,6},{5,7},{6,4},{7,5},{8,10},{9,11},{10,... | collective-permute-start | bytes 589832 | tf_op jit(solution)/shard_map/ppermute | solution.py:275
  70.2 5.7 %collective-permute-start.16 = (f32[128,384]{1,0:T(8,128)S(1)}, f32[128,384]{1,0:T(8,128)S(1)}, u32[]{:S(2)}, u32[]{:S(2)}) collective-permute-start(f32[128,384]{1,0:T(8,128)S(1)} %get-tuple-element.66), channel_id=1, source_target_pairs={{0,4},{1,5},{2,6},{3,7},{4,0},{5,1},{6,2},{7,3},{8,12},{9,13},{10,... | collective-permute-start | bytes 589832 | tf_op jit(solution)/shard_map/ppermute | solution.py:275
  76.0 4.5 %collective-permute-start.20 = (f32[80,256]{1,0:T(8,128)S(1)}, f32[80,256]{1,0:T(8,128)S(1)}, u32[]{:S(2)}, u32[]{:S(2)}) collective-permute-start(f32[80,256]{1,0:T(8,128)S(1)} %pad_maximum_fusion.2), channel_id=1, source_target_pairs={{0,2},{1,3},{2,0},{3,1},{4,6},{5,7},{6,4},{7,5},{8,10},{9,11},{10,... | collective-permute-start | bytes 245768 | tf_op jit(solution)/shard_map/ppermute | solution.py:275
  77.2 5.7 %collective-permute-start.19 = (f32[64,768]{1,0:T(8,128)S(1)}, f32[64,768]{1,0:T(8,128)S(1)}, u32[]{:S(2)}, u32[]{:S(2)}) collective-permute-start(f32[64,768]{1,0:T(8,128)S(1)} %get-tuple-element.76), channel_id=1, source_target_pairs={{0,8},{8,0},{16,24},{24,16},{1,9},{9,1},{17,25},{25,17},{2,10},{10... | collective-permute-start | bytes 589832 | tf_op jit(solution)/shard_map/ppermute | solution.py:275
  83.6 4.7 %collective-permute-start.22 = (f32[48,256]{1,0:T(8,128)S(1)}, f32[48,256]{1,0:T(8,128)S(1)}, u32[]{:S(2)}, u32[]{:S(2)}) collective-permute-start(f32[48,256]{1,0:T(8,128)S(1)} %pad_maximum_fusion.3), channel_id=1, source_target_pairs={{0,4},{1,5},{2,6},{3,7},{4,0},{5,1},{6,2},{7,3},{8,12},{9,13},{10,... | collective-permute-start | bytes 147464 | tf_op jit(solution)/shard_map/ppermute | solution.py:275
  84.9 5.5 %collective-permute-start.21 = (f32[32,768]{1,0:T(8,128)S(1)}, f32[32,768]{1,0:T(8,128)S(1)}, u32[]{:S(2)}, u32[]{:S(2)}) collective-permute-start(f32[32,768]{1,0:T(8,128)S(1)} %get-tuple-element.83), channel_id=1, source_target_pairs={{0,16},{8,24},{16,0},{24,8},{1,17},{9,25},{17,1},{25,9},{2,18},{10... | collective-permute-start | bytes 294920 | tf_op jit(solution)/shard_map/ppermute | solution.py:275
  88.3 2.1 %copy-start.13 = (f32[48,256]{1,0:T(8,128)}, f32[48,256]{1,0:T(8,128)S(1)}, u32[]{:S(2)}) copy-start(f32[48,256]{1,0:T(8,128)S(1)} %collective-permute-done.22.refs_3_) | copy-start | bytes 147460
  90.4 0.6 copy-start.2

commit v3 on v2

--- a/solution.py
+++ b/solution.py
@@ -44,7 +44,6 @@
     columns,
     parts,
     lane_ref,
-    flat_ref,
     asrc_ref,
     asgn_ref,
     bsrc_ref,
@@ -77,6 +76,7 @@
         left_ref,
         state_ref,
         perm_ref,
+        flat_ref,
     ) = refs[2 * streams : -2]
     states, alpha_rows, beta_rows = given[0].shape
     beta_count = beta_parts * beta_rows
@@ -104,12 +104,6 @@
     tables(asrc_ref, asgn_ref, aidx_ref, asf_ref, asb_ref, alpha_rows, my_alpha * alpha_rows)
     tables(bsrc_ref, bsgn_ref, bidx_ref, bsf_ref, bsb_ref, beta_rows, my_beta * beta_rows)
 
-    flat = flat_ref[...]
-    flat_high = flat.astype(BF16).astype(F32)
-    flat_mid = flat - flat_high
-    pad = jnp.zeros((16 - 2 * states, flat.shape[1]), F32)
-    state_ref[...] = jnp.concatenate([flat_high, flat_mid, pad], axis=0).astype(BF16)
-
     natural = lane_ref[0:1, :]
     row = lax.broadcasted_iota(jnp.int32, (pairs, pairs), 0)
     shift = rows_each.bit_length() - 1
@@ -126,6 +120,20 @@
     for j in range(states):
         rows = jnp.concatenate([parts_ref[k, j] for k in range(alpha_parts)], axis=0)
         turned_ref[j] = rows.T
+
+    per = LANES // alpha_rows
+    groups = beta_rows // per
+    for j in range(states):
+        lines = jnp.concatenate(
+            [turned_ref[j, pl.ds(q, groups, stride=per), 0:alpha_rows] for q in range(per)],
+            axis=1,
+        )
+        for g in range(groups):
+            flat_ref[j : j + 1, g * LANES : (g + 1) * LANES] = lines[g : g + 1, :]
+    flat = flat_ref[...]
+    flat_high = flat.astype(BF16).astype(F32)
+    pad = jnp.zeros((16 - 2 * states, flat.shape[1]), F32)
+    state_ref[...] = jnp.concatenate([flat_high, flat - flat_high, pad], axis=0).astype(BF16)
 
     chunk = min(1024, beta_count)
     chunks = beta_count // chunk
@@ -292,14 +300,10 @@
     beta_parts[1] = swap(ci_vectors, "beta", 1, sizes)
     for j in range(2, sizes["beta"], 2):
         beta_parts[j] = swap(ci_vectors, "beta", j, sizes)
-    for j in range(2, sizes["alpha"], 2):
+    for j in range(1, sizes["alpha"]):
         alpha_parts[j] = swap(ci_vectors, "alpha", j, sizes)
-    for j in range(0, sizes["alpha"], 2):
-        alpha_parts[j + 1] = swap(alpha_parts[j], "alpha", 1, sizes)
     for j in range(2, sizes["beta"], 2):
         beta_parts[j + 1] = swap(beta_parts[j], "beta", 1, sizes)
-    late, _ = lax.optimization_barrier((ci_vectors, (alpha_parts[2], beta_parts[-2])))
-    flat = jnp.transpose(late, (0, 2, 1)).reshape(states, alpha_rows * beta_rows)
 
     in_beta = [("beta", i) for i in range(1, beta_bits)]
     in_alpha = [("alpha", i) for i in range(alpha_bits)]
@@ -323,7 +327,7 @@
             jax.ShapeDtypeStruct((half + extra[s], columns[s]), F32) for s in range(streams)
         ]
         * 2,
-        in_specs=[vmem] * 6
+        in_specs=[vmem] * 5
         + [pl.BlockSpec(memory_space=pltpu.HBM)] * (sizes["alpha"] + sizes["beta"] - 1),
         out_specs=[vmem] * (2 * streams),
         scratch_shapes=[
@@ -340,6 +344,7 @@
             pltpu.VMEM((total, depth), BF16),
             pltpu.VMEM((16, depth), BF16),
             pltpu.VMEM((pairs, pairs), BF16),
+            pltpu.VMEM((states, depth), F32),
             pltpu.VMEM((sizes["alpha"] + sizes["beta"] - 1,) + ci_vectors.shape, F32),
             pltpu.SemaphoreType.DMA((sizes["alpha"] + sizes["beta"] - 1,)),
         ],
@@ -347,7 +352,6 @@
         name="excite",
     )(
         jnp.asarray(lane),
-        flat,
         alpha_source,
         alpha_sign,
         beta_source,
@@ -358,7 +362,7 @@
     send, keep = list(results[:streams]), list(results[streams:])
     got = [swap(send[s], "beta", 1, sizes) for s in range(streams)]
     for t in range(len(orders[0])):
-        if t:
+        if 0 < t < 3:
             keep, got = lax.optimization_barrier((keep, got))
         if len(keep) == 3 and orders[0][t:] == orders[1][t:]:
             keep = [jnp.concatenate(keep[:2], axis=1), keep[2]]
@@ -367,7 +371,7 @@
             extra = extra[1:]
         out = [None] * len(keep)
         for s in range(len(keep)):
-            if s:
+            if s and len(keep) == 3:
                 out[s - 1], keep[s], got[s] = lax.optimization_barrier(
                     (out[s - 1], keep[s], got[s])
                 )

time: 93.2 us -> 92.9 us (level)
  waiting for transfers between devices: 23.8 us -> 30.9 us
  starting transfers between devices: 26.5 us -> 20.9 us
  local copies, waits for them, and re-layouts: 4.35 us -> 2.42 us
    ppermute x23, waiting for transfers between devices: 23.8 us -> 30.9 us  [swap(): lax.ppermute(value, kind, [(i, i ^ flip) for i in range(sizes[kind])])]
    ppermute x23, starting transfers between devices: 26.5 us -> 20.9 us  [swap(): lax.ppermute(value, kind, [(i, i ^ flip) for i in range(sizes[kind])])]
    transpose x1 -> x0, local copies, waits for them, and re-layouts: 0.99 us -> none  [shards(): jnp.transpose(late, (0, 2, 1)).reshape(states, alpha_rows * beta_rows)]
    add x10 -> x9, other arithmetic: 2.22 us -> 2.17 us  [shards(): out[s] = keep[s][n:] + got[s][n:]]
  transfers between devices with their start and end apart: 23 -> 23, of which waited for: 12 -> 13; matrix products, arithmetic and copies ran while one was open for 4% -> 3% of each run, Pallas kernels for 0% -> 0%
where the time goes in v3:
time: 92.9 us; the launch traced here: 92.6 us
  Pallas kernels  34.5 us (37%)
  waiting for transfers between devices  30.9 us (33%)
  starting transfers between devices  20.9 us (22%)
  other arithmetic  2.97 us (3%)
  local copies, waits for them, and re-layouts  2.42 us (3%)
    pallas_call x1, Pallas kernels, shards(): pl.pallas_call(functools.partial(main_kernel, rows_each, orders, columns,...  32.7 us
    ppermute x23, waiting for transfers between devices, swap(): lax.ppermute(value, kind, [(i, i ^ flip) for i in range(sizes[kind])])  30.9 us
    ppermute x23, starting transfers between devices, swap(): lax.ppermute(value, kind, [(i, i ^ flip) for i in range(sizes[kind])])  20.9 us
    unnamed x30, local copies, waits for them, and re-layouts  2.39 us
    add x9, other arithmetic, shards(): out[s] = keep[s][n:] + got[s][n:]  2.17 us
  transfers between devices with their start and end apart: 23, of which 13 were waited for; matrix products, arithmetic and copies ran while one was open for 3% of the time, Pallas kernels for 0%

profile of v3, /device:TPU:0, one launch (start us, length us, event | category | flops | bytes accessed | tf_op | source)
XLA Modules:
  0.0 92.6 jit_solution(6038748569648277607)
XLA Ops:
  0.6 3.0 %collective-permute-start.6 = (f32[4,32,128]{2,1,0:T(8,128)}, f32[4,32,128]{2,1,0:T(8,128)S(1)}, u32[]{:S(2)}, u32[]{:S(2)}) collective-permute-start(f32[4,32,128]{2,1,0:T(8,128)} %refs_0_.1), channel_id=1, source_target_pairs={{0,4},{1,5},{2,6},{3,7},{4,0},{5,1},{6,2},{7,3},{8,12},{9,13},{10,... | collective-permute-start | bytes 196616 | tf_op jit(solution)/shard_map/ppermute | solution.py:283
  3.7 1.5 %collective-permute-start.4 = (f32[4,32,128]{2,1,0:T(8,128)}, f32[4,32,128]{2,1,0:T(8,128)S(1)}, u32[]{:S(2)}, u32[]{:S(2)}) collective-permute-start(f32[4,32,128]{2,1,0:T(8,128)} %refs_0_.1), channel_id=1, source_target_pairs={{0,2},{1,3},{2,0},{3,1},{4,6},{5,7},{6,4},{7,5},{8,10},{9,11},{10,... | collective-permute-start | bytes 196616 | tf_op jit(solution)/shard_map/ppermute | solution.py:283
  5.2 0.0 collective-permute-start.3
  5.2 3.6 %collective-permute-start.2 = (f32[4,32,128]{2,1,0:T(8,128)}, f32[4,32,128]{2,1,0:T(8,128)S(1)}, u32[]{:S(2)}, u32[]{:S(2)}) collective-permute-start(f32[4,32,128]{2,1,0:T(8,128)} %refs_0_.1), channel_id=1, source_target_pairs={{0,24},{8,16},{16,8},{24,0},{1,25},{9,17},{17,9},{25,1},{2,26},{10... | collective-permute-start | bytes 196616 | tf_op jit(solution)/shard_map/ppermute | solution.py:283
  8.8 0.5 collective-permute-start.8
  9.2 0.0 collective-permute-done.6.refs_7_
  9.2 0.0 collective-permute-start.1
  9.2 0.0 collective-permute-done.4.refs_5_
  9.3 0.0 copy-start.4
  9.3 1.5 %collective-permute-start = (f32[4,32,128]{2,1,0:T(8,128)}, f32[4,32,128]{2,1,0:T(8,128)S(1)}, u32[]{:S(2)}, u32[]{:S(2)}) collective-permute-start(f32[4,32,128]{2,1,0:T(8,128)} %refs_0_.1), channel_id=1, source_target_pairs={{0,8},{8,0},{16,24},{24,16},{1,9},{9,1},{17,25},{25,17},{2,10},{10... | collective-permute-start | bytes 196616 | tf_op jit(solution)/shard_map/ppermute | solution.py:283
  10.8 0.0 collective-permute-done.3.refs_4_
  10.8 0.0 collective-permute-start.7
  10.8 1.0 %collective-permute-done.2.refs_3_ = f32[4,32,128]{2,1,0:T(8,128)S(1)} collective-permute-done((f32[4,32,128]{2,1,0:T(8,128)}, f32[4,32,128]{2,1,0:T(8,128)S(1)}, u32[]{:S(2)}, u32[]{:S(2)}) %collective-permute-start.2) | collective-permute-done | bytes 65568 | tf_op jit(solution)/shard_map/ppermute | solution.py:283
  11.8 0.0 collective-permute-start.5
  11.8 2.3 %collective-permute-done.8.refs_9_ = f32[4,32,128]{2,1,0:T(8,128)S(1)} collective-permute-done((f32[4,32,128]{2,1,0:T(8,128)}, f32[4,32,128]{2,1,0:T(8,128)S(1)}, u32[]{:S(2)}, u32[]{:S(2)}) %collective-permute-start.8) | collective-permute-done | bytes 65568 | tf_op jit(solution)/shard_map/ppermute | solution.py:283
  14.1 0.0 collective-permute-start.9
  14.1 1.1 %collective-permute-done.1.refs_2_ = f32[4,32,128]{2,1,0:T(8,128)S(1)} collective-permute-done((f32[4,32,128]{2,1,0:T(8,128)}, f32[4,32,128]{2,1,0:T(8,128)S(1)}, u32[]{:S(2)}, u32[]{:S(2)}) %collective-permute-start.1) | collective-permute-done | bytes 65568 | tf_op jit(solution)/shard_map/ppermute | solution.py:283
  15.2 0.0 collective-permute-done.refs_1_
  15.2 0.0 collective-permute-done.7.refs_8_
  15.2 0.0 collective-permute-done.5.refs_6_
  15.2 0.1 collective-permute-done.9.refs_10_
  15.4 0.4 copy-done.8
  15.8 0.0 copy-done.9
  15.9 0.0 copy-done.10
  15.9 0.0 copy-done.11
  15.9 0.6 copy-done.12
  16.5 32.7 %excite.1 = (f32[512,384]{1,0:T(8,128)}, f32[512,384]{1,0:T(8,128)}, f32[528,256]{1,0:T(8,128)}, f32[512,384]{1,0:T(8,128)}, f32[512,384]{1,0:T(8,128)}, /*index=5*/f32[528,256]{1,0:T(8,128)}) custom-call(s32[1,256]{1,0:T(1,128)} %constant.4.clone.lane_ref, s32[32,256]{1,0:T(8,128)} %asrc_ref.1, s32[32,256]{1,0:T(8,128)} %asgn_ref.1, s32[128,256]{1,0:T(8,128)} %bsrc_ref.1, ...), custom_call_target="tpu_custom_call" | custom-call | tf_op jit(solution)/shard_map/excite/pallas_call | solution.py:322
  49.2 0.1 collective-permute-start.10
  49.3 0.5 collective-permute-start.11
  49.7 0.1 collective-permute-start.12
  49.8 1.9 %collective-permute-done.10 = f32[512,384]{1,0:T(8,128)S(1)} collective-permute-done((f32[512,384]{1,0:T(8,128)}, f32[512,384]{1,0:T(8,128)S(1)}, u32[]{:S(2)}, u32[]{:S(2)}) %collective-permute-start.10) | collective-permute-done | bytes 786464 | tf_op jit(solution)/shard_map/ppermute | solution.py:283
  51.7 1.3 %slice_add_fusion = (f32[256,384]{1,0:T(8,128)S(1)}, f32[256,384]{1,0:T(8,128)S(1)}) fusion(f32[512,384]{1,0:T(8,128)S(1)} %collective-permute-done.10, f32[512,384]{1,0:T(8,128)} %get-tuple-element.32), kind=kLoop, calls=%fused_computation | loop fusion | flops 196608 | bytes 2359296 | tf_op jit(solution)/shard_map/add | solution.py:379
  53.0 0.0 collective-permute-done.11
  53.0 0.1 copy-done
  53.1 0.1 slice_add_fusion.2
  53.2 0.4 collective-permute-done.12
  53.6 0.5 copy-done.1
  54.2 1.5 %collective-permute-start.14 = (f32[256,384]{1,0:T(8,128)S(1)}, f32[256,384]{1,0:T(8,128)S(1)}, u32[]{:S(2)}, u32[]{:S(2)}) collective-permute-start(f32[256,384]{1,0:T(8,128)S(1)} %get-tuple-element.43), channel_id=1, source_target_pairs={{0,4},{1,5},{2,6},{3,7},{4,0},{5,1},{6,2},{7,3},{8,12},{9,13},{10,... | collective-permute-start | bytes 1179656 | tf_op jit(solution)/shard_map/ppermute | solution.py:283
  55.7 1.5 %collective-permute-start.13 = (f32[256,384]{1,0:T(8,128)S(1)}, f32[256,384]{1,0:T(8,128)S(1)}, u32[]{:S(2)}, u32[]{:S(2)}) collective-permute-start(f32[256,384]{1,0:T(8,128)S(1)} %get-tuple-element.42), channel_id=1, source_target_pairs={{0,2},{1,3},{2,0},{3,1},{4,6},{5,7},{6,4},{7,5},{8,10},{9,11},{10,... | collective-permute-start | bytes 1179656 | tf_op jit(solution)/shard_map/ppermute | solution.py:283
  57.2 0.2 collective-permute-start.15
  57.4 8.0 %collective-permute-done.15 = f32[272,256]{1,0:T(8,128)S(1)} collective-permute-done((f32[272,256]{1,0:T(8,128)S(1)}, f32[272,256]{1,0:T(8,128)S(1)}, u32[]{:S(2)}, u32[]{:S(2)}) %collective-permute-start.15) | collective-permute-done | bytes 278560 | tf_op jit(solution)/shard_map/ppermute | solution.py:283
  65.4 0.0 collective-permute-done.14
  65.4 1.1 %collective-permute-done.13 = f32[256,384]{1,0:T(8,128)S(1)} collective-permute-done((f32[256,384]{1,0:T(8,128)S(1)}, f32[256,384]{1,0:T(8,128)S(1)}, u32[]{:S(2)}, u32[]{:S(2)}) %collective-permute-start.13) | collective-permute-done | bytes 393248 | tf_op jit(solution)/shard_map/ppermute | solution.py:283
  66.6 0.1 slice_add_fusion.10
  66.6 0.1 slice_add_fusion.8
  66.7 1.6 %collective-permute-start.18 = (f32[144,256]{1,0:T(8,128)S(1)}, f32[144,256]{1,0:T(8,128)S(1)}, u32[]{:S(2)}, u32[]{:S(2)}) collective-permute-start(f32[144,256]{1,0:T(8,128)S(1)} %pad_maximum_fusion.1), channel_id=1, source_target_pairs={{0,16},{8,24},{16,0},{24,8},{1,17},{9,25},{17,1},{25,9},{2,18},{10... | collective-permute-start | bytes 442376 | tf_op jit(solution)/shard_map/ppermute | solution.py:283
  68.3 1.5 %collective-permute-start.17 = (f32[128,384]{1,0:T(8,128)S(1)}, f32[128,384]{1,0:T(8,128)S(1)}, u32[]{:S(2)}, u32[]{:S(2)}) collective-permute-start(f32[128,384]{1,0:T(8,128)S(1)} %get-tuple-element.55), channel_id=1, source_target_pairs={{0,2},{1,3},{2,0},{3,1},{4,6},{5,7},{6,4},{7,5},{8,10},{9,11},{10,... | collective-permute-start | bytes 589832 | tf_op jit(solution)/shard_map/ppermute | solution.py:283
  69.8 0.5 collective-permute-start.16
  70.3 5.0 %collective-permute-done.18 = f32[144,256]{1,0:T(8,128)S(1)} collective-permute-done((f32[144,256]{1,0:T(8,128)S(1)}, f32[144,256]{1,0:T(8,128)S(1)}, u32[]{:S(2)}, u32[]{:S(2)}) %collective-permute-start.18) | collective-permute-done | bytes 147488 | tf_op jit(solution)/shard_map/ppermute | solution.py:283
  75.3 0.0 collective-permute-done.17
  75.3 0.1 collective-permute-done.16
  75.5 1.3 %collective-permute-start.20 = (f32[80,256]{1,0:T(8,128)S(1)}, f32[80,256]{1,0:T(8,128)S(1)}, u32[]{:S(2)}, u32[]{:S(2)}) collective-permute-start(f32[80,256]{1,0:T(8,128)S(1)} %pad_maximum_fusion.2), channel_id=1, source_target_pairs={{0,2},{1,3},{2,0},{3,1},{4,6},{5,7},{6,4},{7,5},{8,10},{9,11},{10,... | collective-permute-start | bytes 245768 | tf_op jit(solution)/shard_map/ppermute | solution.py:283
  76.9 0.7 collective-permute-start.19
  77.6 2.4 %collective-permute-done.20 = f32[80,256]{1,0:T(8,128)S(1)} collective-permute-done((f32[80,256]{1,0:T(8,128)S(1)}, f32[80,256]{1,0:T(8,128)S(1)}, u32[]{:S(2)}, u32[]{:S(2)}) %collective-permute-start.20) | collective-permute-done | bytes 81952 | tf_op jit(solution)/shard_map/ppermute | solution.py:283
  80.0 0.8 collective-permute-start.22
  80.9 2.3 %collective-permute-done.19 = f32[64,768]{1,0:T(8,128)S(1)} collective-permute-done((f32[64,768]{1,0:T(8,128)S(1)}, f32[64,768]{1,0:T(8,128)S(1)}, u32[]{:S(2)}, u32[]{:S(2)}) %collective-permute-start.19) | collective-permute-done | bytes 196640 | tf_op jit(solution)/shard_map/ppermute | solution.py:283
  83.2 0.6 slice_add_fusion.14
  83.8 0.6 collective-permute-start.21
  84.4 0.6 slice_add_fusion.18.refs_1_
  85.1 0.0 collective-permute-done.22.refs_3_
  85.1 5.0 %collective-permute-done.21.refs_2_ = f32[32,768]{1,0:T(8,128)S(1)} collective-permute-done((f32[32,768]{1,0:T(8,128)S(1)}, f32[32,768]{1,0:T(8,128)S(1)}, u32[]{:S(2)}, u32[]{:S(2)}) %collective-permute-start.21) | collective-permute-done | bytes 98336 | tf_op jit(solution)/shard_map/ppermute | solution.py:283
  90.1 0.0 copy-done.13
  90.1 0.6 copy-done.2
  90.7 1.8 %finish.1 = (f32[4,1024]{1,0:T(4,128)}, f32[32,1024]{1,0:T(8,128)}) custom-call(s32[1,256]{1,0:T(1,128)} %constant.5.clone.lane_ref, f32[32,768]{1,0:T(8,128)} %get-tuple-element.73.refs_0_, f32[48,256]{1,0:T(8,128)} %slice_add_fusion.18.refs_1_, f32[32,768]{1,0:T(8,128)} %copy-done.2, f32[48,256]{1,0:T(8,128)} %copy-done.13), custom_call_target="tpu_custom_call" | custom-call | tf_op jit(solution)/shard_map/finish/pallas_call | solution.py:386
  (37 shorter events, 0.3 us)
Async XLA Ops:
  0.6 8.6 %collective-permute-start.6 = (f32[4,32,128]{2,1,0:T(8,128)}, f32[4,32,128]{2,1,0:T(8,128)S(1)}, u32[]{:S(2)}, u32[]{:S(2)}) collective-permute-start(f32[4,32,128]{2,1,0:T(8,128)} %refs_0_.1), channel_id=1, source_target_pairs={{0,4},{1,5},{2,6},{3,7},{4,0},{5,1},{6,2},{7,3},{8,12},{9,13},{10,... | collective-permute-start | bytes 196616 | tf_op jit(solution)/shard_map/ppermute | solution.py:283
  3.7 5.6 %collective-permute-start.4 = (f32[4,32,128]{2,1,0:T(8,128)}, f32[4,32,128]{2,1,0:T(8,128)S(1)}, u32[]{:S(2)}, u32[]{:S(2)}) collective-permute-start(f32[4,32,128]{2,1,0:T(8,128)} %refs_0_.1), channel_id=1, source_target_pairs={{0,2},{1,3},{2,0},{3,1},{4,6},{5,7},{6,4},{7,5},{8,10},{9,11},{10,... | collective-permute-start | bytes 196616 | tf_op jit(solution)/shard_map/ppermute | solution.py:283
  5.2 5.6 %collective-permute-start.3 = (f32[4,32,128]{2,1,0:T(8,128)}, f32[4,32,128]{2,1,0:T(8,128)S(1)}, u32[]{:S(2)}, u32[]{:S(2)}) collective-permute-start(f32[4,32,128]{2,1,0:T(8,128)} %refs_0_.1), channel_id=1, source_target_pairs={{0,1},{1,0},{2,3},{3,2},{4,5},{5,4},{6,7},{7,6},{8,9},{9,8},{10,11... | collective-permute-start | bytes 196616 | tf_op jit(solution)/shard_map/ppermute | solution.py:283
  5.2 6.7 %collective-permute-start.2 = (f32[4,32,128]{2,1,0:T(8,128)}, f32[4,32,128]{2,1,0:T(8,128)S(1)}, u32[]{:S(2)}, u32[]{:S(2)}) collective-permute-start(f32[4,32,128]{2,1,0:T(8,128)} %refs_0_.1), channel_id=1, source_target_pairs={{0,24},{8,16},{16,8},{24,0},{1,25},{9,17},{17,9},{25,1},{2,26},{10... | collective-permute-start | bytes 196616 | tf_op jit(solution)/shard_map/ppermute | solution.py:283
  8.8 5.4 %collective-permute-start.8 = (f32[4,32,128]{2,1,0:T(8,128)}, f32[4,32,128]{2,1,0:T(8,128)S(1)}, u32[]{:S(2)}, u32[]{:S(2)}) collective-permute-start(f32[4,32,128]{2,1,0:T(8,128)} %refs_0_.1), channel_id=1, source_target_pairs={{0,6},{1,7},{2,4},{3,5},{4,2},{5,3},{6,0},{7,1},{8,14},{9,15},{10,... | collective-permute-start | bytes 196616 | tf_op jit(solution)/shard_map/ppermute | solution.py:283
  9.2 6.2 %copy-start.3 = (f32[4,32,128]{2,1,0:T(8,128)}, f32[4,32,128]{2,1,0:T(8,128)S(1)}, u32[]{:S(2)}) copy-start(f32[4,32,128]{2,1,0:T(8,128)S(1)} %collective-permute-done.6.refs_7_) | copy-start | bytes 196612
  9.2 6.0 %collective-permute-start.1 = (f32[4,32,128]{2,1,0:T(8,128)}, f32[4,32,128]{2,1,0:T(8,128)S(1)}, u32[]{:S(2)}, u32[]{:S(2)}) collective-permute-start(f32[4,32,128]{2,1,0:T(8,128)} %refs_0_.1), channel_id=1, source_target_pairs={{0,16},{8,24},{16,0},{24,8},{1,17},{9,25},{17,1},{25,9},{2,18},{10... | collective-permute-start | bytes 196616 | tf_op jit(solution)/shard_map/ppermute | solution.py:283
  9.3 6.1 %copy-start.4 = (f32[4,32,128]{2,1,0:T(8,128)}, f32[4,32,128]{2,1,0:T(8,128)S(1)}, u32[]{:S(2)}) copy-start(f32[4,32,128]{2,1,0:T(8,128)S(1)} %collective-permute-done.4.refs_5_) | copy-start | bytes 196612
  9.3 5.9 %collective-permute-start = (f32[4,32,128]{2,1,0:T(8,128)}, f32[4,32,128]{2,1,0:T(8,128)S(1)}, u32[]{:S(2)}, u32[]{:S(2)}) collective-permute-start(f32[4,32,128]{2,1,0:T(8,128)} %refs_0_.1), channel_id=1, source_target_pairs={{0,8},{8,0},{16,24},{24,16},{1,9},{9,1},{17,25},{25,17},{2,10},{10... | collective-permute-start | bytes 196616 | tf_op jit(solution)/shard_map/ppermute | solution.py:283
  10.8 4.6 %copy-start.5 = (f32[4,32,128]{2,1,0:T(8,128)}, f32[4,32,128]{2,1,0:T(8,128)S(1)}, u32[]{:S(2)}) copy-start(f32[4,32,128]{2,1,0:T(8,128)S(1)} %collective-permute-done.3.refs_4_) | copy-start | bytes 196612
  10.8 4.4 %collective-permute-start.7 = (f32[4,32,128]{2,1,0:T(8,128)S(1)}, f32[4,32,128]{2,1,0:T(8,128)S(1)}, u32[]{:S(2)}, u32[]{:S(2)}) collective-permute-start(f32[4,32,128]{2,1,0:T(8,128)S(1)} %collective-permute-done.6.refs_7_), channel_id=1, source_target_pairs={{0,1},{1,0},{2,3},{3,2},{4,5},{5,4},{6,7},{7,6},{8,9},{9,8},{10,11... | collective-permute-start | bytes 196616 | tf_op jit(solution)/shard_map/ppermute | solution.py:283
  11.8 3.6 %copy-start.6 = (f32[4,32,128]{2,1,0:T(8,128)}, f32[4,32,128]{2,1,0:T(8,128)S(1)}, u32[]{:S(2)}) copy-start(f32[4,32,128]{2,1,0:T(8,128)S(1)} %collective-permute-done.2.refs_3_) | copy-start | bytes 196612
  11.8 3.4 %collective-permute-start.5 = (f32[4,32,128]{2,1,0:T(8,128)S(1)}, f32[4,32,128]{2,1,0:T(8,128)S(1)}, u32[]{:S(2)}, u32[]{:S(2)}) collective-permute-start(f32[4,32,128]{2,1,0:T(8,128)S(1)} %collective-permute-done.4.refs_5_), channel_id=1, source_target_pairs={{0,1},{1,0},{2,3},{3,2},{4,5},{5,4},{6,7},{7,6},{8,9},{9,8},{10,11... | collective-permute-start | bytes 196616 | tf_op jit(solution)/shard_map/ppermute | solution.py:283
  14.1 1.3 %copy-start.7 = (f32[4,32,128]{2,1,0:T(8,128)}, f32[4,32,128]{2,1,0:T(8,128)S(1)}, u32[]{:S(2)}) copy-start(f32[4,32,128]{2,1,0:T(8,128)S(1)} %collective-permute-done.8.refs_9_) | copy-start | bytes 196612
  14.1 1.3 %collective-permute-start.9 = (f32[4,32,128]{2,1,0:T(8,128)S(1)}, f32[4,32,128]{2,1,0:T(8,128)S(1)}, u32[]{:S(2)}, u32[]{:S(2)}) collective-permute-start(f32[4,32,128]{2,1,0:T(8,128)S(1)} %collective-permute-done.8.refs_9_), channel_id=1, source_target_pairs={{0,1},{1,0},{2,3},{3,2},{4,5},{5,4},{6,7},{7,6},{8,9},{9,8},{10,11... | collective-permute-start | bytes 196616 | tf_op jit(solution)/shard_map/ppermute | solution.py:283
  15.2 0.6 copy-start.8
  15.2 0.6 copy-start.9
  15.2 0.7 copy-start.10
  15.2 0.6 copy-start.11
  15.9 0.6 copy-start.12
  49.2 2.6 %collective-permute-start.10 = (f32[512,384]{1,0:T(8,128)}, f32[512,384]{1,0:T(8,128)S(1)}, u32[]{:S(2)}, u32[]{:S(2)}) collective-permute-start(f32[512,384]{1,0:T(8,128)} %get-tuple-element.33), channel_id=1, source_target_pairs={{0,1},{1,0},{2,3},{3,2},{4,5},{5,4},{6,7},{7,6},{8,9},{9,8},{10,11... | collective-permute-start | bytes 2359304 | tf_op jit(solution)/shard_map/ppermute | solution.py:283
  49.3 3.8 %collective-permute-start.11 = (f32[512,384]{1,0:T(8,128)}, f32[512,384]{1,0:T(8,128)S(1)}, u32[]{:S(2)}, u32[]{:S(2)}) collective-permute-start(f32[512,384]{1,0:T(8,128)} %get-tuple-element.35), channel_id=1, source_target_pairs={{0,1},{1,0},{2,3},{3,2},{4,5},{5,4},{6,7},{7,6},{8,9},{9,8},{10,11... | collective-permute-start | bytes 2359304 | tf_op jit(solution)/shard_map/ppermute | solution.py:283
  49.7 3.9 %collective-permute-start.12 = (f32[528,256]{1,0:T(8,128)}, f32[528,256]{1,0:T(8,128)S(1)}, u32[]{:S(2)}, u32[]{:S(2)}) collective-permute-start(f32[528,256]{1,0:T(8,128)} %get-tuple-element.39), channel_id=1, source_target_pairs={{0,1},{1,0},{2,3},{3,2},{4,5},{5,4},{6,7},{7,6},{8,9},{9,8},{10,11... | collective-permute-start | bytes 1622024 | tf_op jit(solution)/shard_map/ppermute | solution.py:283
  51.7 1.4 %copy-start = (f32[512,384]{1,0:T(8,128)S(1)}, f32[512,384]{1,0:T(8,128)}, u32[]{:S(2)}) copy-start(f32[512,384]{1,0:T(8,128)} %get-tuple-element.36) | copy-start | bytes 2359300
  53.1 1.0 %copy-start.1 = (f32[528,256]{1,0:T(8,128)S(1)}, f32[528,256]{1,0:T(8,128)}, u32[]{:S(2)}) copy-start(f32[528,256]{1,0:T(8,128)} %get-tuple-element.40) | copy-start | bytes 1622020
  54.2 11.2 %collective-permute-start.14 = (f32[256,384]{1,0:T(8,128)S(1)}, f32[256,384]{1,0:T(8,128)S(1)}, u32[]{:S(2)}, u32[]{:S(2)}) collective-permute-start(f32[256,384]{1,0:T(8,128)S(1)} %get-tuple-element.43), channel_id=1, source_target_pairs={{0,4},{1,5},{2,6},{3,7},{4,0},{5,1},{6,2},{7,3},{8,12},{9,13},{10,... | collective-permute-start | bytes 1179656 | tf_op jit(solution)/shard_map/ppermute | solution.py:283
  55.7 10.9 %collective-permute-start.13 = (f32[256,384]{1,0:T(8,128)S(1)}, f32[256,384]{1,0:T(8,128)S(1)}, u32[]{:S(2)}, u32[]{:S(2)}) collective-permute-start(f32[256,384]{1,0:T(8,128)S(1)} %get-tuple-element.42), channel_id=1, source_target_pairs={{0,2},{1,3},{2,0},{3,1},{4,6},{5,7},{6,4},{7,5},{8,10},{9,11},{10,... | collective-permute-start | bytes 1179656 | tf_op jit(solution)/shard_map/ppermute | solution.py:283
  57.2 8.2 %collective-permute-start.15 = (f32[272,256]{1,0:T(8,128)S(1)}, f32[272,256]{1,0:T(8,128)S(1)}, u32[]{:S(2)}, u32[]{:S(2)}) collective-permute-start(f32[272,256]{1,0:T(8,128)S(1)} %pad_maximum_fusion), channel_id=1, source_target_pairs={{0,8},{8,0},{16,24},{24,16},{1,9},{9,1},{17,25},{25,17},{2,10},{10... | collective-permute-start | bytes 835592 | tf_op jit(solution)/shard_map/ppermute | solution.py:283
  66.7 8.6 %collective-permute-start.18 = (f32[144,256]{1,0:T(8,128)S(1)}, f32[144,256]{1,0:T(8,128)S(1)}, u32[]{:S(2)}, u32[]{:S(2)}) collective-permute-start(f32[144,256]{1,0:T(8,128)S(1)} %pad_maximum_fusion.1), channel_id=1, source_target_pairs={{0,16},{8,24},{16,0},{24,8},{1,17},{9,25},{17,1},{25,9},{2,18},{10... | collective-permute-start | bytes 442376 | tf_op jit(solution)/shard_map/ppermute | solution.py:283
  68.3 7.0 %collective-permute-start.17 = (f32[128,384]{1,0:T(8,128)S(1)}, f32[128,384]{1,0:T(8,128)S(1)}, u32[]{:S(2)}, u32[]{:S(2)}) collective-permute-start(f32[128,384]{1,0:T(8,128)S(1)} %get-tuple-element.55), channel_id=1, source_target_pairs={{0,2},{1,3},{2,0},{3,1},{4,6},{5,7},{6,4},{7,5},{8,10},{9,11},{10,... | collective-permute-start | bytes 589832 | tf_op jit(solution)/shard_map/ppermute | solution.py:283
  69.8 5.7 %collective-permute-start.16 = (f32[128,384]{1,0:T(8,128)S(1)}, f32[128,384]{1,0:T(8,128)S(1)}, u32[]{:S(2)}, u32[]{:S(2)}) collective-permute-start(f32[128,384]{1,0:T(8,128)S(1)} %get-tuple-element.54), channel_id=1, source_target_pairs={{0,4},{1,5},{2,6},{3,7},{4,0},{5,1},{6,2},{7,3},{8,12},{9,13},{10,... | collective-permute-start | bytes 589832 | tf_op jit(solution)/shard_map/ppermute | solution.py:283
  75.5 4.5 %collective-permute-start.20 = (f32[80,256]{1,0:T(8,128)S(1)}, f32[80,256]{1,0:T(8,128)S(1)}, u32[]{:S(2)}, u32[]{:S(2)}) collective-permute-start(f32[80,256]{1,0:T(8,128)S(1)} %pad_maximum_fusion.2), channel_id=1, source_target_pairs={{0,2},{1,3},{2,0},{3,1},{4,6},{5,7},{6,4},{7,5},{8,10},{9,11},{10,... | collective-permute-start | bytes 245768 | tf_op jit(solution)/shard_map/ppermute | solution.py:283
  76.9 6.2 %collective-permute-start.19 = (f32[64,768]{1,0:T(8,128)S(1)}, f32[64,768]{1,0:T(8,128)S(1)}, u32[]{:S(2)}, u32[]{:S(2)}) collective-permute-start(f32[64,768]{1,0:T(8,128)S(1)} %get-tuple-element.67), channel_id=1, source_target_pairs={{0,8},{8,0},{16,24},{24,16},{1,9},{9,1},{17,25},{25,17},{2,10},{10... | collective-permute-start | bytes 589832 | tf_op jit(solution)/shard_map/ppermute | solution.py:283
  80.0 5.1 %collective-permute-start.22 = (f32[48,256]{1,0:T(8,128)S(1)}, f32[48,256]{1,0:T(8,128)S(1)}, u32[]{:S(2)}, u32[]{:S(2)}) collective-permute-start(f32[48,256]{1,0:T(8,128)S(1)} %pad_maximum_fusion.3), channel_id=1, source_target_pairs={{0,4},{1,5},{2,6},{3,7},{4,0},{5,1},{6,2},{7,3},{8,12},{9,13},{10,... | collective-permute-start | bytes 147464 | tf_op jit(solution)/shard_map/ppermute | solution.py:283
  83.8 6.3 %collective-permute-start.21 = (f32[32,768]{1,0:T(8,128)S(1)}, f32[32,768]{1,0:T(8,128)S(1)}, u32[]{:S(2)}, u32[]{:S(2)}) collective-permute-start(f32[32,768]{1,0:T(8,128)S(1)} %get-tuple-element.72), channel_id=1, source_target_pairs={{0,16},{8,24},{16,0},{24,8},{1,17},{9,25},{17,1},{25,9},{2,18},{10... | collective-permute-start | bytes 294920 | tf_op jit(solution)/shard_map/ppermute | solution.py:283
  85.1 5.0 %copy-start.13 = (f32[48,256]{1,0:T(8,128)}, f32[48,256]{1,0:T(8,128)S(1)}, u32[]{:S(2)}) copy-start(f32[48,256]{1,0:T(8,128)S(1)} %collective-permute-done.22.refs_3_) | copy-start | bytes 147460
  90.1 0.6 copy-start.2

commit v4 on v3

--- a/solution.py
+++ b/solution.py
@@ -362,7 +362,7 @@
     send, keep = list(results[:streams]), list(results[streams:])
     got = [swap(send[s], "beta", 1, sizes) for s in range(streams)]
     for t in range(len(orders[0])):
-        if 0 < t < 3:
+        if t == 1:
             keep, got = lax.optimization_barrier((keep, got))
         if len(keep) == 3 and orders[0][t:] == orders[1][t:]:
             keep = [jnp.concatenate(keep[:2], axis=1), keep[2]]

time: 92.9 us -> 92.8 us (level)
    add x9 -> x7, other arithmetic: 2.17 us -> 2.06 us  [shards(): out[s] = keep[s][n:] + got[s][n:]]
    unnamed x30 -> x29, local copies, waits for them, and re-layouts: 2.39 us -> 2.36 us
  transfers between devices with their start and end apart: 23 -> 23, of which waited for: 13 -> 12; matrix products, arithmetic and copies ran while one was open for 3% -> 3% of each run, Pallas kernels for 0% -> 0%
where the time goes in v4:
time: 92.8 us; the launch traced here: 92.5 us
  Pallas kernels  34.5 us (37%)
  waiting for transfers between devices  31.2 us (34%)
  starting transfers between devices  20.6 us (22%)
  other arithmetic  2.96 us (3%)
  local copies, waits for them, and re-layouts  2.38 us (3%)
    pallas_call x1, Pallas kernels, shards(): pl.pallas_call(functools.partial(main_kernel, rows_each, orders, columns,...  32.7 us
    ppermute x23, waiting for transfers between devices, swap(): lax.ppermute(value, kind, [(i, i ^ flip) for i in range(sizes[kind])])  31.2 us
    ppermute x23, starting transfers between devices, swap(): lax.ppermute(value, kind, [(i, i ^ flip) for i in range(sizes[kind])])  20.6 us
    unnamed x29, local copies, waits for them, and re-layouts  2.36 us
    add x7, other arithmetic, shards(): out[s] = keep[s][n:] + got[s][n:]  2.06 us
  transfers between devices with their start and end apart: 23, of which 12 were waited for; matrix products, arithmetic and copies ran while one was open for 3% of the time, Pallas kernels for 0%

profile of v4, /device:TPU:0, one launch (start us, length us, event | category | flops | bytes accessed | tf_op | source)
XLA Modules:
  0.0 92.5 jit_solution(7419470056580463260)
XLA Ops:
  0.6 3.0 %collective-permute-start.6 = (f32[4,32,128]{2,1,0:T(8,128)}, f32[4,32,128]{2,1,0:T(8,128)S(1)}, u32[]{:S(2)}, u32[]{:S(2)}) collective-permute-start(f32[4,32,128]{2,1,0:T(8,128)} %refs_0_.1), channel_id=1, source_target_pairs={{0,4},{1,5},{2,6},{3,7},{4,0},{5,1},{6,2},{7,3},{8,12},{9,13},{10,... | collective-permute-start | bytes 196616 | tf_op jit(solution)/shard_map/ppermute | solution.py:283
  3.7 1.5 %collective-permute-start.4 = (f32[4,32,128]{2,1,0:T(8,128)}, f32[4,32,128]{2,1,0:T(8,128)S(1)}, u32[]{:S(2)}, u32[]{:S(2)}) collective-permute-start(f32[4,32,128]{2,1,0:T(8,128)} %refs_0_.1), channel_id=1, source_target_pairs={{0,2},{1,3},{2,0},{3,1},{4,6},{5,7},{6,4},{7,5},{8,10},{9,11},{10,... | collective-permute-start | bytes 196616 | tf_op jit(solution)/shard_map/ppermute | solution.py:283
  5.2 0.0 collective-permute-start.3
  5.2 3.6 %collective-permute-start.2 = (f32[4,32,128]{2,1,0:T(8,128)}, f32[4,32,128]{2,1,0:T(8,128)S(1)}, u32[]{:S(2)}, u32[]{:S(2)}) collective-permute-start(f32[4,32,128]{2,1,0:T(8,128)} %refs_0_.1), channel_id=1, source_target_pairs={{0,24},{8,16},{16,8},{24,0},{1,25},{9,17},{17,9},{25,1},{2,26},{10... | collective-permute-start | bytes 196616 | tf_op jit(solution)/shard_map/ppermute | solution.py:283
  8.8 0.5 collective-permute-start.8
  9.2 0.0 collective-permute-done.6.refs_7_
  9.2 0.0 collective-permute-start.1
  9.2 0.0 collective-permute-done.4.refs_5_
  9.3 1.5 %collective-permute-start = (f32[4,32,128]{2,1,0:T(8,128)}, f32[4,32,128]{2,1,0:T(8,128)S(1)}, u32[]{:S(2)}, u32[]{:S(2)}) collective-permute-start(f32[4,32,128]{2,1,0:T(8,128)} %refs_0_.1), channel_id=1, source_target_pairs={{0,8},{8,0},{16,24},{24,16},{1,9},{9,1},{17,25},{25,17},{2,10},{10... | collective-permute-start | bytes 196616 | tf_op jit(solution)/shard_map/ppermute | solution.py:283
  10.8 0.0 collective-permute-done.3.refs_4_
  10.8 0.0 collective-permute-start.7
  10.8 1.0 %collective-permute-done.2.refs_3_ = f32[4,32,128]{2,1,0:T(8,128)S(1)} collective-permute-done((f32[4,32,128]{2,1,0:T(8,128)}, f32[4,32,128]{2,1,0:T(8,128)S(1)}, u32[]{:S(2)}, u32[]{:S(2)}) %collective-permute-start.2) | collective-permute-done | bytes 65568 | tf_op jit(solution)/shard_map/ppermute | solution.py:283
  11.8 0.0 collective-permute-start.5
  11.8 2.3 %collective-permute-done.8.refs_9_ = f32[4,32,128]{2,1,0:T(8,128)S(1)} collective-permute-done((f32[4,32,128]{2,1,0:T(8,128)}, f32[4,32,128]{2,1,0:T(8,128)S(1)}, u32[]{:S(2)}, u32[]{:S(2)}) %collective-permute-start.8) | collective-permute-done | bytes 65568 | tf_op jit(solution)/shard_map/ppermute | solution.py:283
  14.1 0.0 collective-permute-start.9
  14.1 1.1 %collective-permute-done.1.refs_2_ = f32[4,32,128]{2,1,0:T(8,128)S(1)} collective-permute-done((f32[4,32,128]{2,1,0:T(8,128)}, f32[4,32,128]{2,1,0:T(8,128)S(1)}, u32[]{:S(2)}, u32[]{:S(2)}) %collective-permute-start.1) | collective-permute-done | bytes 65568 | tf_op jit(solution)/shard_map/ppermute | solution.py:283
  15.2 0.0 collective-permute-done.refs_1_
  15.2 0.0 collective-permute-done.7.refs_8_
  15.2 0.0 collective-permute-done.5.refs_6_
  15.2 0.0 copy-start.11
  15.2 0.1 collective-permute-done.9.refs_10_
  15.4 0.0 copy-done.6
  15.4 0.4 copy-done.8
  15.8 0.0 copy-done.9
  15.9 0.0 copy-done.10
  15.9 0.0 copy-done.11
  15.9 0.6 copy-done.12
  16.5 32.7 %excite.1 = (f32[512,384]{1,0:T(8,128)}, f32[512,384]{1,0:T(8,128)}, f32[528,256]{1,0:T(8,128)}, f32[512,384]{1,0:T(8,128)}, f32[512,384]{1,0:T(8,128)}, /*index=5*/f32[528,256]{1,0:T(8,128)}) custom-call(s32[1,256]{1,0:T(1,128)} %constant.4.clone.lane_ref, s32[32,256]{1,0:T(8,128)} %asrc_ref.1, s32[32,256]{1,0:T(8,128)} %asgn_ref.1, s32[128,256]{1,0:T(8,128)} %bsrc_ref.1, ...), custom_call_target="tpu_custom_call" | custom-call | tf_op jit(solution)/shard_map/excite/pallas_call | solution.py:322
  49.2 0.1 collective-permute-start.10
  49.2 0.5 collective-permute-start.11
  49.7 0.1 collective-permute-start.12
  49.8 1.9 %collective-permute-done.10 = f32[512,384]{1,0:T(8,128)S(1)} collective-permute-done((f32[512,384]{1,0:T(8,128)}, f32[512,384]{1,0:T(8,128)S(1)}, u32[]{:S(2)}, u32[]{:S(2)}) %collective-permute-start.10) | collective-permute-done | bytes 786464 | tf_op jit(solution)/shard_map/ppermute | solution.py:283
  51.7 1.3 %slice_add_fusion = (f32[256,384]{1,0:T(8,128)S(1)}, f32[256,384]{1,0:T(8,128)S(1)}) fusion(f32[512,384]{1,0:T(8,128)S(1)} %collective-permute-done.10, f32[512,384]{1,0:T(8,128)} %get-tuple-element.26), kind=kLoop, calls=%fused_computation | loop fusion | flops 196608 | bytes 2359296 | tf_op jit(solution)/shard_map/add | solution.py:379
  53.0 0.0 collective-permute-done.11
  53.0 0.1 copy-done
  53.1 0.1 slice_add_fusion.2
  53.2 0.4 collective-permute-done.12
  53.6 0.5 copy-done.1
  54.2 1.5 %collective-permute-start.14 = (f32[256,384]{1,0:T(8,128)S(1)}, f32[256,384]{1,0:T(8,128)S(1)}, u32[]{:S(2)}, u32[]{:S(2)}) collective-permute-start(f32[256,384]{1,0:T(8,128)S(1)} %get-tuple-element.37), channel_id=1, source_target_pairs={{0,4},{1,5},{2,6},{3,7},{4,0},{5,1},{6,2},{7,3},{8,12},{9,13},{10,... | collective-permute-start | bytes 1179656 | tf_op jit(solution)/shard_map/ppermute | solution.py:283
  55.7 1.5 %collective-permute-start.13 = (f32[256,384]{1,0:T(8,128)S(1)}, f32[256,384]{1,0:T(8,128)S(1)}, u32[]{:S(2)}, u32[]{:S(2)}) collective-permute-start(f32[256,384]{1,0:T(8,128)S(1)} %get-tuple-element.36), channel_id=1, source_target_pairs={{0,2},{1,3},{2,0},{3,1},{4,6},{5,7},{6,4},{7,5},{8,10},{9,11},{10,... | collective-permute-start | bytes 1179656 | tf_op jit(solution)/shard_map/ppermute | solution.py:283
  57.2 0.2 collective-permute-start.15
  57.4 8.0 %collective-permute-done.15 = f32[272,256]{1,0:T(8,128)S(1)} collective-permute-done((f32[272,256]{1,0:T(8,128)S(1)}, f32[272,256]{1,0:T(8,128)S(1)}, u32[]{:S(2)}, u32[]{:S(2)}) %collective-permute-start.15) | collective-permute-done | bytes 278560 | tf_op jit(solution)/shard_map/ppermute | solution.py:283
  65.4 0.0 collective-permute-done.14
  65.4 1.1 %collective-permute-done.13 = f32[256,384]{1,0:T(8,128)S(1)} collective-permute-done((f32[256,384]{1,0:T(8,128)S(1)}, f32[256,384]{1,0:T(8,128)S(1)}, u32[]{:S(2)}, u32[]{:S(2)}) %collective-permute-start.13) | collective-permute-done | bytes 393248 | tf_op jit(solution)/shard_map/ppermute | solution.py:283
  66.5 0.1 slice_add_fusion.10
  66.6 0.1 slice_add_fusion.8
  66.7 1.6 %collective-permute-start.19 = (f32[144,256]{1,0:T(8,128)S(1)}, f32[144,256]{1,0:T(8,128)S(1)}, u32[]{:S(2)}, u32[]{:S(2)}) collective-permute-start(f32[144,256]{1,0:T(8,128)S(1)} %pad_maximum_fusion.2), channel_id=1, source_target_pairs={{0,16},{8,24},{16,0},{24,8},{1,17},{9,25},{17,1},{25,9},{2,18},{10... | collective-permute-start | bytes 442376 | tf_op jit(solution)/shard_map/ppermute | solution.py:283
  68.3 1.5 %collective-permute-start.17 = (f32[128,384]{1,0:T(8,128)S(1)}, f32[128,384]{1,0:T(8,128)S(1)}, u32[]{:S(2)}, u32[]{:S(2)}) collective-permute-start(f32[128,384]{1,0:T(8,128)S(1)} %get-tuple-element.47), channel_id=1, source_target_pairs={{0,2},{1,3},{2,0},{3,1},{4,6},{5,7},{6,4},{7,5},{8,10},{9,11},{10,... | collective-permute-start | bytes 589832 | tf_op jit(solution)/shard_map/ppermute | solution.py:283
  69.8 0.5 collective-permute-start.16
  70.3 5.0 %collective-permute-done.19 = f32[144,256]{1,0:T(8,128)S(1)} collective-permute-done((f32[144,256]{1,0:T(8,128)S(1)}, f32[144,256]{1,0:T(8,128)S(1)}, u32[]{:S(2)}, u32[]{:S(2)}) %collective-permute-start.19) | collective-permute-done | bytes 147488 | tf_op jit(solution)/shard_map/ppermute | solution.py:283
  75.3 1.4 %collective-permute-start.20 = (f32[80,256]{1,0:T(8,128)S(1)}, f32[80,256]{1,0:T(8,128)S(1)}, u32[]{:S(2)}, u32[]{:S(2)}) collective-permute-start(f32[80,256]{1,0:T(8,128)S(1)} %pad_maximum_fusion.3), channel_id=1, source_target_pairs={{0,2},{1,3},{2,0},{3,1},{4,6},{5,7},{6,4},{7,5},{8,10},{9,11},{10,... | collective-permute-start | bytes 245768 | tf_op jit(solution)/shard_map/ppermute | solution.py:283
  76.8 0.0 collective-permute-done.16
  76.8 0.0 collective-permute-done.17
  76.9 0.1 collective-permute-start.18
  77.0 2.9 %collective-permute-done.20 = f32[80,256]{1,0:T(8,128)S(1)} collective-permute-done((f32[80,256]{1,0:T(8,128)S(1)}, f32[80,256]{1,0:T(8,128)S(1)}, u32[]{:S(2)}, u32[]{:S(2)}) %collective-permute-start.20) | collective-permute-done | bytes 81952 | tf_op jit(solution)/shard_map/ppermute | solution.py:283
  79.9 1.0 %collective-permute-start.22 = (f32[48,256]{1,0:T(8,128)S(1)}, f32[48,256]{1,0:T(8,128)S(1)}, u32[]{:S(2)}, u32[]{:S(2)}) collective-permute-start(f32[48,256]{1,0:T(8,128)S(1)} %pad_maximum_fusion.4), channel_id=1, source_target_pairs={{0,4},{1,5},{2,6},{3,7},{4,0},{5,1},{6,2},{7,3},{8,12},{9,13},{10,... | collective-permute-start | bytes 147464 | tf_op jit(solution)/shard_map/ppermute | solution.py:283
  80.8 2.3 %collective-permute-done.18 = f32[64,768]{1,0:T(8,128)S(1)} collective-permute-done((f32[64,768]{1,0:T(8,128)S(1)}, f32[64,768]{1,0:T(8,128)S(1)}, u32[]{:S(2)}, u32[]{:S(2)}) %collective-permute-start.18) | collective-permute-done | bytes 196640 | tf_op jit(solution)/shard_map/ppermute | solution.py:283
  83.1 0.6 slice_add_fusion.13
  83.8 0.6 collective-permute-start.21
  84.4 0.6 slice_add_fusion.17.refs_1_
  85.0 0.0 collective-permute-done.22.refs_3_
  85.0 5.0 %collective-permute-done.21.refs_2_ = f32[32,768]{1,0:T(8,128)S(1)} collective-permute-done((f32[32,768]{1,0:T(8,128)S(1)}, f32[32,768]{1,0:T(8,128)S(1)}, u32[]{:S(2)}, u32[]{:S(2)}) %collective-permute-start.21) | collective-permute-done | bytes 98336 | tf_op jit(solution)/shard_map/ppermute | solution.py:283
  90.1 0.6 copy-done.2
  90.7 1.8 %finish.1 = (f32[4,1024]{1,0:T(4,128)}, f32[32,1024]{1,0:T(8,128)}) custom-call(s32[1,256]{1,0:T(1,128)} %constant.5.clone.lane_ref, f32[32,768]{1,0:T(8,128)} %get-tuple-element.61.refs_0_, f32[48,256]{1,0:T(8,128)} %slice_add_fusion.17.refs_1_, f32[32,768]{1,0:T(8,128)} %copy-done.2, f32[48,256]{1,0:T(8,128)} %copy-done.13), custom_call_target="tpu_custom_call" | custom-call | tf_op jit(solution)/shard_map/finish/pallas_call | solution.py:386
  (36 shorter events, 0.3 us)
Async XLA Ops:
  0.6 8.6 %collective-permute-start.6 = (f32[4,32,128]{2,1,0:T(8,128)}, f32[4,32,128]{2,1,0:T(8,128)S(1)}, u32[]{:S(2)}, u32[]{:S(2)}) collective-permute-start(f32[4,32,128]{2,1,0:T(8,128)} %refs_0_.1), channel_id=1, source_target_pairs={{0,4},{1,5},{2,6},{3,7},{4,0},{5,1},{6,2},{7,3},{8,12},{9,13},{10,... | collective-permute-start | bytes 196616 | tf_op jit(solution)/shard_map/ppermute | solution.py:283
  3.7 5.6 %collective-permute-start.4 = (f32[4,32,128]{2,1,0:T(8,128)}, f32[4,32,128]{2,1,0:T(8,128)S(1)}, u32[]{:S(2)}, u32[]{:S(2)}) collective-permute-start(f32[4,32,128]{2,1,0:T(8,128)} %refs_0_.1), channel_id=1, source_target_pairs={{0,2},{1,3},{2,0},{3,1},{4,6},{5,7},{6,4},{7,5},{8,10},{9,11},{10,... | collective-permute-start | bytes 196616 | tf_op jit(solution)/shard_map/ppermute | solution.py:283
  5.2 5.6 %collective-permute-start.3 = (f32[4,32,128]{2,1,0:T(8,128)}, f32[4,32,128]{2,1,0:T(8,128)S(1)}, u32[]{:S(2)}, u32[]{:S(2)}) collective-permute-start(f32[4,32,128]{2,1,0:T(8,128)} %refs_0_.1), channel_id=1, source_target_pairs={{0,1},{1,0},{2,3},{3,2},{4,5},{5,4},{6,7},{7,6},{8,9},{9,8},{10,11... | collective-permute-start | bytes 196616 | tf_op jit(solution)/shard_map/ppermute | solution.py:283
  5.2 6.7 %collective-permute-start.2 = (f32[4,32,128]{2,1,0:T(8,128)}, f32[4,32,128]{2,1,0:T(8,128)S(1)}, u32[]{:S(2)}, u32[]{:S(2)}) collective-permute-start(f32[4,32,128]{2,1,0:T(8,128)} %refs_0_.1), channel_id=1, source_target_pairs={{0,24},{8,16},{16,8},{24,0},{1,25},{9,17},{17,9},{25,1},{2,26},{10... | collective-permute-start | bytes 196616 | tf_op jit(solution)/shard_map/ppermute | solution.py:283
  8.8 5.4 %collective-permute-start.8 = (f32[4,32,128]{2,1,0:T(8,128)}, f32[4,32,128]{2,1,0:T(8,128)S(1)}, u32[]{:S(2)}, u32[]{:S(2)}) collective-permute-start(f32[4,32,128]{2,1,0:T(8,128)} %refs_0_.1), channel_id=1, source_target_pairs={{0,6},{1,7},{2,4},{3,5},{4,2},{5,3},{6,0},{7,1},{8,14},{9,15},{10,... | collective-permute-start | bytes 196616 | tf_op jit(solution)/shard_map/ppermute | solution.py:283
  9.2 6.2 %copy-start.3 = (f32[4,32,128]{2,1,0:T(8,128)}, f32[4,32,128]{2,1,0:T(8,128)S(1)}, u32[]{:S(2)}) copy-start(f32[4,32,128]{2,1,0:T(8,128)S(1)} %collective-permute-done.6.refs_7_) | copy-start | bytes 196612
  9.2 6.0 %collective-permute-start.1 = (f32[4,32,128]{2,1,0:T(8,128)}, f32[4,32,128]{2,1,0:T(8,128)S(1)}, u32[]{:S(2)}, u32[]{:S(2)}) collective-permute-start(f32[4,32,128]{2,1,0:T(8,128)} %refs_0_.1), channel_id=1, source_target_pairs={{0,16},{8,24},{16,0},{24,8},{1,17},{9,25},{17,1},{25,9},{2,18},{10... | collective-permute-start | bytes 196616 | tf_op jit(solution)/shard_map/ppermute | solution.py:283
  9.3 6.1 %copy-start.4 = (f32[4,32,128]{2,1,0:T(8,128)}, f32[4,32,128]{2,1,0:T(8,128)S(1)}, u32[]{:S(2)}) copy-start(f32[4,32,128]{2,1,0:T(8,128)S(1)} %collective-permute-done.4.refs_5_) | copy-start | bytes 196612
  9.3 5.9 %collective-permute-start = (f32[4,32,128]{2,1,0:T(8,128)}, f32[4,32,128]{2,1,0:T(8,128)S(1)}, u32[]{:S(2)}, u32[]{:S(2)}) collective-permute-start(f32[4,32,128]{2,1,0:T(8,128)} %refs_0_.1), channel_id=1, source_target_pairs={{0,8},{8,0},{16,24},{24,16},{1,9},{9,1},{17,25},{25,17},{2,10},{10... | collective-permute-start | bytes 196616 | tf_op jit(solution)/shard_map/ppermute | solution.py:283
  10.8 4.6 %copy-start.5 = (f32[4,32,128]{2,1,0:T(8,128)}, f32[4,32,128]{2,1,0:T(8,128)S(1)}, u32[]{:S(2)}) copy-start(f32[4,32,128]{2,1,0:T(8,128)S(1)} %collective-permute-done.3.refs_4_) | copy-start | bytes 196612
  10.8 4.4 %collective-permute-start.7 = (f32[4,32,128]{2,1,0:T(8,128)S(1)}, f32[4,32,128]{2,1,0:T(8,128)S(1)}, u32[]{:S(2)}, u32[]{:S(2)}) collective-permute-start(f32[4,32,128]{2,1,0:T(8,128)S(1)} %collective-permute-done.6.refs_7_), channel_id=1, source_target_pairs={{0,1},{1,0},{2,3},{3,2},{4,5},{5,4},{6,7},{7,6},{8,9},{9,8},{10,11... | collective-permute-start | bytes 196616 | tf_op jit(solution)/shard_map/ppermute | solution.py:283
  11.8 3.6 %copy-start.6 = (f32[4,32,128]{2,1,0:T(8,128)}, f32[4,32,128]{2,1,0:T(8,128)S(1)}, u32[]{:S(2)}) copy-start(f32[4,32,128]{2,1,0:T(8,128)S(1)} %collective-permute-done.2.refs_3_) | copy-start | bytes 196612
  11.8 3.4 %collective-permute-start.5 = (f32[4,32,128]{2,1,0:T(8,128)S(1)}, f32[4,32,128]{2,1,0:T(8,128)S(1)}, u32[]{:S(2)}, u32[]{:S(2)}) collective-permute-start(f32[4,32,128]{2,1,0:T(8,128)S(1)} %collective-permute-done.4.refs_5_), channel_id=1, source_target_pairs={{0,1},{1,0},{2,3},{3,2},{4,5},{5,4},{6,7},{7,6},{8,9},{9,8},{10,11... | collective-permute-start | bytes 196616 | tf_op jit(solution)/shard_map/ppermute | solution.py:283
  14.1 1.3 %copy-start.7 = (f32[4,32,128]{2,1,0:T(8,128)}, f32[4,32,128]{2,1,0:T(8,128)S(1)}, u32[]{:S(2)}) copy-start(f32[4,32,128]{2,1,0:T(8,128)S(1)} %collective-permute-done.8.refs_9_) | copy-start | bytes 196612
  14.1 1.3 %collective-permute-start.9 = (f32[4,32,128]{2,1,0:T(8,128)S(1)}, f32[4,32,128]{2,1,0:T(8,128)S(1)}, u32[]{:S(2)}, u32[]{:S(2)}) collective-permute-start(f32[4,32,128]{2,1,0:T(8,128)S(1)} %collective-permute-done.8.refs_9_), channel_id=1, source_target_pairs={{0,1},{1,0},{2,3},{3,2},{4,5},{5,4},{6,7},{7,6},{8,9},{9,8},{10,11... | collective-permute-start | bytes 196616 | tf_op jit(solution)/shard_map/ppermute | solution.py:283
  15.2 0.6 copy-start.8
  15.2 0.6 copy-start.9
  15.2 0.6 copy-start.10
  15.2 0.6 copy-start.11
  15.9 0.6 copy-start.12
  49.2 2.6 %collective-permute-start.10 = (f32[512,384]{1,0:T(8,128)}, f32[512,384]{1,0:T(8,128)S(1)}, u32[]{:S(2)}, u32[]{:S(2)}) collective-permute-start(f32[512,384]{1,0:T(8,128)} %get-tuple-element.27), channel_id=1, source_target_pairs={{0,1},{1,0},{2,3},{3,2},{4,5},{5,4},{6,7},{7,6},{8,9},{9,8},{10,11... | collective-permute-start | bytes 2359304 | tf_op jit(solution)/shard_map/ppermute | solution.py:283
  49.2 3.8 %collective-permute-start.11 = (f32[512,384]{1,0:T(8,128)}, f32[512,384]{1,0:T(8,128)S(1)}, u32[]{:S(2)}, u32[]{:S(2)}) collective-permute-start(f32[512,384]{1,0:T(8,128)} %get-tuple-element.29), channel_id=1, source_target_pairs={{0,1},{1,0},{2,3},{3,2},{4,5},{5,4},{6,7},{7,6},{8,9},{9,8},{10,11... | collective-permute-start | bytes 2359304 | tf_op jit(solution)/shard_map/ppermute | solution.py:283
  49.7 3.9 %collective-permute-start.12 = (f32[528,256]{1,0:T(8,128)}, f32[528,256]{1,0:T(8,128)S(1)}, u32[]{:S(2)}, u32[]{:S(2)}) collective-permute-start(f32[528,256]{1,0:T(8,128)} %get-tuple-element.33), channel_id=1, source_target_pairs={{0,1},{1,0},{2,3},{3,2},{4,5},{5,4},{6,7},{7,6},{8,9},{9,8},{10,11... | collective-permute-start | bytes 1622024 | tf_op jit(solution)/shard_map/ppermute | solution.py:283
  51.7 1.4 %copy-start = (f32[512,384]{1,0:T(8,128)S(1)}, f32[512,384]{1,0:T(8,128)}, u32[]{:S(2)}) copy-start(f32[512,384]{1,0:T(8,128)} %get-tuple-element.30) | copy-start | bytes 2359300
  53.1 1.0 %copy-start.1 = (f32[528,256]{1,0:T(8,128)S(1)}, f32[528,256]{1,0:T(8,128)}, u32[]{:S(2)}) copy-start(f32[528,256]{1,0:T(8,128)} %get-tuple-element.34) | copy-start | bytes 1622020
  54.2 11.2 %collective-permute-start.14 = (f32[256,384]{1,0:T(8,128)S(1)}, f32[256,384]{1,0:T(8,128)S(1)}, u32[]{:S(2)}, u32[]{:S(2)}) collective-permute-start(f32[256,384]{1,0:T(8,128)S(1)} %get-tuple-element.37), channel_id=1, source_target_pairs={{0,4},{1,5},{2,6},{3,7},{4,0},{5,1},{6,2},{7,3},{8,12},{9,13},{10,... | collective-permute-start | bytes 1179656 | tf_op jit(solution)/shard_map/ppermute | solution.py:283
  55.7 10.9 %collective-permute-start.13 = (f32[256,384]{1,0:T(8,128)S(1)}, f32[256,384]{1,0:T(8,128)S(1)}, u32[]{:S(2)}, u32[]{:S(2)}) collective-permute-start(f32[256,384]{1,0:T(8,128)S(1)} %get-tuple-element.36), channel_id=1, source_target_pairs={{0,2},{1,3},{2,0},{3,1},{4,6},{5,7},{6,4},{7,5},{8,10},{9,11},{10,... | collective-permute-start | bytes 1179656 | tf_op jit(solution)/shard_map/ppermute | solution.py:283
  57.2 8.2 %collective-permute-start.15 = (f32[272,256]{1,0:T(8,128)S(1)}, f32[272,256]{1,0:T(8,128)S(1)}, u32[]{:S(2)}, u32[]{:S(2)}) collective-permute-start(f32[272,256]{1,0:T(8,128)S(1)} %pad_maximum_fusion), channel_id=1, source_target_pairs={{0,8},{8,0},{16,24},{24,16},{1,9},{9,1},{17,25},{25,17},{2,10},{10... | collective-permute-start | bytes 835592 | tf_op jit(solution)/shard_map/ppermute | solution.py:283
  66.7 8.6 %collective-permute-start.19 = (f32[144,256]{1,0:T(8,128)S(1)}, f32[144,256]{1,0:T(8,128)S(1)}, u32[]{:S(2)}, u32[]{:S(2)}) collective-permute-start(f32[144,256]{1,0:T(8,128)S(1)} %pad_maximum_fusion.2), channel_id=1, source_target_pairs={{0,16},{8,24},{16,0},{24,8},{1,17},{9,25},{17,1},{25,9},{2,18},{10... | collective-permute-start | bytes 442376 | tf_op jit(solution)/shard_map/ppermute | solution.py:283
  68.3 8.5 %collective-permute-start.17 = (f32[128,384]{1,0:T(8,128)S(1)}, f32[128,384]{1,0:T(8,128)S(1)}, u32[]{:S(2)}, u32[]{:S(2)}) collective-permute-start(f32[128,384]{1,0:T(8,128)S(1)} %get-tuple-element.47), channel_id=1, source_target_pairs={{0,2},{1,3},{2,0},{3,1},{4,6},{5,7},{6,4},{7,5},{8,10},{9,11},{10,... | collective-permute-start | bytes 589832 | tf_op jit(solution)/shard_map/ppermute | solution.py:283
  69.8 7.0 %collective-permute-start.16 = (f32[128,384]{1,0:T(8,128)S(1)}, f32[128,384]{1,0:T(8,128)S(1)}, u32[]{:S(2)}, u32[]{:S(2)}) collective-permute-start(f32[128,384]{1,0:T(8,128)S(1)} %get-tuple-element.44), channel_id=1, source_target_pairs={{0,4},{1,5},{2,6},{3,7},{4,0},{5,1},{6,2},{7,3},{8,12},{9,13},{10,... | collective-permute-start | bytes 589832 | tf_op jit(solution)/shard_map/ppermute | solution.py:283
  75.3 4.5 %collective-permute-start.20 = (f32[80,256]{1,0:T(8,128)S(1)}, f32[80,256]{1,0:T(8,128)S(1)}, u32[]{:S(2)}, u32[]{:S(2)}) collective-permute-start(f32[80,256]{1,0:T(8,128)S(1)} %pad_maximum_fusion.3), channel_id=1, source_target_pairs={{0,2},{1,3},{2,0},{3,1},{4,6},{5,7},{6,4},{7,5},{8,10},{9,11},{10,... | collective-permute-start | bytes 245768 | tf_op jit(solution)/shard_map/ppermute | solution.py:283
  76.9 6.2 %collective-permute-start.18 = (f32[64,768]{1,0:T(8,128)S(1)}, f32[64,768]{1,0:T(8,128)S(1)}, u32[]{:S(2)}, u32[]{:S(2)}) collective-permute-start(f32[64,768]{1,0:T(8,128)S(1)} %get-tuple-element.55), channel_id=1, source_target_pairs={{0,8},{8,0},{16,24},{24,16},{1,9},{9,1},{17,25},{25,17},{2,10},{10... | collective-permute-start | bytes 589832 | tf_op jit(solution)/shard_map/ppermute | solution.py:283
  79.9 5.1 %collective-permute-start.22 = (f32[48,256]{1,0:T(8,128)S(1)}, f32[48,256]{1,0:T(8,128)S(1)}, u32[]{:S(2)}, u32[]{:S(2)}) collective-permute-start(f32[48,256]{1,0:T(8,128)S(1)} %pad_maximum_fusion.4), channel_id=1, source_target_pairs={{0,4},{1,5},{2,6},{3,7},{4,0},{5,1},{6,2},{7,3},{8,12},{9,13},{10,... | collective-permute-start | bytes 147464 | tf_op jit(solution)/shard_map/ppermute | solution.py:283
  83.8 6.3 %collective-permute-start.21 = (f32[32,768]{1,0:T(8,128)S(1)}, f32[32,768]{1,0:T(8,128)S(1)}, u32[]{:S(2)}, u32[]{:S(2)}) collective-permute-start(f32[32,768]{1,0:T(8,128)S(1)} %get-tuple-element.60), channel_id=1, source_target_pairs={{0,16},{8,24},{16,0},{24,8},{1,17},{9,25},{17,1},{25,9},{2,18},{10... | collective-permute-start | bytes 294920 | tf_op jit(solution)/shard_map/ppermute | solution.py:283
  85.0 5.0 %copy-start.13 = (f32[48,256]{1,0:T(8,128)}, f32[48,256]{1,0:T(8,128)S(1)}, u32[]{:S(2)}) copy-start(f32[48,256]{1,0:T(8,128)S(1)} %collective-permute-done.22.refs_3_) | copy-start | bytes 147460
  90.1 0.6 copy-start.2
